TPU v7x, 512 devices: a whole 4x4x16 slice. The times are simulated.
512 devices in a mesh: dom: 32 (over x_lo, z), grid: 16 (over x_hi, y, core).
Axes of the slice: x: 4 (x_hi: 2, x_lo: 2; x = x_hi * 2 + x_lo), y: 4, z: 16, core: 2. Of those that a mesh axis runs over, the one named last changes fastest.
Arguments:
- node_feats: bfloat16 [65536, 512], P(('dom', 'grid')), may hold values from -6 to 6
- adj_vals: bfloat16 [32, 16, 16, 4, 128, 128], P('dom', 'grid'), may hold values from -0.109375 to 0.109375
- adj_col: int32 [32, 16, 16, 4], P('dom', 'grid'), may hold values from 0 to 31
- adj_count: int32 [32, 16, 16], P('dom', 'grid'), may hold values from 0 to 4, as said below
- hist_store: bfloat16 [512, 16384], P('grid', 'dom'), may hold values from -6 to 6
- hist_list: int32 [32, 40], replicated, may hold values from 0 to 127, as said below
- hist_adj: bfloat16 [32, 40, 128, 128], P('dom'), may hold values from -0.3125 to 0.3125
- hist_row: int32 [32, 40], P('dom'), may hold values from 0 to 15
- hist_col: int32 [32, 40], P('dom'), may hold values from 0 to 39, each once within a row
- w_first: bfloat16 [512, 512], replicated, may hold values from -0.25 to 0.25
- w_second: bfloat16 [512, 512], replicated, may hold values from -0.25 to 0.25
Outputs:
- hidden: bfloat16 [65536, 512], P(('dom', 'grid'))
- embedding: bfloat16 [65536, 512], P(('dom', 'grid'))
Inputs may be any that keep to these rules, and one draw needn't show every extreme that they name: `adj_count`: slots of a block row at or beyond its count hold values that take no part. Some block row of some tile has 4 live slots. `hist_list`: the ids in one partition's list are distinct; at most 2 of them belong to one owner partition (owner = id // 4), and some list has 2 from one owner.
All inputs are finite; a program needn't handle non-finite values.
Results may differ from a plain program's by a relative error of at most 0.024.
Values may be sent and summed in bfloat16 or wider, within the bound.
No kernel may reach another device: no remote copies, remote signals or barrier semaphores. Data moves between devices by JAX's collectives and lax.ppermute only.
A program may use at most 64 MiB of HBM per device.

v0:
```python
import jax
import jax.numpy as jnp
from jax import lax
from jax.sharding import PartitionSpec as P

F = 512
BLOCK = 128
HOWN = 4
CAP = 2


def tile_product(col_panel, live_vals, tile_cols):
    blocks = col_panel.reshape(-1, BLOCK, col_panel.shape[1])
    picked = jnp.take(blocks, tile_cols, axis=0)
    summed = jnp.einsum("rkab,rkbf->raf", live_vals, picked, preferred_element_type=jnp.float32)
    return summed.reshape(-1, col_panel.shape[1])


def aggregate(source, live_vals, tile_cols, extra_term):
    col_panel = lax.all_gather(source, "dom", axis=0, tiled=True)
    partial_value = tile_product(col_panel, live_vals, tile_cols)
    if extra_term is not None:
        partial_value = partial_value + extra_term
    rounded = lax.optimization_barrier(partial_value.astype(jnp.bfloat16))
    return lax.psum_scatter(
        rounded.astype(jnp.float32).astype(jnp.bfloat16), "grid", scatter_dimension=0, tiled=True
    )


def history_term(hist_store, hist_list, local_adj, local_rows, local_cols, tile_rows):
    list_length = hist_list.shape[1]
    dom_index = lax.axis_index("dom")
    owner_ids = hist_list // HOWN
    local_ids = hist_list % HOWN
    same_owner = owner_ids[:, :, None] == owner_ids[:, None, :]
    earlier = jnp.arange(list_length)[None, :] < jnp.arange(list_length)[:, None]
    order_rank = jnp.sum(same_owner & earlier[None, :, :], axis=2)
    chosen_mask = (owner_ids == dom_index)[:, :, None, None]
    chosen_mask = chosen_mask & (
        order_rank[:, :, None, None] == jnp.arange(CAP)[None, None, :, None]
    )
    chosen_mask = chosen_mask & (
        local_ids[:, :, None, None] == jnp.arange(HOWN)[None, None, None, :]
    )
    selector = jnp.sum(chosen_mask.astype(jnp.int32), axis=1).astype(jnp.bfloat16)
    own_blocks = hist_store.reshape(hist_store.shape[0], HOWN, BLOCK)
    outgoing = jnp.einsum(
        "rch,fhb->rcfb", selector, own_blocks, preferred_element_type=jnp.float32
    ).astype(jnp.bfloat16)
    incoming = lax.all_to_all(outgoing, "dom", split_axis=0, concat_axis=0, tiled=True)
    flat_blocks = incoming.reshape(-1, incoming.shape[2], incoming.shape[3])
    mine_owner = lax.dynamic_index_in_dim(owner_ids, dom_index, 0, keepdims=False)
    mine_rank = lax.dynamic_index_in_dim(order_rank, dom_index, 0, keepdims=False)
    fetched = jnp.take(flat_blocks, mine_owner * CAP + mine_rank, axis=0)
    chosen = jnp.take(fetched, local_cols, axis=0)
    contribs = jnp.einsum("sfb,sab->sfa", chosen, local_adj, preferred_element_type=jnp.float32)
    row_onehot = (local_rows[None, :] == jnp.arange(tile_rows)[:, None]).astype(jnp.float32)
    summed = jnp.einsum("rs,sfa->rfa", row_onehot, contribs, precision=lax.Precision.HIGHEST)
    return summed.transpose(0, 2, 1).reshape(tile_rows * BLOCK, -1)


def local(
    node_feats,
    adj_vals,
    adj_col,
    adj_count,
    hist_store,
    hist_list,
    hist_adj,
    hist_row,
    hist_col,
    w_first,
    w_second,
):
    tile_vals = adj_vals[0, 0]
    tile_cols = adj_col[0, 0]
    row_counts = adj_count[0, 0]
    tile_rows = tile_vals.shape[0]
    live_mask = (jnp.arange(tile_vals.shape[1])[None, :] < row_counts[:, None]).astype(jnp.bfloat16)
    live_vals = tile_vals * live_mask[:, :, None, None]
    agg_first = aggregate(node_feats, live_vals, tile_cols, None)
    hidden = jax.nn.relu(jnp.dot(agg_first, w_first, preferred_element_type=jnp.float32)).astype(
        jnp.bfloat16
    )
    hist_part = history_term(
        hist_store, hist_list, hist_adj[0], hist_row[0], hist_col[0], tile_rows
    )
    grid_index = lax.axis_index("grid")
    placed = lax.dynamic_update_slice_in_dim(
        jnp.zeros((hist_part.shape[0], F), jnp.float32),
        hist_part,
        grid_index * hist_part.shape[1],
        1,
    )
    agg_second = aggregate(hidden, live_vals, tile_cols, placed)
    embedding = jnp.dot(agg_second, w_second, preferred_element_type=jnp.float32).astype(
        jnp.bfloat16
    )
    return (hidden, embedding)


def solution(mesh):
    placed = (
        P(("dom", "grid"), None),
        P("dom", "grid", None, None, None, None),
        P("dom", "grid", None, None),
        P("dom", "grid", None),
        P("grid", "dom"),
        P(),
        P("dom", None, None, None),
        P("dom", None),
        P("dom", None),
        P(),
        P(),
    )
    return jax.shard_map(
        local,
        mesh=mesh,
        in_specs=placed,
        out_specs=(P(("dom", "grid"), None), P(("dom", "grid"), None)),
        check_vma=False,
    )
```

profile of v0, /device:TPU:1, one launch (start us, length us, event | category | flops | bytes accessed | tf_op | source)
XLA Modules:
  0.0 523.9 jit_solution(14827638974284658832)
XLA Ops:
  7.2 0.7 all-gather.3.cloned.1.call-update
  8.0 0.7 compare_select_fusion
  8.7 0.1 reshape.211
  8.8 0.7 compare_and_fusion
  9.5 0.1 copy.31
  9.6 0.7 fusion.22
  10.3 125.7 %all-gather.3.cloned.1.call-done = bf16[4096,512]{1,0:T(8,128)(2,1)} async-done(((bf16[128,512]{1,0:T(8,128)(2,1)}), bf16[4096,512]{1,0:T(8,128)(2,1)}) %all-gather.3.cloned.1.call-update) | async-done | bytes 4194320 | tf_op jit(solution)/shard_map/all_gather | solution.py:20
  136.1 7.7 %gather_fusion.2 = bf16[64,128,512]{2,1,0:T(8,128)(2,1)} fusion(bf16[32,128,512]{2,1,0:T(8,128)(2,1)} %bitcast.56, s32[1024]{0:T(1024)S(1)} %pad_clamp_fusion.2), kind=kCustom, calls=%fused_computation.clone | custom fusion | bytes 16777472 | tf_op jit(solution)/shard_map/jit(_take)/gather | solution.py:14
  143.8 7.2 %bitcast_convert_fusion = bf16[16,128,512]{2,1,0:T(8,128)(2,1)} fusion(bf16[16,4,128,512]{3,2,1,0:T(8,128)(2,1)} %bitcast.58, pred[16,4]{1,0:T(8,128)(4,1)S(1)} %copy.31, bf16[1,1,16,4,128,128]{5,4,3,2,1,0:T(8,128)(2,1)} %param.14, bf16[16,4]{1,0:T(8,128)(2,1)S(1)} %fusion.22), kind=kOutput, calls=%fused_computation.10 | convolution fusion | flops 1080033280 | bytes 12583104 | tf_op jit(solution)/shard_map/rkab,rkbf->raf/dot_general | solution.py:15
  151.1 102.5 %reduce-scatter.3.cloned.1.call-done = bf16[128,512]{1,0:T(8,128)(2,1)} async-done(((bf16[2048,512]{1,0:T(8,128)(2,1)}), bf16[128,512]{1,0:T(8,128)(2,1)}) %reduce-scatter.3.cloned.1.call-update) | async-done | bytes 131088 | tf_op jit(solution)/shard_map/reduce_scatter | solution.py:25
  253.6 1.8 fusion.12
  255.5 0.8 convert_reduce_fusion
  256.4 0.2 convert_reduce_fusion.1
  256.6 0.3 convolution_convert_fusion
  257.0 1.0 copy.35
  258.0 12.8 %all-to-all-start = ((bf16[32,2,32,128]{3,2,1,0:T(8,128)(2,1)}), bf16[32,2,32,128]{3,2,1,0:T(8,128)(2,1)S(1)}, u32[]{:S(2)}, u32[]{:S(2)}) async-start(bf16[32,2,32,128]{3,2,1,0:T(8,128)(2,1)} %copy.35), calls=%async_computation.1 | async-start | bytes 1048576 | tf_op jit(solution)/shard_map/all_to_all | solution.py:50
  270.9 31.6 %all-to-all-done = bf16[32,2,32,128]{3,2,1,0:T(8,128)(2,1)S(1)} async-done(((bf16[32,2,32,128]{3,2,1,0:T(8,128)(2,1)}), bf16[32,2,32,128]{3,2,1,0:T(8,128)(2,1)S(1)}, u32[]{:S(2)}, u32[]{:S(2)}) %all-to-all-start) | async-done | bytes 524320 | tf_op jit(solution)/shard_map/all_to_all | solution.py:50
  302.4 0.6 gather_fusion
  303.1 0.1 broadcast_select_fusion
  303.2 0.6 gather_fusion.1
  303.8 0.8 fusion.10
  304.6 0.7 convolution_bitcast_fusion
  305.4 0.3 copy.41
  305.7 83.8 %all-gather.5.cloned.1.call-done = bf16[4096,512]{1,0:T(8,128)(2,1)} async-done(((bf16[128,512]{1,0:T(8,128)(2,1)}), bf16[4096,512]{1,0:T(8,128)(2,1)}) %all-gather.5.cloned.1.call-update) | async-done | bytes 4194320 | tf_op jit(solution)/shard_map/all_gather | solution.py:20
  389.5 7.7 %gather_fusion.3 = bf16[64,128,512]{2,1,0:T(8,128)(2,1)} fusion(bf16[32,128,512]{2,1,0:T(8,128)(2,1)} %bitcast.55, s32[1024]{0:T(1024)S(1)} %pad_clamp_fusion.2), kind=kCustom, calls=%fused_computation.1.clone | custom fusion | bytes 16777472 | tf_op jit(solution)/shard_map/jit(_take)/gather | solution.py:14
  397.2 5.7 %fusion = f32[16,128,512,1]{2,1,3,0:T(8,128)S(1)} fusion(bf16[16,4,128,512]{3,2,1,0:T(8,128)(2,1)} %bitcast.57, pred[16,4]{1,0:T(8,128)(4,1)S(1)} %copy.31, bf16[1,1,16,4,128,128]{5,4,3,2,1,0:T(8,128)(2,1)} %param.14, bf16[16,4]{1,0:T(8,128)(2,1)S(1)} %fusion.22), kind=kOutput, calls=%fused_computation.4 | convolution fusion | flops 1078984704 | bytes 14680256 | tf_op jit(solution)/shard_map/rkab,rkbf->raf/dot_general | solution.py:15
  403.0 1.9 copy-done.1
  404.9 0.4 bitcast_add_fusion
  405.3 6.6 %add.103 = f32[2048,512]{1,0:T(8,128)} dynamic-update-slice(f32[2048,512]{1,0:T(8,128)} %bitcast.60, f32[2048,32]{1,0:T(8,128)S(1)} %bitcast_add_fusion, s32[]{:T(128)} %constant.76.clone.1, s32[]{:T(128)S(6)} %select_n.66) | dynamic-update-slice | bytes 524292 | tf_op jit(solution)/shard_map/add | solution.py:23
  411.9 3.8 convert_element_type.47
  415.8 99.8 %reduce-scatter.5.cloned.1.call-done = bf16[128,512]{1,0:T(8,128)(2,1)} async-done(((bf16[2048,512]{1,0:T(8,128)(2,1)}), bf16[128,512]{1,0:T(8,128)(2,1)}) %reduce-scatter.5.cloned.1.call-update) | async-done | bytes 131088 | tf_op jit(solution)/shard_map/reduce_scatter | solution.py:25
  515.6 1.8 convolution_convert_fusion.1
  (35 shorter events, 0.5 us)
Async XLA Ops:
  7.2 296.6 %copy-start = (bf16[1,40,128,128]{3,2,1,0:T(8,128)(2,1)S(1)}, bf16[1,40,128,128]{3,2,1,0:T(8,128)(2,1)}, u32[]{:S(2)}) copy-start(bf16[1,40,128,128]{3,2,1,0:T(8,128)(2,1)} %param.19) | copy-start | bytes 3932164
  7.2 128.9 %all-gather.3.cloned.1.call-start = ((), (), s32[]{:S(2)}) async-start(), calls=%async_computation.3 | async-start | bytes 4325376 | tf_op jit(solution)/shard_map/all_gather | solution.py:20
  7.9 245.7 %reduce-scatter.3.cloned.1.call-start = ((), (), s32[]{:S(2)}) async-start(), calls=%async_computation.4 | async-start | bytes 2228224 | tf_op jit(solution)/shard_map/reduce_scatter | solution.py:25
  143.8 109.8 %copy-start.2 = (bf16[512,512]{1,0:T(8,128)(2,1)S(1)}, bf16[512,512]{1,0:T(8,128)(2,1)}, u32[]{:S(2)}) copy-start(bf16[512,512]{1,0:T(8,128)(2,1)} %param.22) | copy-start | bytes 1572868
  143.8 111.6 %copy-start.5 = (bf16[32,512]{1,0:T(8,128)(2,1)S(1)}, bf16[32,512]{1,0:T(8,128)(2,1)}, u32[]{:S(2)}) copy-start(bf16[32,512]{1,0:T(8,128)(2,1)} %param.17) | copy-start | bytes 98308
  143.8 111.7 %copy-start.4 = (s32[32,40]{1,0:T(8,128)S(1)}, s32[32,40]{1,0:T(8,128)}, u32[]{:S(2)}) copy-start(s32[32,40]{1,0:T(8,128)} %param.18) | copy-start | bytes 15364
  151.0 119.8 %copy-start.7 = (s32[1,40]{1,0:T(1,128)S(1)}, s32[1,40]{1,0:T(1,128)}, u32[]{:S(2)}) copy-start(s32[1,40]{1,0:T(1,128)} %param.21) | copy-start | bytes 484
  151.0 153.6 %copy-start.6 = (s32[1,40]{1,0:T(1,128)S(1)}, s32[1,40]{1,0:T(1,128)}, u32[]{:S(2)}) copy-start(s32[1,40]{1,0:T(1,128)} %param.20) | copy-start | bytes 484
  151.0 238.5 %all-gather.5.cloned.1.call-start = ((), (), s32[]{:S(2)}) async-start(), calls=%async_computation.5 | async-start | bytes 4325376 | tf_op jit(solution)/shard_map/all_gather | solution.py:20
  258.0 44.5 %all-to-all-start = ((bf16[32,2,32,128]{3,2,1,0:T(8,128)(2,1)}), bf16[32,2,32,128]{3,2,1,0:T(8,128)(2,1)S(1)}, u32[]{:S(2)}, u32[]{:S(2)}) async-start(bf16[32,2,32,128]{3,2,1,0:T(8,128)(2,1)} %copy.35), calls=%async_computation.1 | async-start | bytes 1048576 | tf_op jit(solution)/shard_map/all_to_all | solution.py:50
  270.7 244.9 %reduce-scatter.5.cloned.1.call-start = ((), (), s32[]{:S(2)}) async-start(), calls=%async_computation.6 | async-start | bytes 2228224 | tf_op jit(solution)/shard_map/reduce_scatter | solution.py:25
  403.0 1.9 copy-start.1
  411.9 103.7 %copy-start.3 = (bf16[512,512]{1,0:T(8,128)(2,1)S(1)}, bf16[512,512]{1,0:T(8,128)(2,1)}, u32[]{:S(2)}) copy-start(bf16[512,512]{1,0:T(8,128)(2,1)} %param.23) | copy-start | bytes 1572868
Sparse Core Ops, SparseCore 0:
  10.1 125.9 all-gather.2
  151.2 102.3 reduce-scatter.2
  256.5 133.0 all-gather.4
  415.9 99.6 reduce-scatter.4
where the time goes:
time: 525 us; the launch traced here: 524 us
  waiting for transfers between devices  444 us (85%)
  local copies, waits for them, and re-layouts  26.9 us (5%)
  matrix products  18.4 us (4%)
  between operations  14 us (3%)
  starting transfers between devices  12.9 us (2%)
  other arithmetic  7.57 us (1%)
    all_gather x2, waiting for transfers between devices, aggregate(): col_panel = lax.all_gather(source, 'dom', axis=0, tiled=True)  210 us
    reduce_scatter x2, waiting for transfers between devices, aggregate(): lax.psum_scatter(rounded.astype(jnp.float32).astype(jnp.bfloat16), 'grid'...  202 us
    all_to_all x1, waiting for transfers between devices, history_term(): lax.all_to_all(outgoing, 'dom', split_axis=0, concat_axis=0, tiled=True)  31.6 us
    gather x2, local copies, waits for them, and re-layouts, tile_product(): picked = jnp.take(blocks, tile_cols, axis=0)  15.4 us
    dot_general x2, matrix products, tile_product(): jnp.einsum('rkab,rkbf->raf', live_vals, picked, preferred_element_type=jn...  12.9 us
    all_to_all x1, starting transfers between devices, history_term(): lax.all_to_all(outgoing, 'dom', split_axis=0, concat_axis=0, tiled=True)  12.8 us
  transfers between devices with their start and end apart: 5, of which 5 were waited for; matrix products, arithmetic and copies ran while one was open for 2% of the time, Pallas kernels for 0%

commit v1 on v0

v1 whole, which is shorter than its diff:
```python
import functools

import jax
import jax.numpy as jnp
from jax import lax
from jax.experimental import pallas as pl
from jax.experimental.pallas import tpu as pltpu
from jax.sharding import Mesh, PartitionSpec as P

F = 512
BLOCK = 128
HOWN = 4
ROWS = 16
SLOTS = 4
FEAT = 32
LIST = 40
WIDE = 128
STRIDE = BLOCK + FEAT
DOM = ("x_lo", "z")
GRID = ("x_hi", "y", "core")
SIDE = ("x_hi", "y")


def tile_body(stride, cols, counts, spot, adj, panel, *rest):
    extra = rest[0] if len(rest) == 4 else None
    keep, send, acc = rest[-3:]
    row = pl.program_id(0)
    count = counts[row]
    core = spot[0]

    def pair(first):
        left = []
        right = []
        for slot in (first, first + 1):
            live = slot < count
            left.append(jnp.where(live, adj[0, slot], jnp.zeros_like(adj[0, slot])))
            start = pl.multiple_of(cols[row * SLOTS + slot] * stride, FEAT)
            right.append(panel[pl.ds(start, BLOCK), :])
        return jnp.dot(
            jnp.concatenate(left, axis=1),
            jnp.concatenate(right, axis=0),
            preferred_element_type=jnp.float32,
        )

    acc[...] = pair(0)

    @pl.when(count > 2)
    def _():
        acc[...] += pair(2)

    if extra is not None:
        for lane in range(F // WIDE):

            @pl.when(spot[1] == lane)
            def _(lane=lane):
                acc[:, lane * WIDE : (lane + 1) * WIDE] += extra[...]

    value = acc[...].astype(jnp.bfloat16)

    @pl.when(row % 2 == core)
    def _():
        keep[0] = value

    @pl.when(row % 2 != core)
    def _():
        send[0] = value


def tile_product(cols, counts, spot, adj, panel, extra):
    operands = [adj, panel]
    specs = [
        pl.BlockSpec((1, SLOTS, BLOCK, BLOCK), lambda q, *_: (q, 0, 0, 0)),
        pl.BlockSpec(panel.shape, lambda q, *_: (0, 0)),
    ]
    if extra is not None:
        operands.append(extra)
        specs.append(pl.BlockSpec((BLOCK, WIDE), lambda q, *_: (q, 0)))
    half = jax.ShapeDtypeStruct((ROWS // 2, BLOCK, F), jnp.bfloat16)
    out_spec = pl.BlockSpec((1, BLOCK, F), lambda q, *_: (q // 2, 0, 0))
    return pl.pallas_call(
        functools.partial(tile_body, panel.shape[0] // 32),
        out_shape=(half, half),
        grid_spec=pltpu.PrefetchScalarGridSpec(
            num_scalar_prefetch=3,
            grid=(ROWS,),
            in_specs=specs,
            out_specs=(out_spec, out_spec),
            scratch_shapes=[pltpu.VMEM((BLOCK, F), jnp.float32)],
        ),
        compiler_params=pltpu.CompilerParams(
            dimension_semantics=("arbitrary",), vmem_limit_bytes=40 << 20
        ),
        name="tile_product",
    )(cols, counts, spot, *operands)


def history_body(places, rows, spot, adj, store, out, wide):
    wide[...] = jnp.zeros_like(wide)
    out[...] = jnp.zeros_like(out)
    offset = pl.multiple_of(spot[2] * FEAT, FEAT)

    def step(slot, carry):
        source = pl.multiple_of((places[slot] // HOWN) * STRIDE + BLOCK, FEAT)
        lane = pl.multiple_of((places[slot] % HOWN) * BLOCK, BLOCK)
        wide[pl.ds(offset, FEAT), :] = store[pl.ds(source, FEAT), pl.ds(lane, BLOCK)]
        part = lax.dot_general(
            adj[slot], wide[...], (((1,), (1,)), ((), ())), preferred_element_type=jnp.float32
        )
        target = pl.multiple_of(rows[slot] * BLOCK, BLOCK)
        out[pl.ds(target, BLOCK), :] += part
        return carry

    lax.fori_loop(0, LIST, step, 0)


def history_term(places, rows, spot, adj, store):
    return pl.pallas_call(
        history_body,
        out_shape=jax.ShapeDtypeStruct((ROWS * BLOCK, WIDE), jnp.float32),
        grid_spec=pltpu.PrefetchScalarGridSpec(
            num_scalar_prefetch=3,
            grid=(1,),
            in_specs=[
                pl.BlockSpec(adj.shape, lambda i, *_: (0, 0, 0)),
                pl.BlockSpec(store.shape, lambda i, *_: (0, 0)),
            ],
            out_specs=pl.BlockSpec((ROWS * BLOCK, WIDE), lambda i, *_: (0, 0)),
            scratch_shapes=[pltpu.VMEM((WIDE, BLOCK), jnp.bfloat16)],
        ),
        compiler_params=pltpu.CompilerParams(
            dimension_semantics=("arbitrary",), vmem_limit_bytes=40 << 20
        ),
        name="history_term",
    )(places, rows, spot, adj, store)


def finish(parts, weight, relu):
    def body(parts_ref, weight_ref, out):
        total = parts_ref[0].astype(jnp.float32)
        for k in range(1, parts.shape[0]):
            total = total + parts_ref[k].astype(jnp.float32)
        value = jnp.dot(
            total.astype(jnp.bfloat16), weight_ref[...], preferred_element_type=jnp.float32
        )
        if relu:
            value = jnp.maximum(value, 0.0)
        out[...] = value.astype(jnp.bfloat16)

    return pl.pallas_call(
        body,
        out_shape=jax.ShapeDtypeStruct((BLOCK, F), jnp.bfloat16),
        compiler_params=pltpu.CompilerParams(vmem_limit_bytes=32 << 20),
        name="finish",
    )(parts, weight)


def gather_panel(source):
    pair = lax.all_gather(source, "x_lo", axis=0, tiled=True)
    return lax.all_gather(pair, "z", axis=0, tiled=True)


def reduce_rows(keep, send):
    swap = [(0, 1), (1, 0)]
    other = lax.ppermute(send, "core", swap)
    both = (keep.astype(jnp.float32) + other.astype(jnp.float32)).astype(jnp.bfloat16)
    return lax.all_to_all(both, SIDE, 0, 0, tiled=True)


def local(
    node_feats,
    adj_vals,
    adj_col,
    adj_count,
    hist_store,
    hist_list,
    hist_adj,
    hist_row,
    hist_col,
    w_first,
    w_second,
):
    adj = adj_vals[0, 0]
    cols = adj_col[0, 0].reshape(-1)
    counts = adj_count[0, 0]
    places = (cols % 16) * 2 + cols // 16
    grid_index = lax.axis_index(GRID)
    spot = jnp.stack([lax.axis_index("core"), grid_index // 4, grid_index % 4]).astype(jnp.int32)

    panel = gather_panel(jnp.concatenate([node_feats, hist_store], axis=0))

    mine = lax.dynamic_index_in_dim(hist_list, lax.axis_index(DOM), 0, keepdims=False)
    wanted = jnp.take(mine, hist_col[0], axis=0)
    owner = wanted // HOWN
    hist_places = ((owner % 16) * 2 + owner // 16) * HOWN + wanted % HOWN
    extra = history_term(hist_places, hist_row[0], spot, hist_adj[0], panel)

    hidden = finish(
        reduce_rows(*tile_product(places, counts, spot, adj, panel, None)), w_first, True
    )
    panel = gather_panel(hidden)
    embedding = finish(
        reduce_rows(*tile_product(places, counts, spot, adj, panel, extra)), w_second, False
    )
    return hidden, embedding


def solution(mesh):
    fine = Mesh(mesh.devices.reshape(2, 16, 2, 4, 2), ("x_lo", "z", "x_hi", "y", "core"))
    placed = (
        P(DOM + GRID, None),
        P(DOM, GRID),
        P(DOM, GRID),
        P(DOM, GRID),
        P(GRID, DOM),
        P(),
        P(DOM),
        P(DOM),
        P(DOM),
        P(),
        P(),
    )
    return jax.shard_map(
        local,
        mesh=fine,
        in_specs=placed,
        out_specs=(P(DOM + GRID, None), P(DOM + GRID, None)),
        check_vma=False,
    )
```

time: 525 us -> 263 us (0.50)
  waiting for transfers between devices: 444 us -> 139 us
  blocking collectives: 0 us -> 54.2 us
  Pallas kernels: 0 us -> 21.2 us
  matrix products: 18.4 us -> 0 us
  local copies, waits for them, and re-layouts: 26.9 us -> 12.4 us
  starting transfers between devices: 12.9 us -> 19.5 us
  other arithmetic: 7.57 us -> 1.68 us
    reduce_scatter x2 -> x0, waiting for transfers between devices: 202 us -> none  [aggregate(): lax.psum_scatter(rounded.astype(jnp.float32).astype(jnp.bfloat16), 'grid'...]
    all_gather x2, waiting for transfers between devices: 210 us -> 134 us  [gather_panel(): return lax.all_gather(pair, 'z', axis=0, tiled=True)]
    all_to_all x0 -> x2, blocking collectives: none -> 43.9 us  [reduce_rows(): return lax.all_to_all(both, SIDE, 0, 0, tiled=True)]
    all_to_all x1 -> x0, waiting for transfers between devices: 31.6 us -> none  [history_term(): lax.all_to_all(outgoing, 'dom', split_axis=0, concat_axis=0, tiled=True)]
    pallas_call x0 -> x5, Pallas kernels: none -> 21.2 us  [the longest x2 12.1 us: tile_product(): pl.pallas_call(functools.partial(tile_body, panel.shape[0] // 32), out_sh...]
    ppermute x0 -> x2, starting transfers between devices: none -> 19.4 us  [reduce_rows(): other = lax.ppermute(send, 'core', swap)]
    dot_general x7 -> x0, matrix products: 18.4 us -> none  [the longest x2 12.9 us: tile_product(): jnp.einsum('rkab,rkbf->raf', live_vals, picked, preferred_element_type=jn...]
    gather x4 -> x1, local copies, waits for them, and re-layouts: 16.7 us -> 0.78 us  [local(): wanted = jnp.take(mine, hist_col[0], axis=0)]
  transfers between devices with their start and end apart: 5 -> 4, of which waited for: 5 -> 4; matrix products, arithmetic and copies ran while one was open for 2% -> 1% of each run, Pallas kernels for 0% -> 3%
where the time goes in v1:
time: 263 us; the launch traced here: 262 us
  waiting for transfers between devices  139 us (53%)
  blocking collectives  54.2 us (21%)
  Pallas kernels  21.2 us (8%)
  starting transfers between devices  19.5 us (7%)
  between operations  14.2 us (5%)
  local copies, waits for them, and re-layouts  12.4 us (5%)
    all_gather x2, waiting for transfers between devices, gather_panel(): return lax.all_gather(pair, 'z', axis=0, tiled=True)  134 us
    all_to_all x2, blocking collectives, reduce_rows(): return lax.all_to_all(both, SIDE, 0, 0, tiled=True)  43.9 us
    ppermute x2, starting transfers between devices, reduce_rows(): other = lax.ppermute(send, 'core', swap)  19.4 us
    pallas_call x2, Pallas kernels, tile_product(): pl.pallas_call(functools.partial(tile_body, panel.shape[0] // 32), out_sh...  12.1 us
    unnamed x27, local copies, waits for them, and re-layouts  11.5 us
    all_gather x2, blocking collectives, gather_panel(): pair = lax.all_gather(source, 'x_lo', axis=0, tiled=True)  10.3 us
    pallas_call x1, Pallas kernels, history_term(): pl.pallas_call(history_body, out_shape=jax.ShapeDtypeStruct((ROWS * BLOCK...  7.25 us
  transfers between devices with their start and end apart: 4, of which 4 were waited for; matrix products, arithmetic and copies ran while one was open for 1% of the time, Pallas kernels for 3%

profile of v1, /device:TPU:1, one launch (start us, length us, event | category | flops | bytes accessed | tf_op | source)
XLA Modules:
  0.0 262.2 jit_solution(17524782066205182980)
XLA Ops:
  7.2 0.0 all-gather.3.cloned.1.call-start
  7.2 0.9 pad_maximum_fusion
  8.2 5.5 %all_gather.12 = bf16[320,512]{1,0:T(8,128)(2,1)} all-gather(bf16[160,512]{1,0:T(8,128)(2,1)S(1)} %pad_maximum_fusion), channel_id=1, replica_groups=mesh['x_lo'=2,'z'=16,'x_hi'=2,'y'=4,'core'=2] {'x_lo'}, dimensions={0}, use_global_device_ids=true | all-gather | bytes 491520 | tf_op jit(solution)/shard_map/all_gather | solution.py:158
  13.7 0.0 all-gather.3.cloned.1.call-update
  13.7 0.0 all-gather.5.cloned.1.call-start
  13.8 0.8 copy.14
  14.5 0.1 reshape_squeeze.3
  14.6 0.1 pad_add_fusion.spot
  14.7 80.3 %all-gather.3.cloned.1.call-done.panel.store = bf16[5120,512]{1,0:T(8,128)(2,1)} async-done(((bf16[320,512]{1,0:T(8,128)(2,1)}), bf16[5120,512]{1,0:T(8,128)(2,1)}) %all-gather.3.cloned.1.call-update) | async-done | bytes 5242896 | tf_op jit(solution)/shard_map/all_gather | solution.py:159
  95.0 2.5 copy-done.1
  97.5 1.6 copy-done.3
  99.1 0.7 copy-done.9
  99.7 5.7 %tile_product.2 = (bf16[8,128,512]{2,1,0:T(8,128)(2,1)S(1)}, bf16[8,128,512]{2,1,0:T(8,128)(2,1)S(1)}) custom-call(s32[64]{0:T(128)S(1)} %fusion.2.cols, s32[16]{0:T(128)S(1)} %bitcast.22, s32[3]{0:T(128)S(1)} %pad_add_fusion.spot, bf16[16,4,128,128]{3,2,1,0:T(8,128)(2,1)S(1)} %bitcast.19, bf16[5120,512]{1,0:T(8,128)(2,1)S(1)} %copy-done.1), custom_call_target="tpu_custom_call" | custom-call | tf_op jit(solution)/shard_map/tile_product/pallas_call | solution.py:80
  105.4 8.4 %collective-permute-start = (bf16[8,128,512]{2,1,0:T(8,128)(2,1)S(1)}, bf16[8,128,512]{2,1,0:T(8,128)(2,1)S(1)}, u32[]{:S(2)}, u32[]{:S(2)}) collective-permute-start(bf16[8,128,512]{2,1,0:T(8,128)(2,1)S(1)} %get-tuple-element.7), channel_id=1, source_target_pairs={{0,1},{1,0},{2,3},{3,2},{4,5},{5,4},{6,7},{7,6},{8,9},{9,8},{10,11... | collective-permute-start | bytes 3145736 | tf_op jit(solution)/shard_map/ppermute | solution.py:164
  113.8 2.3 collective-permute-done
  116.1 0.3 add_convert_fusion.1
  116.5 22.2 %all_to_all.10.parts_ref = bf16[8,128,512]{2,1,0:T(8,128)(2,1)S(1)} all-to-all(bf16[8,128,512]{2,1,0:T(8,128)(2,1)S(1)} %add_convert_fusion.1), channel_id=1, replica_groups=mesh['x_lo'=2,'z'=16,'x_hi'=2,'y'=4,'core'=2] {'x_hi','y'}, dimensions={0} | all-to-all | bytes 2097152 | tf_op jit(solution)/shard_map/all_to_all | solution.py:166
  138.7 0.9 finish.2
  139.6 4.8 %all_gather.14 = bf16[256,512]{1,0:T(8,128)(2,1)} all-gather(bf16[128,512]{1,0:T(8,128)(2,1)} %finish.2), channel_id=1, replica_groups=mesh['x_lo'=2,'z'=16,'x_hi'=2,'y'=4,'core'=2] {'x_lo'}, dimensions={0}, use_global_device_ids=true | all-gather | bytes 393216 | tf_op jit(solution)/shard_map/all_gather | solution.py:158
  144.4 0.0 all-gather.5.cloned.1.call-update
  144.5 0.8 gather_fusion
  145.3 2.5 copy-done.2
  147.8 1.3 copy-done.6
  149.1 7.3 %history_term.1.rest_0_ = f32[2048,128]{1,0:T(8,128)S(1)} custom-call(s32[40]{0:T(128)S(1)} %fusion.places, s32[40]{0:T(128)S(1)} %bitcast.24, s32[3]{0:T(128)S(1)} %pad_add_fusion.spot, bf16[40,128,128]{2,1,0:T(8,128)(2,1)S(1)} %bitcast.21, bf16[5120,512]{1,0:T(8,128)(2,1)S(1)} %copy-done.2), custom_call_target="tpu_custom_call" | custom-call | tf_op jit(solution)/shard_map/history_term/pallas_call | solution.py:117
  156.4 54.2 %all-gather.5.cloned.1.call-done.panel = bf16[4096,512]{1,0:T(8,128)(2,1)} async-done(((bf16[256,512]{1,0:T(8,128)(2,1)}), bf16[4096,512]{1,0:T(8,128)(2,1)}) %all-gather.5.cloned.1.call-update) | async-done | bytes 4194320 | tf_op jit(solution)/shard_map/all_gather | solution.py:159
  210.5 2.2 copy-done.5
  212.7 6.3 %tile_product.3 = (bf16[8,128,512]{2,1,0:T(8,128)(2,1)S(1)}, bf16[8,128,512]{2,1,0:T(8,128)(2,1)S(1)}) custom-call(s32[64]{0:T(128)S(1)} %fusion.2.cols, s32[16]{0:T(128)S(1)} %bitcast.23, s32[3]{0:T(128)S(1)} %pad_add_fusion.spot, bf16[16,4,128,128]{3,2,1,0:T(8,128)(2,1)S(1)} %bitcast.20, bf16[4096,512]{1,0:T(8,128)(2,1)S(1)} %copy-done.5, ...), custom_call_target="tpu_custom_call" | custom-call | tf_op jit(solution)/shard_map/tile_product/pallas_call | solution.py:80
  219.1 11.0 %collective-permute-start.1 = (bf16[8,128,512]{2,1,0:T(8,128)(2,1)S(1)}, bf16[8,128,512]{2,1,0:T(8,128)(2,1)S(1)}, u32[]{:S(2)}, u32[]{:S(2)}) collective-permute-start(bf16[8,128,512]{2,1,0:T(8,128)(2,1)S(1)} %get-tuple-element.9), channel_id=1, source_target_pairs={{0,1},{1,0},{2,3},{3,2},{4,5},{5,4},{6,7},{7,6},{8,9},{9,8},{10,11... | collective-permute-start | bytes 3145736 | tf_op jit(solution)/shard_map/ppermute | solution.py:164
  230.1 2.3 collective-permute-done.1
  232.3 0.3 add_convert_fusion
  232.7 21.7 %all_to_all.11.parts_ref = bf16[8,128,512]{2,1,0:T(8,128)(2,1)S(1)} all-to-all(bf16[8,128,512]{2,1,0:T(8,128)(2,1)S(1)} %add_convert_fusion), channel_id=1, replica_groups=mesh['x_lo'=2,'z'=16,'x_hi'=2,'y'=4,'core'=2] {'x_hi','y'}, dimensions={0} | all-to-all | bytes 2097152 | tf_op jit(solution)/shard_map/all_to_all | solution.py:166
  254.4 0.9 finish.3
  (25 shorter events, 0.1 us)
Async XLA Ops:
  7.2 137.3 %copy-start = (s32[32,40]{1,0:T(8,128)S(1)}, s32[32,40]{1,0:T(8,128)}, u32[]{:S(2)}) copy-start(s32[32,40]{1,0:T(8,128)} %param.16) | copy-start | bytes 15364
  7.2 87.8 %all-gather.3.cloned.1.call-start = ((), (), s32[]{:S(2)}) async-start(), calls=%async_computation.2 | async-start | bytes 5570560 | tf_op jit(solution)/shard_map/all_gather | solution.py:159
  13.7 196.8 %all-gather.5.cloned.1.call-start = ((), (), s32[]{:S(2)}) async-start(), calls=%async_computation.3 | async-start | bytes 4456448 | tf_op jit(solution)/shard_map/all_gather | solution.py:159
  95.0 2.5 copy-start.1
  97.5 1.6 copy-start.3
  99.1 0.7 copy-start.9
  105.4 10.7 %collective-permute-start = (bf16[8,128,512]{2,1,0:T(8,128)(2,1)S(1)}, bf16[8,128,512]{2,1,0:T(8,128)(2,1)S(1)}, u32[]{:S(2)}, u32[]{:S(2)}) collective-permute-start(bf16[8,128,512]{2,1,0:T(8,128)(2,1)S(1)} %get-tuple-element.7), channel_id=1, source_target_pairs={{0,1},{1,0},{2,3},{3,2},{4,5},{5,4},{6,7},{7,6},{8,9},{9,8},{10,11... | collective-permute-start | bytes 3145736 | tf_op jit(solution)/shard_map/ppermute | solution.py:164
  116.1 22.5 %copy-start.7 = (bf16[512,512]{1,0:T(8,128)(2,1)S(1)}, bf16[512,512]{1,0:T(8,128)(2,1)}, u32[]{:S(2)}) copy-start(bf16[512,512]{1,0:T(8,128)(2,1)} %weight_ref.2) | copy-start | bytes 1572868
  116.4 28.0 %copy-start.12 = (s32[1,40]{1,0:T(1,128)S(1)}, s32[1,40]{1,0:T(1,128)}, u32[]{:S(2)}) copy-start(s32[1,40]{1,0:T(1,128)} %param.19) | copy-start | bytes 484
  116.4 28.8 %copy-start.11 = (s32[1,40]{1,0:T(1,128)S(1)}, s32[1,40]{1,0:T(1,128)}, u32[]{:S(2)}) copy-start(s32[1,40]{1,0:T(1,128)} %param.18) | copy-start | bytes 484
  145.3 2.5 copy-start.2
  147.8 1.3 copy-start.6
  149.1 61.4 %copy-start.4 = (bf16[1,1,16,4,128,128]{5,4,3,2,1,0:T(8,128)(2,1)S(1)}, bf16[1,1,16,4,128,128]{5,4,3,2,1,0:T(8,128)(2,1)}, u32[]{:S(2)}) copy-start(bf16[1,1,16,4,128,128]{5,4,3,2,1,0:T(8,128)(2,1)} %param.12) | copy-start | bytes 6291460
  149.1 61.4 %copy-start.10 = (s32[1,1,16]{2,1,0:T(1,128)S(1)}, s32[1,1,16]{2,1,0:T(1,128)}, u32[]{:S(2)}) copy-start(s32[1,1,16]{2,1,0:T(1,128)} %param.14) | copy-start | bytes 196
  210.5 2.2 copy-start.5
  219.1 13.3 %collective-permute-start.1 = (bf16[8,128,512]{2,1,0:T(8,128)(2,1)S(1)}, bf16[8,128,512]{2,1,0:T(8,128)(2,1)S(1)}, u32[]{:S(2)}, u32[]{:S(2)}) collective-permute-start(bf16[8,128,512]{2,1,0:T(8,128)(2,1)S(1)} %get-tuple-element.9), channel_id=1, source_target_pairs={{0,1},{1,0},{2,3},{3,2},{4,5},{5,4},{6,7},{7,6},{8,9},{9,8},{10,11... | collective-permute-start | bytes 3145736 | tf_op jit(solution)/shard_map/ppermute | solution.py:164
  232.3 22.0 %copy-start.8 = (bf16[512,512]{1,0:T(8,128)(2,1)S(1)}, bf16[512,512]{1,0:T(8,128)(2,1)}, u32[]{:S(2)}) copy-start(bf16[512,512]{1,0:T(8,128)(2,1)} %weight_ref.3) | copy-start | bytes 1572868
Sparse Core Ops, SparseCore 0:
  13.8 81.1 all-gather.2
  144.5 65.9 all-gather.4

commit v2 on v1

v2 whole, which is shorter than its diff:
```python
import functools

import jax
import jax.numpy as jnp
from jax import lax
from jax.experimental import pallas as pl
from jax.experimental.pallas import tpu as pltpu
from jax.sharding import Mesh, PartitionSpec as P

F = 512
HALF = 256
BLOCK = 128
HOWN = 4
ROWS = 16
SLOTS = 4
FEAT = 32
LIST = 40
WIDE = 128
META = 16
PAY = BLOCK + 2 * FEAT + META
DOM = ("x_lo", "zh", "zl")
Z = ("zh", "zl")
GRID = ("x_hi", "y", "core")
SIDE = ("x_hi", "y")
SWAP = [(0, 1), (1, 0)]
UP = [(z, (z + 1) % 16) for z in range(16)]
DOWN = [(z, (z + 15) % 16) for z in range(16)]


def params(mib):
    return pltpu.CompilerParams(vmem_limit_bytes=mib << 20)


def payload_body(feats, hist, meta, out):
    for j in range(2):
        out[j, :BLOCK] = feats[:, j * HALF : (j + 1) * HALF]
        for k in range(2):
            start = BLOCK + k * FEAT
            out[j, start : start + FEAT] = hist[:, k * HALF : (k + 1) * HALF]
        out[j, BLOCK + 2 * FEAT :] = meta[...]


def make_payload(feats, hist, meta):
    return pl.pallas_call(
        payload_body,
        out_shape=jax.ShapeDtypeStruct((2, PAY, HALF), jnp.bfloat16),
        compiler_params=params(8),
        name="payload",
    )(feats, hist, meta)


def tile_body(with_extra, places, counts, spot, own, partner, same, above, below, *rest):
    extras = rest[:2] if with_extra else ()
    keep, send, panel, adj, acc, sems = rest[-6:]
    core = spot[1]
    moves = [
        pltpu.make_async_copy(same, panel.at[pl.ds(0, 2048)], sems.at[0]),
        pltpu.make_async_copy(above, panel.at[pl.ds(2048, 1024)], sems.at[1]),
        pltpu.make_async_copy(below, panel.at[pl.ds(3072, 1024)], sems.at[2]),
    ]
    for k, source in enumerate((own, partner)):
        for c in range(4):
            moves.append(
                pltpu.make_async_copy(
                    source.at[pl.ds(16 * c, 16)],
                    adj.at[pl.ds(64 * k + 16 * c, 16)],
                    sems.at[3 + 4 * k + c],
                )
            )
    for move in moves:
        move.start()

    def pair(base, count, first):
        left = []
        right = []
        for slot in (first, first + 1):
            block = adj[base + slot]
            left.append(jnp.where(slot < count, block, jnp.zeros_like(block)))
            start = pl.multiple_of(places[base + slot] * BLOCK, BLOCK)
            right.append(panel[pl.ds(start, BLOCK), :])
        return jnp.dot(
            jnp.concatenate(left, axis=1),
            jnp.concatenate(right, axis=0),
            preferred_element_type=jnp.float32,
        )

    def two_rows(k, j):
        part = spot[0] if k == 0 else 1 - spot[0]
        for side in range(2):
            row = 2 * j + side
            count = counts[ROWS * k + row]
            base = (ROWS * k + row) * SLOTS
            acc[side] = pair(base, count, 0)

            @pl.when(count > 2)
            def _(side=side, base=base, count=count):
                acc[side] += pair(base, count, 2)

            if with_extra:
                for group in range(2):

                    @pl.when(spot[2] == group)
                    def _(side=side, group=group, row=row):
                        start = pl.multiple_of(row * BLOCK, BLOCK)
                        piece = extras[k][pl.ds(start, BLOCK), :].astype(jnp.float32)
                        acc[side, :, group * WIDE : (group + 1) * WIDE] += piece

        even = acc[0].astype(jnp.bfloat16)
        odd = acc[1].astype(jnp.bfloat16)
        keep[j, part] = jnp.where(core == 0, even, odd)
        send[j, part] = jnp.where(core == 0, odd, even)

    for n in range(3):
        moves[n].wait()
    for k in range(2):
        for c in range(4):
            moves[3 + 4 * k + c].wait()

            def step(j, carry, k=k):
                two_rows(k, j)
                return carry

            lax.fori_loop(2 * c, 2 * c + 2, step, 0)


def tile_product(places, counts, spot, own, partner, panels, extras):
    operands = [own, partner, *panels]
    specs = [pl.BlockSpec(memory_space=pl.ANY)] * 5
    for extra in extras:
        operands.append(extra)
        specs.append(pl.BlockSpec(extra.shape, lambda i, *_: (0, 0)))
    half = jax.ShapeDtypeStruct((ROWS // 2, 2, BLOCK, HALF), jnp.bfloat16)
    out_spec = pl.BlockSpec(half.shape, lambda i, *_: (0, 0, 0, 0))
    return pl.pallas_call(
        functools.partial(tile_body, bool(extras)),
        out_shape=(half, half),
        grid_spec=pltpu.PrefetchScalarGridSpec(
            num_scalar_prefetch=3,
            grid=(1,),
            in_specs=specs,
            out_specs=(out_spec, out_spec),
            scratch_shapes=[
                pltpu.VMEM((4096, HALF), jnp.bfloat16),
                pltpu.VMEM((2 * ROWS * SLOTS, BLOCK, BLOCK), jnp.bfloat16),
                pltpu.VMEM((2, BLOCK, HALF), jnp.float32),
                pltpu.SemaphoreType.DMA((11,)),
            ],
        ),
        compiler_params=params(20),
        name="tile_product",
    )(places, counts, spot, *operands)


def history_body(listed, order, rows, spot, adj, store, out, total, wide):
    wide[...] = jnp.zeros_like(wide)
    total[...] = jnp.zeros_like(total)
    offset = pl.multiple_of(spot[1] * FEAT, FEAT)

    def step(slot, carry):
        block = listed[spot[0], order[slot]]
        owner = block // HOWN
        piece = block % HOWN
        spot_row = ((owner % 16) * 2 + owner // 16) * (2 * FEAT) + (piece // 2) * FEAT
        source = pl.multiple_of(spot_row, FEAT)
        lane = pl.multiple_of((piece % 2) * BLOCK, BLOCK)
        wide[pl.ds(offset, FEAT), :] = store[pl.ds(source, FEAT), pl.ds(lane, BLOCK)]
        part = lax.dot_general(
            adj[slot], wide[...], (((1,), (1,)), ((), ())), preferred_element_type=jnp.float32
        )
        target = pl.multiple_of(rows[slot] * BLOCK, BLOCK)
        total[pl.ds(target, BLOCK), :] += part
        return carry

    lax.fori_loop(0, LIST, step, 0)
    out[...] = total[...].astype(jnp.bfloat16)


def history_term(listed, order, rows, spot, adj, store):
    return pl.pallas_call(
        history_body,
        out_shape=jax.ShapeDtypeStruct((ROWS * BLOCK, WIDE), jnp.bfloat16),
        grid_spec=pltpu.PrefetchScalarGridSpec(
            num_scalar_prefetch=4,
            grid=(1,),
            in_specs=[
                pl.BlockSpec(adj.shape, lambda i, *_: (0, 0, 0)),
                pl.BlockSpec(store.shape, lambda i, *_: (0, 0)),
            ],
            out_specs=pl.BlockSpec((ROWS * BLOCK, WIDE), lambda i, *_: (0, 0)),
            scratch_shapes=[
                pltpu.VMEM((ROWS * BLOCK, WIDE), jnp.float32),
                pltpu.VMEM((WIDE, BLOCK), jnp.bfloat16),
            ],
        ),
        compiler_params=params(16),
        name="history_term",
    )(listed, order, rows, spot, adj, store)


def add_parts(parts):
    def body(parts_ref, out):
        total = parts_ref[0].astype(jnp.float32)
        for k in range(1, parts.shape[0]):
            total = total + parts_ref[k].astype(jnp.float32)
        out[...] = total.astype(jnp.bfloat16)

    return pl.pallas_call(
        body,
        out_shape=jax.ShapeDtypeStruct(parts.shape[1:], jnp.bfloat16),
        compiler_params=params(8),
        name="add_parts",
    )(parts)


def first_dense(halves, weight, spot):
    def body(spot_ref, halves_ref, weight_ref, hidden, chunk):
        rows = [
            jnp.concatenate([halves_ref[0, part], halves_ref[1, part]], axis=1)
            for part in range(2)
        ]
        value = jnp.dot(
            jnp.concatenate(rows, axis=0), weight_ref[...], preferred_element_type=jnp.float32
        )
        value = jnp.maximum(value, 0.0).astype(jnp.bfloat16)
        low = spot_ref[0] == 0
        hidden[...] = jnp.where(low, value[:BLOCK], value[BLOCK:])
        chunk[...] = jnp.where(low, value[:, :HALF], value[:, HALF:])

    return pl.pallas_call(
        body,
        out_shape=(
            jax.ShapeDtypeStruct((BLOCK, F), jnp.bfloat16),
            jax.ShapeDtypeStruct((2 * BLOCK, HALF), jnp.bfloat16),
        ),
        grid_spec=pltpu.PrefetchScalarGridSpec(
            num_scalar_prefetch=1,
            grid=(1,),
            in_specs=[
                pl.BlockSpec(halves.shape, lambda i, *_: (0, 0, 0, 0)),
                pl.BlockSpec(weight.shape, lambda i, *_: (0, 0)),
            ],
            out_specs=(
                pl.BlockSpec((BLOCK, F), lambda i, *_: (0, 0)),
                pl.BlockSpec((2 * BLOCK, HALF), lambda i, *_: (0, 0)),
            ),
        ),
        compiler_params=params(8),
        name="first_dense",
    )(spot, halves, weight)


def second_dense(halves, weight):
    def body(halves_ref, weight_ref, out):
        rows = jnp.concatenate([halves_ref[0], halves_ref[1]], axis=1)
        value = jnp.dot(rows, weight_ref[...], preferred_element_type=jnp.float32)
        out[...] = value.astype(jnp.bfloat16)

    return pl.pallas_call(
        body,
        out_shape=jax.ShapeDtypeStruct((BLOCK, F), jnp.bfloat16),
        compiler_params=params(8),
        name="second_dense",
    )(halves, weight)


def gather_panel(chunk, first=None):
    same = lax.all_gather(chunk, "zh", axis=0, tiled=True)
    if first is not None:
        same, first = lax.optimization_barrier((same, first))
    above = lax.ppermute(same[:1024], Z, DOWN)
    below = lax.ppermute(same[1024:], Z, UP)
    panels = (same, above, below)
    return panels if first is None else (panels, first)


def reduce_rows(keep, send):
    other = lax.ppermute(send, "core", SWAP)
    both = (keep.astype(jnp.float32) + other.astype(jnp.float32)).astype(jnp.bfloat16)
    return add_parts(lax.all_to_all(both, SIDE, 0, 0, tiled=True))


def local(
    node_feats,
    adj_vals,
    adj_col,
    adj_count,
    hist_store,
    hist_list,
    hist_adj,
    hist_row,
    hist_col,
    w_first,
    w_second,
):
    adj = adj_vals[0, 0].reshape(ROWS * SLOTS, BLOCK, BLOCK)
    x_lo = lax.axis_index("x_lo")
    x_hi = lax.axis_index("x_hi")
    zl = lax.axis_index("zl")
    grid_index = lax.axis_index(GRID)
    group = jnp.where(x_lo == x_hi, (grid_index // 4) % 2, -1)
    spot = jnp.stack([x_lo, lax.axis_index("core"), group]).astype(jnp.int32)
    hist_spot = jnp.stack([lax.axis_index(DOM), grid_index % 4]).astype(jnp.int32)

    numbers = jnp.concatenate([adj_col.reshape(-1), adj_count.reshape(-1)])
    meta = jnp.pad(numbers.astype(jnp.bfloat16)[None, :], ((0, META - 1), (0, HALF - 80)))
    payload = make_payload(node_feats, hist_store, meta)
    received = lax.all_to_all(payload, "x_lo", 0, 0, tiled=True)
    adj_held, received = lax.optimization_barrier((adj, received))
    near = lax.all_gather(
        received[:, BLOCK : BLOCK + 2 * FEAT].reshape(4 * FEAT, HALF), "zl", axis=0, tiled=True
    )
    panels, near = gather_panel(received[:, :BLOCK].reshape(2 * BLOCK, HALF), near)
    partner = lax.ppermute(adj_held, "x_lo", SWAP)

    theirs = lax.dynamic_index_in_dim(received[:, BLOCK + 2 * FEAT, :80], 1 - x_lo, 0, False)
    both = jnp.stack([numbers, theirs.astype(jnp.int32)])
    cols = both[:, :64]
    places = ((cols & 1) ^ zl) * 16 + ((cols & 15) >> 1) * 2 + (cols >> 4)
    places = places.reshape(-1).astype(jnp.int32)
    counts = both[:, 64:].reshape(-1)

    store = lax.all_gather(near, "zh", axis=0, tiled=True)
    mine = history_term(hist_list, hist_col[0], hist_row[0], hist_spot, hist_adj[0], store)
    extras = (mine, lax.ppermute(mine, "x_lo", SWAP))

    agg = reduce_rows(*tile_product(places, counts, spot, adj, partner, panels, ()))
    halves = lax.all_gather(agg, "x_lo", axis=0, tiled=False)
    hidden, chunk = first_dense(halves, w_first, spot)

    panels = gather_panel(chunk)
    agg = reduce_rows(*tile_product(places, counts, spot, adj, partner, panels, extras))
    embedding = second_dense(lax.all_to_all(agg, "x_lo", 0, 0, tiled=True), w_second)
    return hidden, embedding


def solution(mesh):
    fine = Mesh(
        mesh.devices.reshape(2, 8, 2, 2, 4, 2), ("x_lo", "zh", "zl", "x_hi", "y", "core")
    )
    placed = (
        P(DOM + GRID, None),
        P(DOM, GRID),
        P(DOM, GRID),
        P(DOM, GRID),
        P(GRID, DOM),
        P(),
        P(DOM),
        P(DOM),
        P(DOM),
        P(),
        P(),
    )
    return jax.shard_map(
        local,
        mesh=fine,
        in_specs=placed,
        out_specs=(P(DOM + GRID, None), P(DOM + GRID, None)),
        check_vma=False,
    )
```

time: 263 us -> 278 us (1.057)
  waiting for transfers between devices: 139 us -> 124 us
  starting transfers between devices: 19.5 us -> 32.2 us
  blocking collectives: 54.2 us -> 62.9 us
  Pallas kernels: 21.2 us -> 27.6 us
    all_gather x2 -> x3, waiting for transfers between devices: 134 us -> 103 us  [the longest x2 87.6 us: gather_panel(): same = lax.all_gather(chunk, 'zh', axis=0, tiled=True)]
    ppermute x2 -> x8, waiting for transfers between devices: 4.53 us -> 20.5 us  [the longest x2 14.1 us: gather_panel(): below = lax.ppermute(same[1024:], Z, UP)]
    ppermute x2 -> x8, starting transfers between devices: 19.4 us -> 32.1 us  [the longest x2 14.3 us: reduce_rows(): other = lax.ppermute(send, 'core', SWAP)]
    all_to_all x2 -> x4, blocking collectives: 43.9 us -> 53.5 us  [the longest x2 40.9 us: reduce_rows(): return add_parts(lax.all_to_all(both, SIDE, 0, 0, tiled=True))]
    pallas_call x4 -> x7, Pallas kernels: 13.9 us -> 20.1 us  [the longest x2 17.4 us: tile_product(): pl.pallas_call(functools.partial(tile_body, bool(extras)), out_shape=(hal...]
    unnamed x27, local copies, waits for them, and re-layouts: 11.5 us -> 6.04 us
    slice x0 -> x6, local copies, waits for them, and re-layouts: none -> 4.44 us  [the longest x2 3.69 us: gather_panel(): below = lax.ppermute(same[1024:], Z, UP)]
  transfers between devices with their start and end apart: 4 -> 11, of which waited for: 4 -> 9; matrix products, arithmetic and copies ran while one was open for 1% -> 3% of each run, Pallas kernels for 3% -> 3%
where the time goes in v2:
time: 278 us; the launch traced here: 275 us
  waiting for transfers between devices  124 us (45%)
  blocking collectives  62.9 us (23%)
  starting transfers between devices  32.2 us (12%)
  Pallas kernels  27.6 us (10%)
  between operations  14 us (5%)
  local copies, waits for them, and re-layouts  10.9 us (4%)
  other arithmetic  4.32 us (2%)
    all_gather x2, waiting for transfers between devices, gather_panel(): same = lax.all_gather(chunk, 'zh', axis=0, tiled=True)  87.6 us
    all_to_all x2, blocking collectives, reduce_rows(): return add_parts(lax.all_to_all(both, SIDE, 0, 0, tiled=True))  40.9 us
    pallas_call x2, Pallas kernels, tile_product(): pl.pallas_call(functools.partial(tile_body, bool(extras)), out_shape=(hal...  17.4 us
    all_gather x1, waiting for transfers between devices, local(): store = lax.all_gather(near, 'zh', axis=0, tiled=True)  15.4 us
    ppermute x2, starting transfers between devices, reduce_rows(): other = lax.ppermute(send, 'core', SWAP)  14.3 us
    ppermute x2, waiting for transfers between devices, gather_panel(): below = lax.ppermute(same[1024:], Z, UP)  14.1 us
    ppermute x2, starting transfers between devices, gather_panel(): above = lax.ppermute(same[:1024], Z, DOWN)  9.15 us
    pallas_call x1, Pallas kernels, history_term(): pl.pallas_call(history_body, out_shape=jax.ShapeDtypeStruct((ROWS * BLOCK...  7.47 us
  transfers between devices with their start and end apart: 11, of which 9 were waited for; matrix products, arithmetic and copies ran while one was open for 3% of the time, Pallas kernels for 3%

profile of v2, /device:TPU:1, one launch (start us, length us, event | category | flops | bytes accessed | tf_op | source)
XLA Modules:
  0.0 275.5 jit_solution(8980110067382317890)
XLA Ops:
  9.0 0.9 copy-done.8
  10.7 6.9 %all_to_all.20 = bf16[2,208,256]{2,1,0:T(8,128)(2,1)S(1)} all-to-all(bf16[2,208,256]{2,1,0:T(8,128)(2,1)S(1)} %payload.1), channel_id=1, replica_groups=mesh['x_lo'=2,'zh'=8,'zl'=2,'x_hi'=2,'y'=4,'core'=2] {'x_lo'}, dimensions={0} | all-to-all | bytes 425984 | tf_op jit(solution)/shard_map/all_to_all | solution.py:307
  18.3 1.9 collective-permute-start
  21.9 4.5 %all_gather.19 = bf16[256,256]{1,0:T(8,128)(2,1)} all-gather(bf16[128,256]{1,0:T(8,128)(2,1)S(1)} %bitcast.32), channel_id=1, replica_groups=mesh['x_lo'=2,'zh'=8,'zl'=2,'x_hi'=2,'y'=4,'core'=2] {'zl'}, dimensions={0}, use_global_device_ids=true | all-gather | bytes 196608 | tf_op jit(solution)/shard_map/all_gather | solution.py:309
  26.4 48.1 %all-gather.5.cloned.1.call-done.same = bf16[2048,256]{1,0:T(8,128)(2,1)} async-done(((bf16[256,256]{1,0:T(8,128)(2,1)}), bf16[2048,256]{1,0:T(8,128)(2,1)}) %all-gather.5.cloned.1.call-update) | async-done | bytes 1048592 | tf_op jit(solution)/shard_map/all_gather | solution.py:267
  74.5 2.3 fusion.7
  76.8 1.9 collective-permute-start.2
  78.7 4.6 %collective-permute-start.1 = (bf16[1024,256]{1,0:T(8,128)(2,1)}, bf16[1024,256]{1,0:T(8,128)(2,1)}, u32[]{:S(2)}, u32[]{:S(2)}) collective-permute-start(bf16[1024,256]{1,0:T(8,128)(2,1)} %get-tuple-element.25), channel_id=1, source_target_pairs={{0,240},{16,0},{32,16},{48,32},{64,48},{80,64},{96,80},{112,96},{1... | collective-permute-start | bytes 1572872 | tf_op jit(solution)/shard_map/ppermute | solution.py:270
  83.7 7.0 %collective-permute-done.2.below = bf16[1024,256]{1,0:T(8,128)(2,1)} collective-permute-done((bf16[1024,256]{1,0:T(8,128)(2,1)}, bf16[1024,256]{1,0:T(8,128)(2,1)}, u32[]{:S(2)}, u32[]{:S(2)}) %collective-permute-start.2) | collective-permute-done | bytes 524320 | tf_op jit(solution)/shard_map/ppermute | solution.py:271
  91.6 9.4 %tile_product.2 = (bf16[8,2,128,256]{3,2,1,0:T(8,128)(2,1)S(1)}, bf16[8,2,128,256]{3,2,1,0:T(8,128)(2,1)}) custom-call(s32[128]{0:T(128)S(1)} %reshape.71.places, s32[32]{0:T(128)S(1)} %reshape.72.counts, s32[3]{0:T(128)S(1)} %pad_add_fusion.1.spot.spot_ref, bf16[64,128,128]{2,1,0:T(8,128)(2,1)S(1)} %bitcast.25, ...), custom_call_target="tpu_custom_call" | custom-call | tf_op jit(solution)/shard_map/tile_product/pallas_call | solution.py:134
  101.0 1.0 copy-done.4
  102.0 7.2 %collective-permute-start.3 = (bf16[8,2,128,256]{3,2,1,0:T(8,128)(2,1)}, bf16[8,2,128,256]{3,2,1,0:T(8,128)(2,1)S(1)}, u32[]{:S(2)}, u32[]{:S(2)}) collective-permute-start(bf16[8,2,128,256]{3,2,1,0:T(8,128)(2,1)} %get-tuple-element.16), channel_id=1, source_target_pairs={{0,1},{1,0},{2,3},{3,2},{4,5},{5,4},{6,7},{7,6},{8,9},{9,8},{10,11... | collective-permute-start | bytes 3145736 | tf_op jit(solution)/shard_map/ppermute | solution.py:277
  109.3 2.4 collective-permute-done.3
  111.7 1.5 add_convert_fusion.1
  113.3 20.6 %all_to_all.21.parts_ref = bf16[8,2,128,256]{3,2,1,0:T(8,128)(2,1)S(1)} all-to-all(bf16[8,2,128,256]{3,2,1,0:T(8,128)(2,1)S(1)} %add_convert_fusion.1), channel_id=1, replica_groups=mesh['x_lo'=2,'zh'=8,'zl'=2,'x_hi'=2,'y'=4,'core'=2] {'x_hi','y'}, dimensions={0} | all-to-all | bytes 2097152 | tf_op jit(solution)/shard_map/all_to_all | solution.py:279
  134.0 4.9 %all-gather = bf16[4,128,256]{2,1,0:T(8,128)(2,1)S(1)} all-gather(bf16[2,128,256]{2,1,0:T(8,128)(2,1)S(1)} %add_parts.2), channel_id=2, replica_groups=mesh['x_lo'=2,'zh'=8,'zl'=2,'x_hi'=2,'y'=4,'core'=2] {'x_lo'}, dimensions={0}, use_global_device_ids=true | all-gather | bytes 393216 | tf_op jit(solution)/shard_map/all_gather | solution.py:327
  138.9 1.5 first_dense.1
  140.6 15.4 %all-gather.9.cloned.1.call-done.store = bf16[2048,256]{1,0:T(8,128)(2,1)} async-done(((bf16[256,256]{1,0:T(8,128)(2,1)}), bf16[2048,256]{1,0:T(8,128)(2,1)}) %all-gather.9.cloned.1.call-update) | async-done | bytes 1048592 | tf_op jit(solution)/shard_map/all_gather | solution.py:322
  156.0 1.3 copy-done.3
  157.3 1.2 copy-done.5
  158.5 7.5 %history_term.1.rest_0_ = bf16[2048,128]{1,0:T(8,128)(2,1)S(1)} custom-call(s32[32,40]{1,0:T(8,128)S(1)} %copy-done.10, s32[40]{0:T(128)S(1)} %bitcast.29, s32[40]{0:T(128)S(1)} %bitcast.30, s32[2]{0:T(128)S(1)} %pad_add_fusion.2.spot, bf16[40,128,128]{2,1,0:T(8,128)(2,1)S(1)} %bitcast.27, bf16[2048,256]{1,0:T(8,128)(2,1)S(1)} %copy-done.5), custom_call_target="tpu_custom_call" | custom-call | tf_op jit(solution)/shard_map/history_term/pallas_call | solution.py:179
  166.0 2.8 %collective-permute-start.6 = (bf16[2048,128]{1,0:T(8,128)(2,1)S(1)}, bf16[2048,128]{1,0:T(8,128)(2,1)S(1)}, u32[]{:S(2)}, u32[]{:S(2)}) collective-permute-start(bf16[2048,128]{1,0:T(8,128)(2,1)S(1)} %history_term.1.rest_0_), channel_id=1, source_target_pairs={{0,256},{256,0},{1,257},{257,1},{2,258},{258,2},{3,259},{259,3},{4... | collective-permute-start | bytes 1572872 | tf_op jit(solution)/shard_map/ppermute | solution.py:324
  168.8 39.5 %all-gather.7.cloned.1.call-done.same = bf16[2048,256]{1,0:T(8,128)(2,1)} async-done(((bf16[256,256]{1,0:T(8,128)(2,1)}), bf16[2048,256]{1,0:T(8,128)(2,1)}) %all-gather.7.cloned.1.call-update) | async-done | bytes 1048592 | tf_op jit(solution)/shard_map/all_gather | solution.py:267
  208.3 1.4 fusion.6
  209.7 1.9 collective-permute-start.5
  211.6 4.6 %collective-permute-start.4 = (bf16[1024,256]{1,0:T(8,128)(2,1)S(1)}, bf16[1024,256]{1,0:T(8,128)(2,1)S(1)}, u32[]{:S(2)}, u32[]{:S(2)}) collective-permute-start(bf16[1024,256]{1,0:T(8,128)(2,1)S(1)} %get-tuple-element.23), channel_id=1, source_target_pairs={{0,240},{16,0},{32,16},{48,32},{64,48},{80,64},{96,80},{112,96},{1... | collective-permute-start | bytes 1572872 | tf_op jit(solution)/shard_map/ppermute | solution.py:270
  216.2 7.0 %collective-permute-done.5.below = bf16[1024,256]{1,0:T(8,128)(2,1)S(1)} collective-permute-done((bf16[1024,256]{1,0:T(8,128)(2,1)S(1)}, bf16[1024,256]{1,0:T(8,128)(2,1)S(1)}, u32[]{:S(2)}, u32[]{:S(2)}) %collective-permute-start.5) | collective-permute-done | bytes 524320 | tf_op jit(solution)/shard_map/ppermute | solution.py:271
  224.1 8.0 %tile_product.3 = (bf16[8,2,128,256]{3,2,1,0:T(8,128)(2,1)S(1)}, bf16[8,2,128,256]{3,2,1,0:T(8,128)(2,1)S(1)}) custom-call(s32[128]{0:T(128)S(1)} %reshape.71.places, s32[32]{0:T(128)S(1)} %reshape.72.counts, s32[3]{0:T(128)S(1)} %pad_add_fusion.1.spot.spot_ref, bf16[64,128,128]{2,1,0:T(8,128)(2,1)S(1)} %bitcast.26, ...), custom_call_target="tpu_custom_call" | custom-call | tf_op jit(solution)/shard_map/tile_product/pallas_call | solution.py:134
  232.1 7.2 %collective-permute-start.7 = (bf16[8,2,128,256]{3,2,1,0:T(8,128)(2,1)S(1)}, bf16[8,2,128,256]{3,2,1,0:T(8,128)(2,1)S(1)}, u32[]{:S(2)}, u32[]{:S(2)}) collective-permute-start(bf16[8,2,128,256]{3,2,1,0:T(8,128)(2,1)S(1)} %get-tuple-element.21), channel_id=1, source_target_pairs={{0,1},{1,0},{2,3},{3,2},{4,5},{5,4},{6,7},{7,6},{8,9},{9,8},{10,11... | collective-permute-start | bytes 3145736 | tf_op jit(solution)/shard_map/ppermute | solution.py:277
  239.3 2.3 collective-permute-done.7
  241.9 20.3 %all_to_all.22.parts_ref = bf16[8,2,128,256]{3,2,1,0:T(8,128)(2,1)S(1)} all-to-all(bf16[8,2,128,256]{3,2,1,0:T(8,128)(2,1)S(1)} %add_convert_fusion), channel_id=1, replica_groups=mesh['x_lo'=2,'zh'=8,'zl'=2,'x_hi'=2,'y'=4,'core'=2] {'x_hi','y'}, dimensions={0} | all-to-all | bytes 2097152 | tf_op jit(solution)/shard_map/all_to_all | solution.py:279
  262.3 5.7 %all_to_all.23.halves_ref = bf16[2,128,256]{2,1,0:T(8,128)(2,1)S(1)} all-to-all(bf16[2,128,256]{2,1,0:T(8,128)(2,1)S(1)} %add_parts.3), channel_id=1, replica_groups=mesh['x_lo'=2,'zh'=8,'zl'=2,'x_hi'=2,'y'=4,'core'=2] {'x_lo'}, dimensions={0} | all-to-all | bytes 262144 | tf_op jit(solution)/shard_map/all_to_all | solution.py:332
  (56 shorter events, 8.7 us)
Async XLA Ops:
  7.2 84.4 %copy-start = (bf16[1,1,16,4,128,128]{5,4,3,2,1,0:T(8,128)(2,1)S(1)}, bf16[1,1,16,4,128,128]{5,4,3,2,1,0:T(8,128)(2,1)}, u32[]{:S(2)}) copy-start(bf16[1,1,16,4,128,128]{5,4,3,2,1,0:T(8,128)(2,1)} %param.12) | copy-start | bytes 6291460
  7.2 67.3 %all-gather.5.cloned.1.call-start = ((), (), s32[]{:S(2)}) async-start(), calls=%async_computation.4 | async-start | bytes 1179648 | tf_op jit(solution)/shard_map/all_gather | solution.py:267
  9.0 0.9 copy-start.8
  9.9 0.8 copy-start.9
  18.2 137.7 %all-gather.9.cloned.1.call-start = ((), (), s32[]{:S(2)}) async-start(), calls=%async_computation.6 | async-start | bytes 1179648 | tf_op jit(solution)/shard_map/all_gather | solution.py:322
  18.3 65.4 %collective-permute-start = (bf16[64,128,128]{2,1,0:T(8,128)(2,1)}, bf16[64,128,128]{2,1,0:T(8,128)(2,1)}, u32[]{:S(2)}, u32[]{:S(2)}) collective-permute-start(bf16[64,128,128]{2,1,0:T(8,128)(2,1)} %bitcast.24), channel_id=1, source_target_pairs={{0,256},{256,0},{1,257},{257,1},{2,258},{258,2},{3,259},{259,3},{4... | collective-permute-start | bytes 6291464 | tf_op jit(solution)/shard_map/ppermute | solution.py:313
  74.5 17.1 %copy-start.1 = (bf16[2048,256]{1,0:T(8,128)(2,1)S(1)}, bf16[2048,256]{1,0:T(8,128)(2,1)}, u32[]{:S(2)}) copy-start(bf16[2048,256]{1,0:T(8,128)(2,1)} %all-gather.5.cloned.1.call-done.same) | copy-start | bytes 3145732
  76.8 13.9 %collective-permute-start.2 = (bf16[1024,256]{1,0:T(8,128)(2,1)}, bf16[1024,256]{1,0:T(8,128)(2,1)}, u32[]{:S(2)}, u32[]{:S(2)}) collective-permute-start(bf16[1024,256]{1,0:T(8,128)(2,1)} %get-tuple-element.24), channel_id=1, source_target_pairs={{0,16},{16,32},{32,48},{48,64},{64,80},{80,96},{96,112},{112,128},... | collective-permute-start | bytes 1572872 | tf_op jit(solution)/shard_map/ppermute | solution.py:271
  78.7 12.9 %collective-permute-start.1 = (bf16[1024,256]{1,0:T(8,128)(2,1)}, bf16[1024,256]{1,0:T(8,128)(2,1)}, u32[]{:S(2)}, u32[]{:S(2)}) collective-permute-start(bf16[1024,256]{1,0:T(8,128)(2,1)} %get-tuple-element.25), channel_id=1, source_target_pairs={{0,240},{16,0},{32,16},{48,32},{64,48},{80,64},{96,80},{112,96},{1... | collective-permute-start | bytes 1572872 | tf_op jit(solution)/shard_map/ppermute | solution.py:270
  101.0 1.0 copy-start.4
  102.0 9.7 %collective-permute-start.3 = (bf16[8,2,128,256]{3,2,1,0:T(8,128)(2,1)}, bf16[8,2,128,256]{3,2,1,0:T(8,128)(2,1)S(1)}, u32[]{:S(2)}, u32[]{:S(2)}) collective-permute-start(bf16[8,2,128,256]{3,2,1,0:T(8,128)(2,1)} %get-tuple-element.16), channel_id=1, source_target_pairs={{0,1},{1,0},{2,3},{3,2},{4,5},{5,4},{6,7},{7,6},{8,9},{9,8},{10,11... | collective-permute-start | bytes 3145736 | tf_op jit(solution)/shard_map/ppermute | solution.py:277
  109.2 99.1 %all-gather.7.cloned.1.call-start = ((), (), s32[]{:S(2)}) async-start(), calls=%async_computation.5 | async-start | bytes 1179648 | tf_op jit(solution)/shard_map/all_gather | solution.py:267
  113.2 25.7 %copy-start.7 = (bf16[512,512]{1,0:T(8,128)(2,1)S(1)}, bf16[512,512]{1,0:T(8,128)(2,1)}, u32[]{:S(2)}) copy-start(bf16[512,512]{1,0:T(8,128)(2,1)} %weight_ref.2) | copy-start | bytes 1572868
  113.2 42.7 %copy-start.10 = (s32[32,40]{1,0:T(8,128)S(1)}, s32[32,40]{1,0:T(8,128)}, u32[]{:S(2)}) copy-start(s32[32,40]{1,0:T(8,128)} %listed.1) | copy-start | bytes 15364
  113.2 42.7 %copy-start.11 = (s32[1,40]{1,0:T(1,128)S(1)}, s32[1,40]{1,0:T(1,128)}, u32[]{:S(2)}) copy-start(s32[1,40]{1,0:T(1,128)} %param.19) | copy-start | bytes 484
  113.3 42.7 %copy-start.12 = (s32[1,40]{1,0:T(1,128)S(1)}, s32[1,40]{1,0:T(1,128)}, u32[]{:S(2)}) copy-start(s32[1,40]{1,0:T(1,128)} %param.18) | copy-start | bytes 484
  156.0 1.3 copy-start.3
  157.3 1.2 copy-start.5
  166.0 50.2 %collective-permute-start.6 = (bf16[2048,128]{1,0:T(8,128)(2,1)S(1)}, bf16[2048,128]{1,0:T(8,128)(2,1)S(1)}, u32[]{:S(2)}, u32[]{:S(2)}) collective-permute-start(bf16[2048,128]{1,0:T(8,128)(2,1)S(1)} %history_term.1.rest_0_), channel_id=1, source_target_pairs={{0,256},{256,0},{1,257},{257,1},{2,258},{258,2},{3,259},{259,3},{4... | collective-permute-start | bytes 1572872 | tf_op jit(solution)/shard_map/ppermute | solution.py:324
  208.3 15.8 %copy-start.2 = (bf16[2048,256]{1,0:T(8,128)(2,1)S(1)}, bf16[2048,256]{1,0:T(8,128)(2,1)}, u32[]{:S(2)}) copy-start(bf16[2048,256]{1,0:T(8,128)(2,1)} %all-gather.7.cloned.1.call-done.same) | copy-start | bytes 3145732
  209.7 13.6 %collective-permute-start.5 = (bf16[1024,256]{1,0:T(8,128)(2,1)S(1)}, bf16[1024,256]{1,0:T(8,128)(2,1)S(1)}, u32[]{:S(2)}, u32[]{:S(2)}) collective-permute-start(bf16[1024,256]{1,0:T(8,128)(2,1)S(1)} %get-tuple-element.22), channel_id=1, source_target_pairs={{0,16},{16,32},{32,48},{48,64},{64,80},{80,96},{96,112},{112,128},... | collective-permute-start | bytes 1572872 | tf_op jit(solution)/shard_map/ppermute | solution.py:271
  211.6 12.5 %collective-permute-start.4 = (bf16[1024,256]{1,0:T(8,128)(2,1)S(1)}, bf16[1024,256]{1,0:T(8,128)(2,1)S(1)}, u32[]{:S(2)}, u32[]{:S(2)}) collective-permute-start(bf16[1024,256]{1,0:T(8,128)(2,1)S(1)} %get-tuple-element.23), channel_id=1, source_target_pairs={{0,240},{16,0},{32,16},{48,32},{64,48},{80,64},{96,80},{112,96},{1... | collective-permute-start | bytes 1572872 | tf_op jit(solution)/shard_map/ppermute | solution.py:270
  232.1 9.5 %collective-permute-start.7 = (bf16[8,2,128,256]{3,2,1,0:T(8,128)(2,1)S(1)}, bf16[8,2,128,256]{3,2,1,0:T(8,128)(2,1)S(1)}, u32[]{:S(2)}, u32[]{:S(2)}) collective-permute-start(bf16[8,2,128,256]{3,2,1,0:T(8,128)(2,1)S(1)} %get-tuple-element.21), channel_id=1, source_target_pairs={{0,1},{1,0},{2,3},{3,2},{4,5},{5,4},{6,7},{7,6},{8,9},{9,8},{10,11... | collective-permute-start | bytes 3145736 | tf_op jit(solution)/shard_map/ppermute | solution.py:277
  241.9 26.1 %copy-start.6 = (bf16[512,512]{1,0:T(8,128)(2,1)S(1)}, bf16[512,512]{1,0:T(8,128)(2,1)}, u32[]{:S(2)}) copy-start(bf16[512,512]{1,0:T(8,128)(2,1)} %weight_ref.3) | copy-start | bytes 1572868
Sparse Core Ops, SparseCore 0:
  18.3 56.0 all-gather.4
  109.4 46.5 all-gather.8
  158.6 49.6 all-gather.6

commit v3 on v2

v3 whole, which is shorter than its diff:
```python
import functools

import jax
import jax.numpy as jnp
from jax import lax
from jax.experimental import pallas as pl
from jax.experimental.pallas import tpu as pltpu
from jax.sharding import Mesh, PartitionSpec as P

F = 512
HALF = 256
BLOCK = 128
HOWN = 4
ROWS = 16
SLOTS = 4
FEAT = 32
LIST = 40
WIDE = 128
META = 16
CARRY = BLOCK + 2 * FEAT
PAY = CARRY + META
DOM = ("x_lo", "z")
GRID = ("x_hi", "y", "core")
SIDE = ("x_hi", "y")
SWAP = [(0, 1), (1, 0)]
UP = [(z, (z + 1) % 16) for z in range(16)]
DOWN = [(z, (z + 15) % 16) for z in range(16)]


def params(mib):
    return pltpu.CompilerParams(vmem_limit_bytes=mib << 20)


def payload_body(cols, counts, feats, hist, out, feats_in, hist_in, sems):
    moves = [
        pltpu.make_async_copy(feats, feats_in, sems.at[0]),
        pltpu.make_async_copy(hist, hist_in, sems.at[1]),
    ]
    for move in moves:
        move.start()
    lane = lax.broadcasted_iota(jnp.int32, (META, HALF), 1)
    meta = jnp.zeros((META, HALF), jnp.float32)
    for row in range(ROWS):
        for slot in range(SLOTS):
            meta = jnp.where(lane == row * SLOTS + slot, cols[slot, row].astype(jnp.float32), meta)
        meta = jnp.where(lane == ROWS * SLOTS + row, counts[row].astype(jnp.float32), meta)
    meta = meta.astype(jnp.bfloat16)
    for move in moves:
        move.wait()
    for j in range(2):
        out[j, :BLOCK] = feats_in[:, j * HALF : (j + 1) * HALF]
        for k in range(2):
            start = BLOCK + k * FEAT
            out[j, start : start + FEAT] = hist_in[:, k * HALF : (k + 1) * HALF]
        out[j, CARRY:] = meta


def make_payload(cols, counts, feats, hist):
    return pl.pallas_call(
        payload_body,
        out_shape=jax.ShapeDtypeStruct((2, PAY, HALF), jnp.bfloat16),
        grid_spec=pltpu.PrefetchScalarGridSpec(
            num_scalar_prefetch=2,
            grid=(1,),
            in_specs=[pl.BlockSpec(memory_space=pltpu.HBM)] * 2,
            out_specs=pl.BlockSpec((2, PAY, HALF), lambda i, *_: (0, 0, 0)),
            scratch_shapes=[
                pltpu.VMEM(feats.shape, jnp.bfloat16),
                pltpu.VMEM(hist.shape, jnp.bfloat16),
                pltpu.SemaphoreType.DMA((2,)),
            ],
        ),
        compiler_params=params(8),
        name="payload",
    )(cols, counts, feats, hist)


def tile_body(n_chunks, stride, with_extra, cols, counts, theirs, spot, own, partner, *rest):
    chunks = rest[:n_chunks]
    extras = rest[n_chunks : n_chunks + 2] if with_extra else ()
    keep, send, panel, adj, sems = rest[-5:]
    core = spot[1]
    moves = []
    start = 0
    for source in chunks:
        size = source.shape[0]
        target = panel.at[pl.ds(start, size)]
        moves.append(pltpu.make_async_copy(source, target, sems.at[len(moves)]))
        start += size
    for k, source in enumerate((own, partner)):
        for c in range(4):
            target = adj.at[pl.ds(64 * k + 16 * c, 16)]
            moves.append(
                pltpu.make_async_copy(
                    source.at[pl.ds(16 * c, 16)], target, sems.at[len(moves)]
                )
            )
    for move in moves:
        move.start()

    def product(k, row):
        base = (ROWS * k + row) * SLOTS
        count = counts[row] if k == 0 else theirs[ROWS * SLOTS + row]
        left = []
        right = []
        for slot in range(SLOTS):
            block = adj[base + slot]
            left.append(jnp.where(slot < count, block, jnp.zeros_like(block)))
            col = cols[slot, row] if k == 0 else theirs[row * SLOTS + slot]
            place = (((col & 15) - spot[3]) & 15) * 2 + (col >> 4)
            right.append(panel[pl.ds(pl.multiple_of(place * stride, 2 * FEAT), BLOCK), :])
        return jnp.dot(
            jnp.concatenate(left, axis=1),
            jnp.concatenate(right, axis=0),
            preferred_element_type=jnp.float32,
        )

    def with_history(k, row, value):
        start = pl.multiple_of(row * BLOCK, BLOCK)
        piece = extras[k][pl.ds(start, BLOCK), :].astype(jnp.float32)
        zero = jnp.zeros_like(piece)
        wide = [jnp.where(spot[2] == group, piece, zero) for group in range(2)]
        return value + jnp.concatenate(wide, axis=1)

    def two_rows(k, j):
        part = spot[0] if k == 0 else 1 - spot[0]
        pair = [product(k, 2 * j + side) for side in range(2)]
        if with_extra:
            pair = [with_history(k, 2 * j + side, pair[side]) for side in range(2)]
        even, odd = [value.astype(jnp.bfloat16) for value in pair]
        keep[j, part] = jnp.where(core == 0, even, odd)
        send[j, part] = jnp.where(core == 0, odd, even)

    for n in range(n_chunks):
        moves[n].wait()
    for k in range(2):
        for c in range(4):
            moves[n_chunks + 4 * k + c].wait()
            two_rows(k, 2 * c)
            two_rows(k, 2 * c + 1)


def tile_product(cols, counts, theirs, spot, own, partner, chunks, extras):
    operands = [own, partner, *chunks]
    specs = [pl.BlockSpec(memory_space=pltpu.HBM)] * len(operands)
    stride = chunks[0].shape[0] // 2
    for extra in extras:
        operands.append(extra)
        specs.append(pl.BlockSpec(extra.shape, lambda i, *_: (0, 0)))
    half = jax.ShapeDtypeStruct((ROWS // 2, 2, BLOCK, HALF), jnp.bfloat16)
    out_spec = pl.BlockSpec(half.shape, lambda i, *_: (0, 0, 0, 0))
    return pl.pallas_call(
        functools.partial(tile_body, len(chunks), stride, bool(extras)),
        out_shape=(half, half),
        grid_spec=pltpu.PrefetchScalarGridSpec(
            num_scalar_prefetch=4,
            grid=(1,),
            in_specs=specs,
            out_specs=(out_spec, out_spec),
            scratch_shapes=[
                pltpu.VMEM((32 * stride, HALF), jnp.bfloat16),
                pltpu.VMEM((2 * ROWS * SLOTS, BLOCK, BLOCK), jnp.bfloat16),
                pltpu.SemaphoreType.DMA((len(chunks) + 8,)),
            ],
        ),
        compiler_params=params(20),
        name="tile_product",
    )(cols, counts, theirs, spot, *operands)


def history_body(n_chunks, listed, order, rows, spot, adj, *rest):
    chunks = rest[:n_chunks]
    out, weights, store, total, sems = rest[n_chunks:]
    moves = [pltpu.make_async_copy(adj, weights, sems.at[0])]
    start = 0
    for source in chunks:
        for k in range(source.shape[0] // CARRY):
            moves.append(
                pltpu.make_async_copy(
                    source.at[pl.ds(k * CARRY + BLOCK, 2 * FEAT)],
                    store.at[pl.ds(start, 2 * FEAT)],
                    sems.at[len(moves)],
                )
            )
            start += 2 * FEAT
    for move in moves:
        move.start()
    total[...] = jnp.zeros_like(total)
    for move in moves:
        move.wait()

    def one(slot):
        block = listed[spot[0], order[slot]]
        owner = block >> 2
        piece = block & 3
        place = (((owner & 15) - spot[2]) & 15) * 2 + (owner >> 4)
        source = pl.multiple_of(place * (2 * FEAT) + (piece >> 1) * FEAT, FEAT)
        lane = pl.multiple_of((piece & 1) * BLOCK, BLOCK)
        return lax.dot_general(
            weights[slot],
            store[pl.ds(source, FEAT), pl.ds(lane, BLOCK)],
            (((1,), (1,)), ((), ())),
            preferred_element_type=jnp.float32,
        )

    def step(n, carry):
        parts = [one(n * 5 + k) for k in range(5)]
        for k, part in enumerate(parts):
            target = pl.multiple_of(rows[n * 5 + k] * BLOCK, BLOCK)
            total[pl.ds(target, BLOCK), :FEAT] += part
        return carry

    lax.fori_loop(0, LIST // 5, step, 0)
    out[...] = pltpu.roll(total[...], spot[1] * FEAT, 1).astype(jnp.bfloat16)


def history_term(listed, order, rows, spot, adj, chunks):
    return pl.pallas_call(
        functools.partial(history_body, len(chunks)),
        out_shape=jax.ShapeDtypeStruct((ROWS * BLOCK, WIDE), jnp.bfloat16),
        grid_spec=pltpu.PrefetchScalarGridSpec(
            num_scalar_prefetch=4,
            grid=(1,),
            in_specs=[pl.BlockSpec(memory_space=pltpu.HBM)] * (1 + len(chunks)),
            out_specs=pl.BlockSpec((ROWS * BLOCK, WIDE), lambda i, *_: (0, 0)),
            scratch_shapes=[
                pltpu.VMEM(adj.shape, jnp.bfloat16),
                pltpu.VMEM((64 * FEAT, HALF), jnp.bfloat16),
                pltpu.VMEM((ROWS * BLOCK, WIDE), jnp.float32),
                pltpu.SemaphoreType.DMA((33,)),
            ],
        ),
        compiler_params=params(16),
        name="history_term",
    )(listed, order, rows, spot, adj, *chunks)


def add_parts(parts):
    def body(parts_ref, out):
        total = parts_ref[0].astype(jnp.float32)
        for k in range(1, parts.shape[0]):
            total = total + parts_ref[k].astype(jnp.float32)
        out[...] = total.astype(jnp.bfloat16)

    return pl.pallas_call(
        body,
        out_shape=jax.ShapeDtypeStruct(parts.shape[1:], jnp.bfloat16),
        compiler_params=params(8),
        name="add_parts",
    )(parts)


def first_dense(halves, weight, spot):
    def body(spot_ref, halves_ref, weight_ref, hidden, chunk):
        rows = [
            jnp.concatenate([halves_ref[0, part], halves_ref[1, part]], axis=1)
            for part in range(2)
        ]
        value = jnp.dot(
            jnp.concatenate(rows, axis=0), weight_ref[...], preferred_element_type=jnp.float32
        )
        value = jnp.maximum(value, 0.0).astype(jnp.bfloat16)
        low = spot_ref[0] == 0
        hidden[...] = jnp.where(low, value[:BLOCK], value[BLOCK:])
        chunk[...] = jnp.where(low, value[:, :HALF], value[:, HALF:])

    return pl.pallas_call(
        body,
        out_shape=(
            jax.ShapeDtypeStruct((BLOCK, F), jnp.bfloat16),
            jax.ShapeDtypeStruct((2 * BLOCK, HALF), jnp.bfloat16),
        ),
        grid_spec=pltpu.PrefetchScalarGridSpec(
            num_scalar_prefetch=1,
            grid=(1,),
            in_specs=[
                pl.BlockSpec(halves.shape, lambda i, *_: (0, 0, 0, 0)),
                pl.BlockSpec(weight.shape, lambda i, *_: (0, 0)),
            ],
            out_specs=(
                pl.BlockSpec((BLOCK, F), lambda i, *_: (0, 0)),
                pl.BlockSpec((2 * BLOCK, HALF), lambda i, *_: (0, 0)),
            ),
        ),
        compiler_params=params(8),
        name="first_dense",
    )(spot, halves, weight)


def second_dense(halves, weight):
    def body(halves_ref, weight_ref, out):
        rows = jnp.concatenate([halves_ref[0], halves_ref[1]], axis=1)
        value = jnp.dot(rows, weight_ref[...], preferred_element_type=jnp.float32)
        out[...] = value.astype(jnp.bfloat16)

    return pl.pallas_call(
        body,
        out_shape=jax.ShapeDtypeStruct((BLOCK, F), jnp.bfloat16),
        compiler_params=params(8),
        name="second_dense",
    )(halves, weight)


def gather_ring(chunk):
    up = [chunk]
    down = [chunk]
    for _ in range(7):
        up.append(lax.ppermute(up[-1], "z", UP))
        down.append(lax.ppermute(down[-1], "z", DOWN))
    half = chunk.shape[0] // 2
    far = [
        lax.ppermute(down[7][:half], "z", DOWN),
        lax.ppermute(up[7][half:], "z", UP),
    ]
    return down + far + up[:0:-1]


def reduce_rows(keep, send):
    other = lax.ppermute(send, "core", SWAP)
    both = (keep.astype(jnp.float32) + other.astype(jnp.float32)).astype(jnp.bfloat16)
    return add_parts(lax.all_to_all(both, SIDE, 0, 0, tiled=True))


def local(
    node_feats,
    adj_vals,
    adj_col,
    adj_count,
    hist_store,
    hist_list,
    hist_adj,
    hist_row,
    hist_col,
    w_first,
    w_second,
):
    adj = adj_vals[0, 0].reshape(ROWS * SLOTS, BLOCK, BLOCK)
    cols = adj_col[0, 0].T
    counts = adj_count[0, 0]
    x_lo = lax.axis_index("x_lo")
    x_hi = lax.axis_index("x_hi")
    grid_index = lax.axis_index(GRID)
    group = jnp.where(x_lo == x_hi, (grid_index // 4) % 2, -1)
    spot = jnp.stack([x_lo, lax.axis_index("core"), group, lax.axis_index("z")])
    spot = spot.astype(jnp.int32)
    hist_spot = jnp.stack([lax.axis_index(DOM), grid_index % 4, lax.axis_index("z")]).astype(jnp.int32)

    payload = make_payload(
        cols,
        counts,
        pltpu.with_memory_space_constraint(node_feats, pltpu.HBM),
        pltpu.with_memory_space_constraint(hist_store, pltpu.HBM),
    )
    received = lax.all_to_all(payload, "x_lo", 0, 0, tiled=True)
    adj_held, received = lax.optimization_barrier((adj, received))
    partner = lax.ppermute(adj_held, "x_lo", SWAP)
    chunks = gather_ring(received[:, :CARRY].reshape(2 * CARRY, HALF))
    chunks = [pltpu.with_memory_space_constraint(chunk, pltpu.HBM) for chunk in chunks]
    partner = pltpu.with_memory_space_constraint(partner, pltpu.HBM)
    adj = pltpu.with_memory_space_constraint(adj, pltpu.HBM)
    theirs = lax.dynamic_index_in_dim(received[:, CARRY, :80], 1 - x_lo, 0, False)
    theirs = theirs.astype(jnp.int32)
    mine = history_term(hist_list, hist_col[0], hist_row[0], hist_spot, hist_adj[0], chunks)

    tables = (cols, counts, theirs, spot)
    agg = reduce_rows(*tile_product(*tables, adj, partner, chunks, ()))
    halves = lax.all_gather(agg, "x_lo", axis=0, tiled=False)
    hidden, chunk = first_dense(halves, w_first, spot)

    chunk, mine = lax.optimization_barrier((chunk, mine))
    extras = (mine, lax.ppermute(mine, "x_lo", SWAP))
    chunks = gather_ring(chunk)
    agg = reduce_rows(*tile_product(*tables, adj, partner, chunks, extras))
    embedding = second_dense(lax.all_to_all(agg, "x_lo", 0, 0, tiled=True), w_second)
    return hidden, embedding


def solution(mesh):
    fine = Mesh(
        mesh.devices.reshape(2, 16, 2, 4, 2), ("x_lo", "z", "x_hi", "y", "core")
    )
    placed = (
        P(DOM + GRID, None),
        P(DOM, GRID),
        P(DOM, GRID),
        P(DOM, GRID),
        P(GRID, DOM),
        P(),
        P(DOM),
        P(DOM),
        P(DOM),
        P(),
        P(),
    )
    return jax.shard_map(
        local,
        mesh=fine,
        in_specs=placed,
        out_specs=(P(DOM + GRID, None), P(DOM + GRID, None)),
        check_vma=False,
    )
```

time: 278 us -> 251 us (0.903)
  starting transfers between devices: 32.2 us -> 149 us
  waiting for transfers between devices: 124 us -> 32.2 us
  blocking collectives: 62.9 us -> 38.8 us
  between operations: 14 us -> 1.4 us
  Pallas kernels: 27.6 us -> 21.1 us
  local copies, waits for them, and re-layouts: 10.9 us -> 4.73 us
    all_gather x3 -> x0, waiting for transfers between devices: 103 us -> none  [the longest x2 87.6 us: gather_panel(): same = lax.all_gather(chunk, 'zh', axis=0, tiled=True)]
    ppermute x4 -> x32, starting transfers between devices: 13 us -> 112 us  [the longest x14 69.9 us: gather_ring(): down.append(lax.ppermute(down[-1], 'z', DOWN))]
    all_to_all x2 -> x1, blocking collectives: 40.9 us -> 21.3 us  [reduce_rows(): return add_parts(lax.all_to_all(both, SIDE, 0, 0, tiled=True))]
    ppermute x2, starting transfers between devices: 14.3 us -> 25.1 us  [reduce_rows(): other = lax.ppermute(send, 'core', SWAP)]
    all_to_all x0 -> x1, waiting for transfers between devices: none -> 10.2 us  [reduce_rows(): return add_parts(lax.all_to_all(both, SIDE, 0, 0, tiled=True))]
    pallas_call x3, Pallas kernels: 24.9 us -> 17 us  [the longest x2 12.8 us: tile_product(): pl.pallas_call(functools.partial(tile_body, len(chunks), stride, bool(ext...]
    all_to_all x0 -> x1, starting transfers between devices: none -> 6.45 us  [reduce_rows(): return add_parts(lax.all_to_all(both, SIDE, 0, 0, tiled=True))]
    all_gather x1 -> x0, blocking collectives: 4.5 us -> none  [local(): lax.all_gather(received[:, BLOCK:BLOCK + 2 * FEAT].reshape(4 * FEAT, HALF...]
  transfers between devices with their start and end apart: 11 -> 37, of which waited for: 9 -> 19; matrix products, arithmetic and copies ran while one was open for 3% -> 0% of each run, Pallas kernels for 3% -> 2%
where the time goes in v3:
time: 251 us; the launch traced here: 249 us
  starting transfers between devices  149 us (59%)
  blocking collectives  38.8 us (15%)
  waiting for transfers between devices  32.2 us (13%)
  Pallas kernels  21.1 us (8%)
  local copies, waits for them, and re-layouts  4.73 us (2%)
    ppermute x14, starting transfers between devices, gather_ring(): down.append(lax.ppermute(down[-1], 'z', DOWN))  69.9 us
    ppermute x14, starting transfers between devices, gather_ring(): up.append(lax.ppermute(up[-1], 'z', UP))  28.8 us
    ppermute x2, starting transfers between devices, reduce_rows(): other = lax.ppermute(send, 'core', SWAP)  25.1 us
    all_to_all x1, blocking collectives, reduce_rows(): return add_parts(lax.all_to_all(both, SIDE, 0, 0, tiled=True))  21.3 us
    ppermute x14, waiting for transfers between devices, gather_ring(): up.append(lax.ppermute(up[-1], 'z', UP))  14.3 us
    pallas_call x2, Pallas kernels, tile_product(): pl.pallas_call(functools.partial(tile_body, len(chunks), stride, bool(ext...  12.8 us
    all_to_all x1, waiting for transfers between devices, reduce_rows(): return add_parts(lax.all_to_all(both, SIDE, 0, 0, tiled=True))  10.2 us
    ppermute x2, starting transfers between devices, gather_ring(): lax.ppermute(down[7][:half], 'z', DOWN)  9.66 us
  transfers between devices with their start and end apart: 37, of which 19 were waited for; matrix products, arithmetic and copies ran while one was open for 0% of the time, Pallas kernels for 2%

profile of v3, /device:TPU:1, one launch (start us, length us, event | category | flops | bytes accessed | tf_op | source)
XLA Modules:
  0.0 249.1 jit_solution(4213825076506760157)
XLA Ops:
  3.5 6.9 %all_to_all.20 = bf16[2,208,256]{2,1,0:T(8,128)(2,1)S(1)} all-to-all(bf16[2,208,256]{2,1,0:T(8,128)(2,1)S(1)} %payload.1), channel_id=1, replica_groups=mesh['x_lo'=2,'z'=16,'x_hi'=2,'y'=4,'core'=2] {'x_lo'}, dimensions={0} | all-to-all | bytes 425984 | tf_op jit(solution)/shard_map/all_to_all | solution.py:354
  12.3 4.0 %collective-permute-start.9 = (bf16[384,256]{1,0:T(8,128)(2,1)S(1)}, bf16[384,256]{1,0:T(8,128)(2,1)S(1)}, u32[]{:S(2)}, u32[]{:S(2)}) collective-permute-start(bf16[384,256]{1,0:T(8,128)(2,1)S(1)} %bitcast.32), channel_id=1, source_target_pairs={{0,16},{16,32},{32,48},{48,64},{64,80},{80,96},{96,112},{112,128},... | collective-permute-start | bytes 589832 | tf_op jit(solution)/shard_map/ppermute | solution.py:308
  16.3 9.5 %collective-permute-start.1 = (bf16[384,256]{1,0:T(8,128)(2,1)S(1)}, bf16[384,256]{1,0:T(8,128)(2,1)S(1)}, u32[]{:S(2)}, u32[]{:S(2)}) collective-permute-start(bf16[384,256]{1,0:T(8,128)(2,1)S(1)} %bitcast.33), channel_id=1, source_target_pairs={{0,240},{16,0},{32,16},{48,32},{64,48},{80,64},{96,80},{112,96},{1... | collective-permute-start | bytes 589832 | tf_op jit(solution)/shard_map/ppermute | solution.py:309
  29.3 4.6 %collective-permute-start.2 = (bf16[384,256]{1,0:T(8,128)(2,1)S(1)}, bf16[384,256]{1,0:T(8,128)(2,1)S(1)}, u32[]{:S(2)}, u32[]{:S(2)}) collective-permute-start(bf16[384,256]{1,0:T(8,128)(2,1)S(1)} %collective-permute-done.1.rest_1_), channel_id=1, source_target_pairs={{0,240},{16,0},{32,16},{48,32},{64,48},{80,64},{96,80},{112,96},{1... | collective-permute-start | bytes 589832 | tf_op jit(solution)/shard_map/ppermute | solution.py:309
  36.9 4.6 %collective-permute-start.3 = (bf16[384,256]{1,0:T(8,128)(2,1)S(1)}, bf16[384,256]{1,0:T(8,128)(2,1)S(1)}, u32[]{:S(2)}, u32[]{:S(2)}) collective-permute-start(bf16[384,256]{1,0:T(8,128)(2,1)S(1)} %collective-permute-done.2.rest_2_), channel_id=1, source_target_pairs={{0,240},{16,0},{32,16},{48,32},{64,48},{80,64},{96,80},{112,96},{1... | collective-permute-start | bytes 589832 | tf_op jit(solution)/shard_map/ppermute | solution.py:309
  44.5 4.6 %collective-permute-start.4 = (bf16[384,256]{1,0:T(8,128)(2,1)S(1)}, bf16[384,256]{1,0:T(8,128)(2,1)S(1)}, u32[]{:S(2)}, u32[]{:S(2)}) collective-permute-start(bf16[384,256]{1,0:T(8,128)(2,1)S(1)} %collective-permute-done.3.rest_3_), channel_id=1, source_target_pairs={{0,240},{16,0},{32,16},{48,32},{64,48},{80,64},{96,80},{112,96},{1... | collective-permute-start | bytes 589832 | tf_op jit(solution)/shard_map/ppermute | solution.py:309
  52.2 4.6 %collective-permute-start.5 = (bf16[384,256]{1,0:T(8,128)(2,1)S(1)}, bf16[384,256]{1,0:T(8,128)(2,1)S(1)}, u32[]{:S(2)}, u32[]{:S(2)}) collective-permute-start(bf16[384,256]{1,0:T(8,128)(2,1)S(1)} %collective-permute-done.4.rest_4_), channel_id=1, source_target_pairs={{0,240},{16,0},{32,16},{48,32},{64,48},{80,64},{96,80},{112,96},{1... | collective-permute-start | bytes 589832 | tf_op jit(solution)/shard_map/ppermute | solution.py:309
  59.8 4.6 %collective-permute-start.6 = (bf16[384,256]{1,0:T(8,128)(2,1)S(1)}, bf16[384,256]{1,0:T(8,128)(2,1)}, u32[]{:S(2)}, u32[]{:S(2)}) collective-permute-start(bf16[384,256]{1,0:T(8,128)(2,1)S(1)} %collective-permute-done.5.rest_5_), channel_id=1, source_target_pairs={{0,240},{16,0},{32,16},{48,32},{64,48},{80,64},{96,80},{112,96},{1... | collective-permute-start | bytes 589832 | tf_op jit(solution)/shard_map/ppermute | solution.py:309
  68.3 4.8 %collective-permute-start.7 = (bf16[384,256]{1,0:T(8,128)(2,1)}, bf16[384,256]{1,0:T(8,128)(2,1)S(1)}, u32[]{:S(2)}, u32[]{:S(2)}) collective-permute-start(bf16[384,256]{1,0:T(8,128)(2,1)} %collective-permute-done.6.rest_6_), channel_id=1, source_target_pairs={{0,240},{16,0},{32,16},{48,32},{64,48},{80,64},{96,80},{112,96},{1... | collective-permute-start | bytes 589832 | tf_op jit(solution)/shard_map/ppermute | solution.py:309
  73.3 2.4 collective-permute-done.15.rest_10_
  77.9 5.1 %collective-permute-start.8 = (bf16[192,256]{1,0:T(8,128)(2,1)S(1)}, bf16[192,256]{1,0:T(8,128)(2,1)S(1)}, u32[]{:S(2)}, u32[]{:S(2)}) collective-permute-start(bf16[192,256]{1,0:T(8,128)(2,1)S(1)} %slice.24), channel_id=1, source_target_pairs={{0,240},{16,0},{32,16},{48,32},{64,48},{80,64},{96,80},{112,96},{1... | collective-permute-start | bytes 294920 | tf_op jit(solution)/shard_map/ppermute | solution.py:312
  87.9 5.4 %tile_product.2 = (bf16[8,2,128,256]{3,2,1,0:T(8,128)(2,1)S(1)}, bf16[8,2,128,256]{3,2,1,0:T(8,128)(2,1)S(1)}) custom-call(s32[4,16]{1,0:T(4,128)S(1)} %bitcast.22, s32[16]{0:T(128)S(1)} %bitcast.25, s32[80]{0:T(128)S(1)} %bitcast_convert_fusion.theirs, s32[4]{0:T(128)S(1)} %pad_add_fusion.spot.spot_ref, bf16[64,128,128]{2,1,0:T(8,128)(2,1)} %bitcast.30, ...), custom_call_target="tpu_custom_call" | custom-call | tf_op jit(solution)/shard_map/tile_product/pallas_call | solution.py:152
  93.3 12.2 %collective-permute-start.17 = (bf16[8,2,128,256]{3,2,1,0:T(8,128)(2,1)S(1)}, bf16[8,2,128,256]{3,2,1,0:T(8,128)(2,1)S(1)}, u32[]{:S(2)}, u32[]{:S(2)}) collective-permute-start(bf16[8,2,128,256]{3,2,1,0:T(8,128)(2,1)S(1)} %get-tuple-element.15), channel_id=1, source_target_pairs={{0,1},{1,0},{2,3},{3,2},{4,5},{5,4},{6,7},{7,6},{8,9},{9,8},{10,11... | collective-permute-start | bytes 3145736 | tf_op jit(solution)/shard_map/ppermute | solution.py:319
  105.6 2.3 collective-permute-done.17
  109.1 6.4 %all-to-all-start.1 = ((bf16[8,2,128,256]{3,2,1,0:T(8,128)(2,1)}), bf16[8,2,128,256]{3,2,1,0:T(8,128)(2,1)S(1)}, u32[]{:S(2)}, u32[]{:S(2)}) async-start(bf16[8,2,128,256]{3,2,1,0:T(8,128)(2,1)} %add_convert_fusion.1), calls=%async_computation.1 | async-start | bytes 2097152 | tf_op jit(solution)/shard_map/all_to_all | solution.py:321
  115.7 4.2 %history_term.1.rest_17_ = bf16[2048,128]{1,0:T(8,128)(2,1)S(1)} custom-call(s32[32,40]{1,0:T(8,128)S(1)} %copy-done.6, s32[40]{0:T(128)S(1)} %bitcast.27, s32[40]{0:T(128)S(1)} %bitcast.28, s32[3]{0:T(128)S(1)} %pad_add_fusion.1.spot, bf16[40,128,128]{2,1,0:T(8,128)(2,1)S(1)} %bitcast.19, bf16[384,256]{1,0:T(8,128)(2,1)} %bitcast.35, ...), custom_call_target="tpu_custom_call" | custom-call | tf_op jit(solution)/shard_map/history_term/pallas_call | solution.py:218
  119.9 10.2 %all-to-all-done.1.parts_ref = bf16[8,2,128,256]{3,2,1,0:T(8,128)(2,1)S(1)} async-done(((bf16[8,2,128,256]{3,2,1,0:T(8,128)(2,1)}), bf16[8,2,128,256]{3,2,1,0:T(8,128)(2,1)S(1)}, u32[]{:S(2)}, u32[]{:S(2)}) %all-to-all-start.1) | async-done | bytes 1048608 | tf_op jit(solution)/shard_map/all_to_all | solution.py:321
  130.3 5.0 %all-gather = bf16[4,128,256]{2,1,0:T(8,128)(2,1)S(1)} all-gather(bf16[2,128,256]{2,1,0:T(8,128)(2,1)S(1)} %add_parts.2), channel_id=2, replica_groups=mesh['x_lo'=2,'z'=16,'x_hi'=2,'y'=4,'core'=2] {'x_lo'}, dimensions={0}, use_global_device_ids=true | all-gather | bytes 393216 | tf_op jit(solution)/shard_map/all_gather | solution.py:367
  138.7 5.2 %collective-permute-start.18 = (bf16[256,256]{1,0:T(8,128)(2,1)S(1)}, bf16[256,256]{1,0:T(8,128)(2,1)S(1)}, u32[]{:S(2)}, u32[]{:S(2)}) collective-permute-start(bf16[256,256]{1,0:T(8,128)(2,1)S(1)} %get-tuple-element.18.rest_0_), channel_id=1, source_target_pairs={{0,240},{16,0},{32,16},{48,32},{64,48},{80,64},{96,80},{112,96},{1... | collective-permute-start | bytes 393224 | tf_op jit(solution)/shard_map/ppermute | solution.py:309
  146.3 4.6 %collective-permute-start.19 = (bf16[256,256]{1,0:T(8,128)(2,1)S(1)}, bf16[256,256]{1,0:T(8,128)(2,1)S(1)}, u32[]{:S(2)}, u32[]{:S(2)}) collective-permute-start(bf16[256,256]{1,0:T(8,128)(2,1)S(1)} %collective-permute-done.18.rest_1_), channel_id=1, source_target_pairs={{0,240},{16,0},{32,16},{48,32},{64,48},{80,64},{96,80},{112,96},{1... | collective-permute-start | bytes 393224 | tf_op jit(solution)/shard_map/ppermute | solution.py:309
  153.2 4.6 %collective-permute-start.20 = (bf16[256,256]{1,0:T(8,128)(2,1)S(1)}, bf16[256,256]{1,0:T(8,128)(2,1)S(1)}, u32[]{:S(2)}, u32[]{:S(2)}) collective-permute-start(bf16[256,256]{1,0:T(8,128)(2,1)S(1)} %collective-permute-done.19.rest_2_), channel_id=1, source_target_pairs={{0,240},{16,0},{32,16},{48,32},{64,48},{80,64},{96,80},{112,96},{1... | collective-permute-start | bytes 393224 | tf_op jit(solution)/shard_map/ppermute | solution.py:309
  160.1 4.6 %collective-permute-start.21 = (bf16[256,256]{1,0:T(8,128)(2,1)S(1)}, bf16[256,256]{1,0:T(8,128)(2,1)S(1)}, u32[]{:S(2)}, u32[]{:S(2)}) collective-permute-start(bf16[256,256]{1,0:T(8,128)(2,1)S(1)} %collective-permute-done.20.rest_3_), channel_id=1, source_target_pairs={{0,240},{16,0},{32,16},{48,32},{64,48},{80,64},{96,80},{112,96},{1... | collective-permute-start | bytes 393224 | tf_op jit(solution)/shard_map/ppermute | solution.py:309
  164.7 3.4 %collective-permute-start.34 = (bf16[2048,128]{1,0:T(8,128)(2,1)S(1)}, bf16[2048,128]{1,0:T(8,128)(2,1)S(1)}, u32[]{:S(2)}, u32[]{:S(2)}) collective-permute-start(bf16[2048,128]{1,0:T(8,128)(2,1)S(1)} %history_term.1.rest_17_), channel_id=1, source_target_pairs={{0,256},{256,0},{1,257},{257,1},{2,258},{258,2},{3,259},{259,3},{4... | collective-permute-start | bytes 1572872 | tf_op jit(solution)/shard_map/ppermute | solution.py:371
  170.0 4.6 %collective-permute-start.22 = (bf16[256,256]{1,0:T(8,128)(2,1)S(1)}, bf16[256,256]{1,0:T(8,128)(2,1)S(1)}, u32[]{:S(2)}, u32[]{:S(2)}) collective-permute-start(bf16[256,256]{1,0:T(8,128)(2,1)S(1)} %collective-permute-done.21.rest_4_), channel_id=1, source_target_pairs={{0,240},{16,0},{32,16},{48,32},{64,48},{80,64},{96,80},{112,96},{1... | collective-permute-start | bytes 393224 | tf_op jit(solution)/shard_map/ppermute | solution.py:309
  176.9 4.6 %collective-permute-start.23 = (bf16[256,256]{1,0:T(8,128)(2,1)S(1)}, bf16[256,256]{1,0:T(8,128)(2,1)S(1)}, u32[]{:S(2)}, u32[]{:S(2)}) collective-permute-start(bf16[256,256]{1,0:T(8,128)(2,1)S(1)} %collective-permute-done.22.rest_5_), channel_id=1, source_target_pairs={{0,240},{16,0},{32,16},{48,32},{64,48},{80,64},{96,80},{112,96},{1... | collective-permute-start | bytes 393224 | tf_op jit(solution)/shard_map/ppermute | solution.py:309
  185.1 4.6 %collective-permute-start.24 = (bf16[256,256]{1,0:T(8,128)(2,1)S(1)}, bf16[256,256]{1,0:T(8,128)(2,1)S(1)}, u32[]{:S(2)}, u32[]{:S(2)}) collective-permute-start(bf16[256,256]{1,0:T(8,128)(2,1)S(1)} %collective-permute-done.23.rest_6_), channel_id=1, source_target_pairs={{0,240},{16,0},{32,16},{48,32},{64,48},{80,64},{96,80},{112,96},{1... | collective-permute-start | bytes 393224 | tf_op jit(solution)/shard_map/ppermute | solution.py:309
  192.3 4.6 %collective-permute-start.25 = (bf16[128,256]{1,0:T(8,128)(2,1)S(1)}, bf16[128,256]{1,0:T(8,128)(2,1)S(1)}, u32[]{:S(2)}, u32[]{:S(2)}) collective-permute-start(bf16[128,256]{1,0:T(8,128)(2,1)S(1)} %slice.26), channel_id=1, source_target_pairs={{0,240},{16,0},{32,16},{48,32},{64,48},{80,64},{96,80},{112,96},{1... | collective-permute-start | bytes 196616 | tf_op jit(solution)/shard_map/ppermute | solution.py:312
  198.2 7.4 %tile_product.3 = (bf16[8,2,128,256]{3,2,1,0:T(8,128)(2,1)S(1)}, bf16[8,2,128,256]{3,2,1,0:T(8,128)(2,1)S(1)}) custom-call(s32[4,16]{1,0:T(4,128)S(1)} %bitcast.23, s32[16]{0:T(128)S(1)} %bitcast.26, s32[80]{0:T(128)S(1)} %bitcast_convert_fusion.theirs, s32[4]{0:T(128)S(1)} %pad_add_fusion.spot.spot_ref, bf16[64,128,128]{2,1,0:T(8,128)(2,1)} %bitcast.31, ...), custom_call_target="tpu_custom_call" | custom-call | tf_op jit(solution)/shard_map/tile_product/pallas_call | solution.py:152
  205.6 12.9 %collective-permute-start.35 = (bf16[8,2,128,256]{3,2,1,0:T(8,128)(2,1)S(1)}, bf16[8,2,128,256]{3,2,1,0:T(8,128)(2,1)S(1)}, u32[]{:S(2)}, u32[]{:S(2)}) collective-permute-start(bf16[8,2,128,256]{3,2,1,0:T(8,128)(2,1)S(1)} %get-tuple-element.21), channel_id=1, source_target_pairs={{0,1},{1,0},{2,3},{3,2},{4,5},{5,4},{6,7},{7,6},{8,9},{9,8},{10,11... | collective-permute-start | bytes 3145736 | tf_op jit(solution)/shard_map/ppermute | solution.py:319
  218.5 2.3 collective-permute-done.35
  221.1 21.3 %all_to_all.21.parts_ref = bf16[8,2,128,256]{3,2,1,0:T(8,128)(2,1)S(1)} all-to-all(bf16[8,2,128,256]{3,2,1,0:T(8,128)(2,1)S(1)} %add_convert_fusion), channel_id=1, replica_groups=mesh['x_lo'=2,'z'=16,'x_hi'=2,'y'=4,'core'=2] {'x_hi','y'}, dimensions={0} | all-to-all | bytes 2097152 | tf_op jit(solution)/shard_map/all_to_all | solution.py:321
  242.5 5.7 %all_to_all.22.halves_ref = bf16[2,128,256]{2,1,0:T(8,128)(2,1)S(1)} all-to-all(bf16[2,128,256]{2,1,0:T(8,128)(2,1)S(1)} %add_parts.3), channel_id=1, replica_groups=mesh['x_lo'=2,'z'=16,'x_hi'=2,'y'=4,'core'=2] {'x_lo'}, dimensions={0} | all-to-all | bytes 262144 | tf_op jit(solution)/shard_map/all_to_all | solution.py:374
  (121 shorter events, 56.3 us)
Async XLA Ops:
  10.3 74.3 %collective-permute-start = (bf16[64,128,128]{2,1,0:T(8,128)(2,1)}, bf16[64,128,128]{2,1,0:T(8,128)(2,1)S(1)}, u32[]{:S(2)}, u32[]{:S(2)}) collective-permute-start(bf16[64,128,128]{2,1,0:T(8,128)(2,1)} %bitcast.29), channel_id=1, source_target_pairs={{0,256},{256,0},{1,257},{257,1},{2,258},{258,2},{3,259},{259,3},{4... | collective-permute-start | bytes 6291464 | tf_op jit(solution)/shard_map/ppermute | solution.py:356
  12.3 15.1 %collective-permute-start.9 = (bf16[384,256]{1,0:T(8,128)(2,1)S(1)}, bf16[384,256]{1,0:T(8,128)(2,1)S(1)}, u32[]{:S(2)}, u32[]{:S(2)}) collective-permute-start(bf16[384,256]{1,0:T(8,128)(2,1)S(1)} %bitcast.32), channel_id=1, source_target_pairs={{0,16},{16,32},{32,48},{48,64},{64,80},{80,96},{96,112},{112,128},... | collective-permute-start | bytes 589832 | tf_op jit(solution)/shard_map/ppermute | solution.py:308
  16.3 13.0 %collective-permute-start.1 = (bf16[384,256]{1,0:T(8,128)(2,1)S(1)}, bf16[384,256]{1,0:T(8,128)(2,1)S(1)}, u32[]{:S(2)}, u32[]{:S(2)}) collective-permute-start(bf16[384,256]{1,0:T(8,128)(2,1)S(1)} %bitcast.33), channel_id=1, source_target_pairs={{0,240},{16,0},{32,16},{48,32},{64,48},{80,64},{96,80},{112,96},{1... | collective-permute-start | bytes 589832 | tf_op jit(solution)/shard_map/ppermute | solution.py:309
  27.4 7.6 %collective-permute-start.10 = (bf16[384,256]{1,0:T(8,128)(2,1)S(1)}, bf16[384,256]{1,0:T(8,128)(2,1)S(1)}, u32[]{:S(2)}, u32[]{:S(2)}) collective-permute-start(bf16[384,256]{1,0:T(8,128)(2,1)S(1)} %collective-permute-done.9.rest_16_), channel_id=1, source_target_pairs={{0,16},{16,32},{32,48},{48,64},{64,80},{80,96},{96,112},{112,128},... | collective-permute-start | bytes 589832 | tf_op jit(solution)/shard_map/ppermute | solution.py:308
  29.3 7.6 %collective-permute-start.2 = (bf16[384,256]{1,0:T(8,128)(2,1)S(1)}, bf16[384,256]{1,0:T(8,128)(2,1)S(1)}, u32[]{:S(2)}, u32[]{:S(2)}) collective-permute-start(bf16[384,256]{1,0:T(8,128)(2,1)S(1)} %collective-permute-done.1.rest_1_), channel_id=1, source_target_pairs={{0,240},{16,0},{32,16},{48,32},{64,48},{80,64},{96,80},{112,96},{1... | collective-permute-start | bytes 589832 | tf_op jit(solution)/shard_map/ppermute | solution.py:309
  35.0 7.6 %collective-permute-start.11 = (bf16[384,256]{1,0:T(8,128)(2,1)S(1)}, bf16[384,256]{1,0:T(8,128)(2,1)S(1)}, u32[]{:S(2)}, u32[]{:S(2)}) collective-permute-start(bf16[384,256]{1,0:T(8,128)(2,1)S(1)} %collective-permute-done.10.rest_15_), channel_id=1, source_target_pairs={{0,16},{16,32},{32,48},{48,64},{64,80},{80,96},{96,112},{112,128},... | collective-permute-start | bytes 589832 | tf_op jit(solution)/shard_map/ppermute | solution.py:308
  36.9 7.6 %collective-permute-start.3 = (bf16[384,256]{1,0:T(8,128)(2,1)S(1)}, bf16[384,256]{1,0:T(8,128)(2,1)S(1)}, u32[]{:S(2)}, u32[]{:S(2)}) collective-permute-start(bf16[384,256]{1,0:T(8,128)(2,1)S(1)} %collective-permute-done.2.rest_2_), channel_id=1, source_target_pairs={{0,240},{16,0},{32,16},{48,32},{64,48},{80,64},{96,80},{112,96},{1... | collective-permute-start | bytes 589832 | tf_op jit(solution)/shard_map/ppermute | solution.py:309
  42.6 7.6 %collective-permute-start.12 = (bf16[384,256]{1,0:T(8,128)(2,1)S(1)}, bf16[384,256]{1,0:T(8,128)(2,1)S(1)}, u32[]{:S(2)}, u32[]{:S(2)}) collective-permute-start(bf16[384,256]{1,0:T(8,128)(2,1)S(1)} %collective-permute-done.11.rest_14_), channel_id=1, source_target_pairs={{0,16},{16,32},{32,48},{48,64},{64,80},{80,96},{96,112},{112,128},... | collective-permute-start | bytes 589832 | tf_op jit(solution)/shard_map/ppermute | solution.py:308
  44.5 7.6 %collective-permute-start.4 = (bf16[384,256]{1,0:T(8,128)(2,1)S(1)}, bf16[384,256]{1,0:T(8,128)(2,1)S(1)}, u32[]{:S(2)}, u32[]{:S(2)}) collective-permute-start(bf16[384,256]{1,0:T(8,128)(2,1)S(1)} %collective-permute-done.3.rest_3_), channel_id=1, source_target_pairs={{0,240},{16,0},{32,16},{48,32},{64,48},{80,64},{96,80},{112,96},{1... | collective-permute-start | bytes 589832 | tf_op jit(solution)/shard_map/ppermute | solution.py:309
  50.2 7.6 %collective-permute-start.13 = (bf16[384,256]{1,0:T(8,128)(2,1)S(1)}, bf16[384,256]{1,0:T(8,128)(2,1)S(1)}, u32[]{:S(2)}, u32[]{:S(2)}) collective-permute-start(bf16[384,256]{1,0:T(8,128)(2,1)S(1)} %collective-permute-done.12.rest_13_), channel_id=1, source_target_pairs={{0,16},{16,32},{32,48},{48,64},{64,80},{80,96},{96,112},{112,128},... | collective-permute-start | bytes 589832 | tf_op jit(solution)/shard_map/ppermute | solution.py:308
  52.2 7.6 %collective-permute-start.5 = (bf16[384,256]{1,0:T(8,128)(2,1)S(1)}, bf16[384,256]{1,0:T(8,128)(2,1)S(1)}, u32[]{:S(2)}, u32[]{:S(2)}) collective-permute-start(bf16[384,256]{1,0:T(8,128)(2,1)S(1)} %collective-permute-done.4.rest_4_), channel_id=1, source_target_pairs={{0,240},{16,0},{32,16},{48,32},{64,48},{80,64},{96,80},{112,96},{1... | collective-permute-start | bytes 589832 | tf_op jit(solution)/shard_map/ppermute | solution.py:309
  57.8 8.5 %collective-permute-start.14 = (bf16[384,256]{1,0:T(8,128)(2,1)S(1)}, bf16[384,256]{1,0:T(8,128)(2,1)}, u32[]{:S(2)}, u32[]{:S(2)}) collective-permute-start(bf16[384,256]{1,0:T(8,128)(2,1)S(1)} %collective-permute-done.13.rest_12_), channel_id=1, source_target_pairs={{0,16},{16,32},{32,48},{48,64},{64,80},{80,96},{96,112},{112,128},... | collective-permute-start | bytes 589832 | tf_op jit(solution)/shard_map/ppermute | solution.py:308
  59.8 8.5 %collective-permute-start.6 = (bf16[384,256]{1,0:T(8,128)(2,1)S(1)}, bf16[384,256]{1,0:T(8,128)(2,1)}, u32[]{:S(2)}, u32[]{:S(2)}) collective-permute-start(bf16[384,256]{1,0:T(8,128)(2,1)S(1)} %collective-permute-done.5.rest_5_), channel_id=1, source_target_pairs={{0,240},{16,0},{32,16},{48,32},{64,48},{80,64},{96,80},{112,96},{1... | collective-permute-start | bytes 589832 | tf_op jit(solution)/shard_map/ppermute | solution.py:309
  66.3 9.4 %collective-permute-start.15 = (bf16[384,256]{1,0:T(8,128)(2,1)}, bf16[384,256]{1,0:T(8,128)(2,1)S(1)}, u32[]{:S(2)}, u32[]{:S(2)}) collective-permute-start(bf16[384,256]{1,0:T(8,128)(2,1)} %collective-permute-done.14.rest_11_), channel_id=1, source_target_pairs={{0,16},{16,32},{32,48},{48,64},{64,80},{80,96},{96,112},{112,128},... | collective-permute-start | bytes 589832 | tf_op jit(solution)/shard_map/ppermute | solution.py:308
  68.3 9.6 %collective-permute-start.7 = (bf16[384,256]{1,0:T(8,128)(2,1)}, bf16[384,256]{1,0:T(8,128)(2,1)S(1)}, u32[]{:S(2)}, u32[]{:S(2)}) collective-permute-start(bf16[384,256]{1,0:T(8,128)(2,1)} %collective-permute-done.6.rest_6_), channel_id=1, source_target_pairs={{0,240},{16,0},{32,16},{48,32},{64,48},{80,64},{96,80},{112,96},{1... | collective-permute-start | bytes 589832 | tf_op jit(solution)/shard_map/ppermute | solution.py:309
  75.7 7.3 %collective-permute-start.16 = (bf16[192,256]{1,0:T(8,128)(2,1)S(1)}, bf16[192,256]{1,0:T(8,128)(2,1)S(1)}, u32[]{:S(2)}, u32[]{:S(2)}) collective-permute-start(bf16[192,256]{1,0:T(8,128)(2,1)S(1)} %slice.25), channel_id=1, source_target_pairs={{0,16},{16,32},{32,48},{48,64},{64,80},{80,96},{96,112},{112,128},... | collective-permute-start | bytes 294920 | tf_op jit(solution)/shard_map/ppermute | solution.py:313
  93.3 14.5 %collective-permute-start.17 = (bf16[8,2,128,256]{3,2,1,0:T(8,128)(2,1)S(1)}, bf16[8,2,128,256]{3,2,1,0:T(8,128)(2,1)S(1)}, u32[]{:S(2)}, u32[]{:S(2)}) collective-permute-start(bf16[8,2,128,256]{3,2,1,0:T(8,128)(2,1)S(1)} %get-tuple-element.15), channel_id=1, source_target_pairs={{0,1},{1,0},{2,3},{3,2},{4,5},{5,4},{6,7},{7,6},{8,9},{9,8},{10,11... | collective-permute-start | bytes 3145736 | tf_op jit(solution)/shard_map/ppermute | solution.py:319
  109.1 21.0 %all-to-all-start.1 = ((bf16[8,2,128,256]{3,2,1,0:T(8,128)(2,1)}), bf16[8,2,128,256]{3,2,1,0:T(8,128)(2,1)S(1)}, u32[]{:S(2)}, u32[]{:S(2)}) async-start(bf16[8,2,128,256]{3,2,1,0:T(8,128)(2,1)} %add_convert_fusion.1), calls=%async_computation.1 | async-start | bytes 2097152 | tf_op jit(solution)/shard_map/all_to_all | solution.py:321
  136.8 7.6 %collective-permute-start.26 = (bf16[256,256]{1,0:T(8,128)(2,1)S(1)}, bf16[256,256]{1,0:T(8,128)(2,1)S(1)}, u32[]{:S(2)}, u32[]{:S(2)}) collective-permute-start(bf16[256,256]{1,0:T(8,128)(2,1)S(1)} %get-tuple-element.18.rest_0_), channel_id=1, source_target_pairs={{0,16},{16,32},{32,48},{48,64},{64,80},{80,96},{96,112},{112,128},... | collective-permute-start | bytes 393224 | tf_op jit(solution)/shard_map/ppermute | solution.py:308
  138.7 7.6 %collective-permute-start.18 = (bf16[256,256]{1,0:T(8,128)(2,1)S(1)}, bf16[256,256]{1,0:T(8,128)(2,1)S(1)}, u32[]{:S(2)}, u32[]{:S(2)}) collective-permute-start(bf16[256,256]{1,0:T(8,128)(2,1)S(1)} %get-tuple-element.18.rest_0_), channel_id=1, source_target_pairs={{0,240},{16,0},{32,16},{48,32},{64,48},{80,64},{96,80},{112,96},{1... | collective-permute-start | bytes 393224 | tf_op jit(solution)/shard_map/ppermute | solution.py:309
  144.3 6.9 %collective-permute-start.27 = (bf16[256,256]{1,0:T(8,128)(2,1)S(1)}, bf16[256,256]{1,0:T(8,128)(2,1)S(1)}, u32[]{:S(2)}, u32[]{:S(2)}) collective-permute-start(bf16[256,256]{1,0:T(8,128)(2,1)S(1)} %collective-permute-done.26.rest_16_), channel_id=1, source_target_pairs={{0,16},{16,32},{32,48},{48,64},{64,80},{80,96},{96,112},{112,128},... | collective-permute-start | bytes 393224 | tf_op jit(solution)/shard_map/ppermute | solution.py:308
  146.3 6.9 %collective-permute-start.19 = (bf16[256,256]{1,0:T(8,128)(2,1)S(1)}, bf16[256,256]{1,0:T(8,128)(2,1)S(1)}, u32[]{:S(2)}, u32[]{:S(2)}) collective-permute-start(bf16[256,256]{1,0:T(8,128)(2,1)S(1)} %collective-permute-done.18.rest_1_), channel_id=1, source_target_pairs={{0,240},{16,0},{32,16},{48,32},{64,48},{80,64},{96,80},{112,96},{1... | collective-permute-start | bytes 393224 | tf_op jit(solution)/shard_map/ppermute | solution.py:309
  151.2 6.9 %collective-permute-start.28 = (bf16[256,256]{1,0:T(8,128)(2,1)S(1)}, bf16[256,256]{1,0:T(8,128)(2,1)S(1)}, u32[]{:S(2)}, u32[]{:S(2)}) collective-permute-start(bf16[256,256]{1,0:T(8,128)(2,1)S(1)} %collective-permute-done.27.rest_15_), channel_id=1, source_target_pairs={{0,16},{16,32},{32,48},{48,64},{64,80},{80,96},{96,112},{112,128},... | collective-permute-start | bytes 393224 | tf_op jit(solution)/shard_map/ppermute | solution.py:308
  158.2 9.9 %collective-permute-start.29 = (bf16[256,256]{1,0:T(8,128)(2,1)S(1)}, bf16[256,256]{1,0:T(8,128)(2,1)S(1)}, u32[]{:S(2)}, u32[]{:S(2)}) collective-permute-start(bf16[256,256]{1,0:T(8,128)(2,1)S(1)} %collective-permute-done.28.rest_14_), channel_id=1, source_target_pairs={{0,16},{16,32},{32,48},{48,64},{64,80},{80,96},{96,112},{112,128},... | collective-permute-start | bytes 393224 | tf_op jit(solution)/shard_map/ppermute | solution.py:308
  160.1 9.9 %collective-permute-start.21 = (bf16[256,256]{1,0:T(8,128)(2,1)S(1)}, bf16[256,256]{1,0:T(8,128)(2,1)S(1)}, u32[]{:S(2)}, u32[]{:S(2)}) collective-permute-start(bf16[256,256]{1,0:T(8,128)(2,1)S(1)} %collective-permute-done.20.rest_3_), channel_id=1, source_target_pairs={{0,240},{16,0},{32,16},{48,32},{64,48},{80,64},{96,80},{112,96},{1... | collective-permute-start | bytes 393224 | tf_op jit(solution)/shard_map/ppermute | solution.py:309
  164.7 32.3 %collective-permute-start.34 = (bf16[2048,128]{1,0:T(8,128)(2,1)S(1)}, bf16[2048,128]{1,0:T(8,128)(2,1)S(1)}, u32[]{:S(2)}, u32[]{:S(2)}) collective-permute-start(bf16[2048,128]{1,0:T(8,128)(2,1)S(1)} %history_term.1.rest_17_), channel_id=1, source_target_pairs={{0,256},{256,0},{1,257},{257,1},{2,258},{258,2},{3,259},{259,3},{4... | collective-permute-start | bytes 1572872 | tf_op jit(solution)/shard_map/ppermute | solution.py:371
  168.1 6.9 %collective-permute-start.30 = (bf16[256,256]{1,0:T(8,128)(2,1)S(1)}, bf16[256,256]{1,0:T(8,128)(2,1)S(1)}, u32[]{:S(2)}, u32[]{:S(2)}) collective-permute-start(bf16[256,256]{1,0:T(8,128)(2,1)S(1)} %collective-permute-done.29.rest_13_), channel_id=1, source_target_pairs={{0,16},{16,32},{32,48},{48,64},{64,80},{80,96},{96,112},{112,128},... | collective-permute-start | bytes 393224 | tf_op jit(solution)/shard_map/ppermute | solution.py:308
  175.0 8.2 %collective-permute-start.31 = (bf16[256,256]{1,0:T(8,128)(2,1)S(1)}, bf16[256,256]{1,0:T(8,128)(2,1)S(1)}, u32[]{:S(2)}, u32[]{:S(2)}) collective-permute-start(bf16[256,256]{1,0:T(8,128)(2,1)S(1)} %collective-permute-done.30.rest_12_), channel_id=1, source_target_pairs={{0,16},{16,32},{32,48},{48,64},{64,80},{80,96},{96,112},{112,128},... | collective-permute-start | bytes 393224 | tf_op jit(solution)/shard_map/ppermute | solution.py:308
  176.9 8.1 %collective-permute-start.23 = (bf16[256,256]{1,0:T(8,128)(2,1)S(1)}, bf16[256,256]{1,0:T(8,128)(2,1)S(1)}, u32[]{:S(2)}, u32[]{:S(2)}) collective-permute-start(bf16[256,256]{1,0:T(8,128)(2,1)S(1)} %collective-permute-done.22.rest_5_), channel_id=1, source_target_pairs={{0,240},{16,0},{32,16},{48,32},{64,48},{80,64},{96,80},{112,96},{1... | collective-permute-start | bytes 393224 | tf_op jit(solution)/shard_map/ppermute | solution.py:309
  183.2 7.2 %collective-permute-start.32 = (bf16[256,256]{1,0:T(8,128)(2,1)S(1)}, bf16[256,256]{1,0:T(8,128)(2,1)S(1)}, u32[]{:S(2)}, u32[]{:S(2)}) collective-permute-start(bf16[256,256]{1,0:T(8,128)(2,1)S(1)} %collective-permute-done.31.rest_11_), channel_id=1, source_target_pairs={{0,16},{16,32},{32,48},{48,64},{64,80},{80,96},{96,112},{112,128},... | collective-permute-start | bytes 393224 | tf_op jit(solution)/shard_map/ppermute | solution.py:308
  185.1 7.2 %collective-permute-start.24 = (bf16[256,256]{1,0:T(8,128)(2,1)S(1)}, bf16[256,256]{1,0:T(8,128)(2,1)S(1)}, u32[]{:S(2)}, u32[]{:S(2)}) collective-permute-start(bf16[256,256]{1,0:T(8,128)(2,1)S(1)} %collective-permute-done.23.rest_6_), channel_id=1, source_target_pairs={{0,240},{16,0},{32,16},{48,32},{64,48},{80,64},{96,80},{112,96},{1... | collective-permute-start | bytes 393224 | tf_op jit(solution)/shard_map/ppermute | solution.py:309
  205.6 15.2 %collective-permute-start.35 = (bf16[8,2,128,256]{3,2,1,0:T(8,128)(2,1)S(1)}, bf16[8,2,128,256]{3,2,1,0:T(8,128)(2,1)S(1)}, u32[]{:S(2)}, u32[]{:S(2)}) collective-permute-start(bf16[8,2,128,256]{3,2,1,0:T(8,128)(2,1)S(1)} %get-tuple-element.21), channel_id=1, source_target_pairs={{0,1},{1,0},{2,3},{3,2},{4,5},{5,4},{6,7},{7,6},{8,9},{9,8},{10,11... | collective-permute-start | bytes 3145736 | tf_op jit(solution)/shard_map/ppermute | solution.py:319
  (33 other events, 662.2 us)

commit v4 on v3

--- a/solution.py
+++ b/solution.py
@@ -17,21 +17,23 @@
 LIST = 40
 WIDE = 128
 META = 16
-CARRY = BLOCK + 2 * FEAT
-PAY = CARRY + META
+PAY = BLOCK + META
+FAR = 6
 DOM = ("x_lo", "z")
 GRID = ("x_hi", "y", "core")
 SIDE = ("x_hi", "y")
 SWAP = [(0, 1), (1, 0)]
-UP = [(z, (z + 1) % 16) for z in range(16)]
-DOWN = [(z, (z + 15) % 16) for z in range(16)]
+
+
+def from_z(value, offset):
+    return lax.ppermute(value, "z", [((z + offset) % 16, z) for z in range(16)])
 
 
 def params(mib):
     return pltpu.CompilerParams(vmem_limit_bytes=mib << 20)
 
 
-def payload_body(cols, counts, feats, hist, out, feats_in, hist_in, sems):
+def payload_body(cols, counts, feats, hist, out, own, feats_in, hist_in, sems):
     moves = [
         pltpu.make_async_copy(feats, feats_in, sems.at[0]),
         pltpu.make_async_copy(hist, hist_in, sems.at[1]),
@@ -49,21 +51,25 @@
         move.wait()
     for j in range(2):
         out[j, :BLOCK] = feats_in[:, j * HALF : (j + 1) * HALF]
-        for k in range(2):
-            start = BLOCK + k * FEAT
-            out[j, start : start + FEAT] = hist_in[:, k * HALF : (k + 1) * HALF]
-        out[j, CARRY:] = meta
+        out[j, BLOCK:] = meta
+        own[j * FEAT : (j + 1) * FEAT] = hist_in[:, j * HALF : (j + 1) * HALF]
 
 
 def make_payload(cols, counts, feats, hist):
     return pl.pallas_call(
         payload_body,
-        out_shape=jax.ShapeDtypeStruct((2, PAY, HALF), jnp.bfloat16),
+        out_shape=(
+            jax.ShapeDtypeStruct((2, PAY, HALF), jnp.bfloat16),
+            jax.ShapeDtypeStruct((2 * FEAT, HALF), jnp.bfloat16),
+        ),
         grid_spec=pltpu.PrefetchScalarGridSpec(
             num_scalar_prefetch=2,
             grid=(1,),
             in_specs=[pl.BlockSpec(memory_space=pltpu.HBM)] * 2,
-            out_specs=pl.BlockSpec((2, PAY, HALF), lambda i, *_: (0, 0, 0)),
+            out_specs=(
+                pl.BlockSpec((2, PAY, HALF), lambda i, *_: (0, 0, 0)),
+                pl.BlockSpec((2 * FEAT, HALF), lambda i, *_: (0, 0)),
+            ),
             scratch_shapes=[
                 pltpu.VMEM(feats.shape, jnp.bfloat16),
                 pltpu.VMEM(hist.shape, jnp.bfloat16),
@@ -75,28 +81,30 @@
     )(cols, counts, feats, hist)
 
 
-def tile_body(n_chunks, stride, with_extra, cols, counts, theirs, spot, own, partner, *rest):
+def tile_body(n_chunks, stride, second, cols, counts, theirs, spot, own, partner, *rest):
     chunks = rest[:n_chunks]
-    extras = rest[n_chunks : n_chunks + 2] if with_extra else ()
-    keep, send, panel, adj, sems = rest[-5:]
+    if second:
+        extras = rest[n_chunks : n_chunks + 2]
+        keep, send, panel, adj, sems, added = rest[-6:]
+    else:
+        keep, send, store, panel, adj, sems = rest[-6:]
     core = spot[1]
     moves = []
+
+    def move(source, target):
+        moves.append(pltpu.make_async_copy(source, target, sems.at[len(moves)]))
+        moves[-1].start()
+
     start = 0
     for source in chunks:
-        size = source.shape[0]
-        target = panel.at[pl.ds(start, size)]
-        moves.append(pltpu.make_async_copy(source, target, sems.at[len(moves)]))
-        start += size
+        move(source, panel.at[pl.ds(start, source.shape[0])])
+        start += source.shape[0]
     for k, source in enumerate((own, partner)):
         for c in range(4):
-            target = adj.at[pl.ds(64 * k + 16 * c, 16)]
-            moves.append(
-                pltpu.make_async_copy(
-                    source.at[pl.ds(16 * c, 16)], target, sems.at[len(moves)]
-                )
-            )
-    for move in moves:
-        move.start()
+            move(source.at[pl.ds(16 * c, 16)], adj.at[pl.ds(64 * k + 16 * c, 16)])
+    if second:
+        for k in range(2):
+            move(extras[k], added.at[k])
 
     def product(k, row):
         base = (ROWS * k + row) * SLOTS
@@ -107,8 +115,8 @@
             block = adj[base + slot]
             left.append(jnp.where(slot < count, block, jnp.zeros_like(block)))
             col = cols[slot, row] if k == 0 else theirs[row * SLOTS + slot]
-            place = (((col & 15) - spot[3]) & 15) * 2 + (col >> 4)
-            right.append(panel[pl.ds(pl.multiple_of(place * stride, 2 * FEAT), BLOCK), :])
+            place = (((col & 15) - spot[3]) & 15) * stride + (col >> 4) * BLOCK
+            right.append(panel[pl.ds(pl.multiple_of(place, 2 * FEAT), BLOCK), :])
         return jnp.dot(
             jnp.concatenate(left, axis=1),
             jnp.concatenate(right, axis=0),
@@ -116,8 +124,7 @@
         )
 
     def with_history(k, row, value):
-        start = pl.multiple_of(row * BLOCK, BLOCK)
-        piece = extras[k][pl.ds(start, BLOCK), :].astype(jnp.float32)
+        piece = added[k, row * BLOCK : (row + 1) * BLOCK, :].astype(jnp.float32)
         zero = jnp.zeros_like(piece)
         wide = [jnp.where(spot[2] == group, piece, zero) for group in range(2)]
         return value + jnp.concatenate(wide, axis=1)
@@ -125,7 +132,7 @@
     def two_rows(k, j):
         part = spot[0] if k == 0 else 1 - spot[0]
         pair = [product(k, 2 * j + side) for side in range(2)]
-        if with_extra:
+        if second:
             pair = [with_history(k, 2 * j + side, pair[side]) for side in range(2)]
         even, odd = [value.astype(jnp.bfloat16) for value in pair]
         keep[j, part] = jnp.where(core == 0, even, odd)
@@ -133,56 +140,60 @@
 
     for n in range(n_chunks):
         moves[n].wait()
+    if not second:
+        for d in range(16):
+            source = panel.at[pl.ds(d * stride + 2 * BLOCK, 2 * FEAT)]
+            move(source, store.at[pl.ds(d * 2 * FEAT, 2 * FEAT)])
     for k in range(2):
         for c in range(4):
             moves[n_chunks + 4 * k + c].wait()
+            if second and c == 0:
+                moves[n_chunks + 8 + k].wait()
             two_rows(k, 2 * c)
             two_rows(k, 2 * c + 1)
+    if not second:
+        for d in range(16):
+            moves[n_chunks + 8 + d].wait()
 
 
 def tile_product(cols, counts, theirs, spot, own, partner, chunks, extras):
-    operands = [own, partner, *chunks]
-    specs = [pl.BlockSpec(memory_space=pltpu.HBM)] * len(operands)
-    stride = chunks[0].shape[0] // 2
-    for extra in extras:
-        operands.append(extra)
-        specs.append(pl.BlockSpec(extra.shape, lambda i, *_: (0, 0)))
+    operands = [own, partner, *chunks, *extras]
+    stride = chunks[0].shape[0]
+    second = bool(extras)
     half = jax.ShapeDtypeStruct((ROWS // 2, 2, BLOCK, HALF), jnp.bfloat16)
-    out_spec = pl.BlockSpec(half.shape, lambda i, *_: (0, 0, 0, 0))
-    return pl.pallas_call(
-        functools.partial(tile_body, len(chunks), stride, bool(extras)),
-        out_shape=(half, half),
+    outs = [half, half]
+    out_specs = [pl.BlockSpec(half.shape, lambda i, *_: (0, 0, 0, 0))] * 2
+    scratch = [
+        pltpu.VMEM((16 * stride, HALF), jnp.bfloat16),
+        pltpu.VMEM((2 * ROWS * SLOTS, BLOCK, BLOCK), jnp.bfloat16),
+        pltpu.SemaphoreType.DMA((len(chunks) + 8 + (2 if second else 16),)),
+    ]
+    if second:
+        scratch.append(pltpu.VMEM((2, ROWS * BLOCK, WIDE), jnp.bfloat16))
+    else:
+        outs.append(jax.ShapeDtypeStruct((32 * FEAT, HALF), jnp.bfloat16))
+        out_specs.append(pl.BlockSpec(memory_space=pltpu.HBM))
+    return pl.pallas_call(
+        functools.partial(tile_body, len(chunks), stride, second),
+        out_shape=tuple(outs),
         grid_spec=pltpu.PrefetchScalarGridSpec(
             num_scalar_prefetch=4,
             grid=(1,),
-            in_specs=specs,
-            out_specs=(out_spec, out_spec),
-            scratch_shapes=[
-                pltpu.VMEM((32 * stride, HALF), jnp.bfloat16),
-                pltpu.VMEM((2 * ROWS * SLOTS, BLOCK, BLOCK), jnp.bfloat16),
-                pltpu.SemaphoreType.DMA((len(chunks) + 8,)),
-            ],
+            in_specs=[pl.BlockSpec(memory_space=pltpu.HBM)] * len(operands),
+            out_specs=tuple(out_specs),
+            scratch_shapes=scratch,
         ),
         compiler_params=params(20),
         name="tile_product",
     )(cols, counts, theirs, spot, *operands)
 
 
-def history_body(n_chunks, listed, order, rows, spot, adj, *rest):
-    chunks = rest[:n_chunks]
-    out, weights, store, total, sems = rest[n_chunks:]
-    moves = [pltpu.make_async_copy(adj, weights, sems.at[0])]
-    start = 0
-    for source in chunks:
-        for k in range(source.shape[0] // CARRY):
-            moves.append(
-                pltpu.make_async_copy(
-                    source.at[pl.ds(k * CARRY + BLOCK, 2 * FEAT)],
-                    store.at[pl.ds(start, 2 * FEAT)],
-                    sems.at[len(moves)],
-                )
-            )
-            start += 2 * FEAT
+def history_body(listed, order, rows, spot, adj, same, other, out, weights, store, total, sems):
+    moves = [
+        pltpu.make_async_copy(adj, weights, sems.at[0]),
+        pltpu.make_async_copy(same, store.at[0], sems.at[1]),
+        pltpu.make_async_copy(other, store.at[1], sems.at[2]),
+    ]
     for move in moves:
         move.start()
     total[...] = jnp.zeros_like(total)
@@ -193,12 +204,12 @@
         block = listed[spot[0], order[slot]]
         owner = block >> 2
         piece = block & 3
-        place = (((owner & 15) - spot[2]) & 15) * 2 + (owner >> 4)
-        source = pl.multiple_of(place * (2 * FEAT) + (piece >> 1) * FEAT, FEAT)
+        place = (((owner & 15) - spot[2]) & 15) * (2 * FEAT) + (piece >> 1) * FEAT
+        source = pl.multiple_of(place, FEAT)
         lane = pl.multiple_of((piece & 1) * BLOCK, BLOCK)
         return lax.dot_general(
             weights[slot],
-            store[pl.ds(source, FEAT), pl.ds(lane, BLOCK)],
+            store[(owner >> 4) ^ spot[3], pl.ds(source, FEAT), pl.ds(lane, BLOCK)],
             (((1,), (1,)), ((), ())),
             preferred_element_type=jnp.float32,
         )
@@ -214,25 +225,25 @@
     out[...] = pltpu.roll(total[...], spot[1] * FEAT, 1).astype(jnp.bfloat16)
 
 
-def history_term(listed, order, rows, spot, adj, chunks):
-    return pl.pallas_call(
-        functools.partial(history_body, len(chunks)),
+def history_term(listed, order, rows, spot, adj, same, other):
+    return pl.pallas_call(
+        history_body,
         out_shape=jax.ShapeDtypeStruct((ROWS * BLOCK, WIDE), jnp.bfloat16),
         grid_spec=pltpu.PrefetchScalarGridSpec(
             num_scalar_prefetch=4,
             grid=(1,),
-            in_specs=[pl.BlockSpec(memory_space=pltpu.HBM)] * (1 + len(chunks)),
+            in_specs=[pl.BlockSpec(memory_space=pltpu.HBM)] * 3,
             out_specs=pl.BlockSpec((ROWS * BLOCK, WIDE), lambda i, *_: (0, 0)),
             scratch_shapes=[
                 pltpu.VMEM(adj.shape, jnp.bfloat16),
-                pltpu.VMEM((64 * FEAT, HALF), jnp.bfloat16),
+                pltpu.VMEM((2, *same.shape), jnp.bfloat16),
                 pltpu.VMEM((ROWS * BLOCK, WIDE), jnp.float32),
-                pltpu.SemaphoreType.DMA((33,)),
+                pltpu.SemaphoreType.DMA((3,)),
             ],
         ),
         compiler_params=params(16),
         name="history_term",
-    )(listed, order, rows, spot, adj, *chunks)
+    )(listed, order, rows, spot, adj, same, other)
 
 
 def add_parts(parts):
@@ -302,17 +313,23 @@
 
 
 def gather_ring(chunk):
-    up = [chunk]
-    down = [chunk]
-    for _ in range(7):
-        up.append(lax.ppermute(up[-1], "z", UP))
-        down.append(lax.ppermute(down[-1], "z", DOWN))
+    ahead = {0: chunk}
+    behind = {0: chunk}
+    far_ahead = from_z(chunk, FAR)
+    far_behind = from_z(chunk, -FAR)
+    for d in range(1, FAR):
+        ahead[d] = from_z(ahead[d - 1], 1)
+        behind[d] = from_z(behind[d - 1], -1)
+        if d == 3:
+            far_ahead, ahead[3] = lax.optimization_barrier((far_ahead, ahead[3]))
+            far_behind, behind[3] = lax.optimization_barrier((far_behind, behind[3]))
+            ahead[FAR] = far_ahead
+            behind[FAR] = far_behind
+    ahead[7] = from_z(ahead[6], 1)
+    behind[7] = from_z(behind[6], -1)
     half = chunk.shape[0] // 2
-    far = [
-        lax.ppermute(down[7][:half], "z", DOWN),
-        lax.ppermute(up[7][half:], "z", UP),
-    ]
-    return down + far + up[:0:-1]
+    across = [from_z(ahead[7][:half], 1), from_z(behind[7][half:], -1)]
+    return [ahead[d] for d in range(8)] + across + [behind[d] for d in range(7, 0, -1)]
 
 
 def reduce_rows(keep, send):
@@ -343,9 +360,10 @@
     group = jnp.where(x_lo == x_hi, (grid_index // 4) % 2, -1)
     spot = jnp.stack([x_lo, lax.axis_index("core"), group, lax.axis_index("z")])
     spot = spot.astype(jnp.int32)
-    hist_spot = jnp.stack([lax.axis_index(DOM), grid_index % 4, lax.axis_index("z")]).astype(jnp.int32)
-
-    payload = make_payload(
+    hist_spot = jnp.stack([lax.axis_index(DOM), grid_index % 4, lax.axis_index("z"), x_lo])
+    hist_spot = hist_spot.astype(jnp.int32)
+
+    payload, own_store = make_payload(
         cols,
         counts,
         pltpu.with_memory_space_constraint(node_feats, pltpu.HBM),
@@ -354,20 +372,23 @@
     received = lax.all_to_all(payload, "x_lo", 0, 0, tiled=True)
     adj_held, received = lax.optimization_barrier((adj, received))
     partner = lax.ppermute(adj_held, "x_lo", SWAP)
-    chunks = gather_ring(received[:, :CARRY].reshape(2 * CARRY, HALF))
+    chunk = jnp.concatenate([received[0, :BLOCK], received[1, :BLOCK], own_store], axis=0)
+    chunks = gather_ring(chunk)
     chunks = [pltpu.with_memory_space_constraint(chunk, pltpu.HBM) for chunk in chunks]
     partner = pltpu.with_memory_space_constraint(partner, pltpu.HBM)
     adj = pltpu.with_memory_space_constraint(adj, pltpu.HBM)
-    theirs = lax.dynamic_index_in_dim(received[:, CARRY, :80], 1 - x_lo, 0, False)
-    theirs = theirs.astype(jnp.int32)
-    mine = history_term(hist_list, hist_col[0], hist_row[0], hist_spot, hist_adj[0], chunks)
-
-    tables = (cols, counts, theirs, spot)
-    agg = reduce_rows(*tile_product(*tables, adj, partner, chunks, ()))
+    theirs = lax.dynamic_index_in_dim(received[:, BLOCK, :80], 1 - x_lo, 0, False)
+    tables = (cols, counts, theirs.astype(jnp.int32), spot)
+
+    keep, send, store = tile_product(*tables, adj, partner, chunks, ())
+    agg = reduce_rows(keep, send)
+    other_store = lax.ppermute(store, "x_lo", SWAP)
+    mine = history_term(
+        hist_list, hist_col[0], hist_row[0], hist_spot, hist_adj[0], store, other_store
+    )
     halves = lax.all_gather(agg, "x_lo", axis=0, tiled=False)
     hidden, chunk = first_dense(halves, w_first, spot)
 
-    chunk, mine = lax.optimization_barrier((chunk, mine))
     extras = (mine, lax.ppermute(mine, "x_lo", SWAP))
     chunks = gather_ring(chunk)
     agg = reduce_rows(*tile_product(*tables, adj, partner, chunks, extras))

time: 251 us -> 278 us (1.11)
  waiting for transfers between devices: 32.2 us -> 52.5 us
  blocking collectives: 38.8 us -> 46.4 us
  starting transfers between devices: 149 us -> 146 us
    ppermute x32 -> x33, waiting for transfers between devices: 17.4 us -> 36.1 us  [the longest x32 36.1 us: from_z(): return lax.ppermute(value, 'z', [((z + offset) % 16, z) for z in range(16)])]
    ppermute x2, starting transfers between devices: 25.1 us -> 10.2 us  [reduce_rows(): other = lax.ppermute(send, 'core', SWAP)]
    ppermute x32 -> x33, starting transfers between devices: 112 us -> 125 us  [the longest x32 122 us: from_z(): return lax.ppermute(value, 'z', [((z + offset) % 16, z) for z in range(16)])]
    all_gather x1, blocking collectives: 5.02 us -> 12 us  [local(): halves = lax.all_gather(agg, 'x_lo', axis=0, tiled=False)]
  transfers between devices with their start and end apart: 37 -> 38, of which waited for: 19 -> 12; matrix products, arithmetic and copies ran while one was open for 0% -> 0% of each run, Pallas kernels for 2% -> 2%
where the time goes in v4:
time: 278 us; the launch traced here: 274 us
  starting transfers between devices  146 us (53%)
  waiting for transfers between devices  52.5 us (19%)
  blocking collectives  46.4 us (17%)
  Pallas kernels  21.4 us (8%)
  local copies, waits for them, and re-layouts  4.68 us (2%)
    ppermute x32, starting transfers between devices, from_z(): return lax.ppermute(value, 'z', [((z + offset) % 16, z) for z in range(16)])  122 us
    ppermute x32, waiting for transfers between devices, from_z(): return lax.ppermute(value, 'z', [((z + offset) % 16, z) for z in range(16)])  36.1 us
    all_to_all x1, blocking collectives, reduce_rows(): return add_parts(lax.all_to_all(both, SIDE, 0, 0, tiled=True))  22.2 us
    pallas_call x2, Pallas kernels, tile_product(): pl.pallas_call(functools.partial(tile_body, len(chunks), stride, second),...  13.4 us
    all_gather x1, blocking collectives, local(): halves = lax.all_gather(agg, 'x_lo', axis=0, tiled=False)  12 us
    all_to_all x1, waiting for transfers between devices, reduce_rows(): return add_parts(lax.all_to_all(both, SIDE, 0, 0, tiled=True))  11.8 us
    ppermute x2, starting transfers between devices, reduce_rows(): other = lax.ppermute(send, 'core', SWAP)  10.2 us
    all_to_all x1, starting transfers between devices, reduce_rows(): return add_parts(lax.all_to_all(both, SIDE, 0, 0, tiled=True))  6.84 us
  transfers between devices with their start and end apart: 38, of which 12 were waited for; matrix products, arithmetic and copies ran while one was open for 0% of the time, Pallas kernels for 2%

profile of v4, /device:TPU:1, one launch (start us, length us, event | category | flops | bytes accessed | tf_op | source)
XLA Modules:
  0.0 274.4 jit_solution(9874151429750108942)
XLA Ops:
  3.5 6.5 %all_to_all.20 = bf16[2,144,256]{2,1,0:T(8,128)(2,1)S(1)} all-to-all(bf16[2,144,256]{2,1,0:T(8,128)(2,1)S(1)} %get-tuple-element.21), channel_id=1, replica_groups=mesh['x_lo'=2,'z'=16,'x_hi'=2,'y'=4,'core'=2] {'x_lo'}, dimensions={0} | all-to-all | bytes 294912 | tf_op jit(solution)/shard_map/all_to_all | solution.py:372
  15.6 9.5 %collective-permute-start.1 = (bf16[320,256]{1,0:T(8,128)(2,1)S(1)}, bf16[320,256]{1,0:T(8,128)(2,1)S(1)}, u32[]{:S(2)}, u32[]{:S(2)}) collective-permute-start(bf16[320,256]{1,0:T(8,128)(2,1)S(1)} %pad_maximum_fusion.rest_0_), channel_id=1, source_target_pairs={{16,0},{32,16},{48,32},{64,48},{80,64},{96,80},{112,96},{128,112},... | collective-permute-start | bytes 491528 | tf_op jit(solution)/shard_map/ppermute | solution.py:29
  27.8 4.6 %collective-permute-start.2 = (bf16[320,256]{1,0:T(8,128)(2,1)S(1)}, bf16[320,256]{1,0:T(8,128)(2,1)S(1)}, u32[]{:S(2)}, u32[]{:S(2)}) collective-permute-start(bf16[320,256]{1,0:T(8,128)(2,1)S(1)} %collective-permute-done.1.rest_1_), channel_id=1, source_target_pairs={{16,0},{32,16},{48,32},{64,48},{80,64},{96,80},{112,96},{128,112},... | collective-permute-start | bytes 491528 | tf_op jit(solution)/shard_map/ppermute | solution.py:29
  32.4 4.4 %collective-permute-start.9 = (bf16[320,256]{1,0:T(8,128)(2,1)S(1)}, bf16[320,256]{1,0:T(8,128)(2,1)S(1)}, u32[]{:S(2)}, u32[]{:S(2)}) collective-permute-start(bf16[320,256]{1,0:T(8,128)(2,1)S(1)} %pad_maximum_fusion.rest_0_), channel_id=1, source_target_pairs={{160,0},{176,16},{192,32},{208,48},{224,64},{240,80},{0,96},{16,11... | collective-permute-start | bytes 491528 | tf_op jit(solution)/shard_map/ppermute | solution.py:29
  36.8 4.3 %collective-permute-start.12 = (bf16[320,256]{1,0:T(8,128)(2,1)S(1)}, bf16[320,256]{1,0:T(8,128)(2,1)S(1)}, u32[]{:S(2)}, u32[]{:S(2)}) collective-permute-start(bf16[320,256]{1,0:T(8,128)(2,1)S(1)} %collective-permute-done.11.rest_15_), channel_id=1, source_target_pairs={{240,0},{0,16},{16,32},{32,48},{48,64},{64,80},{80,96},{96,112},{1... | collective-permute-start | bytes 491528 | tf_op jit(solution)/shard_map/ppermute | solution.py:29
  41.1 5.4 %collective-permute-start.3 = (bf16[320,256]{1,0:T(8,128)(2,1)S(1)}, bf16[320,256]{1,0:T(8,128)(2,1)S(1)}, u32[]{:S(2)}, u32[]{:S(2)}) collective-permute-start(bf16[320,256]{1,0:T(8,128)(2,1)S(1)} %pad_maximum_fusion.rest_0_), channel_id=1, source_target_pairs={{96,0},{112,16},{128,32},{144,48},{160,64},{176,80},{192,96},{208,... | collective-permute-start | bytes 491528 | tf_op jit(solution)/shard_map/ppermute | solution.py:29
  49.9 6.6 %collective-permute-done.9.rest_11_ = bf16[320,256]{1,0:T(8,128)(2,1)S(1)} collective-permute-done((bf16[320,256]{1,0:T(8,128)(2,1)S(1)}, bf16[320,256]{1,0:T(8,128)(2,1)S(1)}, u32[]{:S(2)}, u32[]{:S(2)}) %collective-permute-start.9) | collective-permute-done | bytes 163872 | tf_op jit(solution)/shard_map/ppermute | solution.py:29
  56.5 5.3 %collective-permute-done.12.rest_14_ = bf16[320,256]{1,0:T(8,128)(2,1)S(1)} collective-permute-done((bf16[320,256]{1,0:T(8,128)(2,1)S(1)}, bf16[320,256]{1,0:T(8,128)(2,1)S(1)}, u32[]{:S(2)}, u32[]{:S(2)}) %collective-permute-start.12) | collective-permute-done | bytes 163872 | tf_op jit(solution)/shard_map/ppermute | solution.py:29
  65.4 6.0 %collective-permute-done.4.rest_3_ = bf16[320,256]{1,0:T(8,128)(2,1)S(1)} collective-permute-done((bf16[320,256]{1,0:T(8,128)(2,1)S(1)}, bf16[320,256]{1,0:T(8,128)(2,1)S(1)}, u32[]{:S(2)}, u32[]{:S(2)}) %collective-permute-start.4) | collective-permute-done | bytes 163872 | tf_op jit(solution)/shard_map/ppermute | solution.py:29
  77.1 4.6 %collective-permute-start.7 = (bf16[320,256]{1,0:T(8,128)(2,1)S(1)}, bf16[320,256]{1,0:T(8,128)(2,1)S(1)}, u32[]{:S(2)}, u32[]{:S(2)}) collective-permute-start(bf16[320,256]{1,0:T(8,128)(2,1)S(1)} %collective-permute-done.3.rest_6_), channel_id=1, source_target_pairs={{16,0},{32,16},{48,32},{64,48},{80,64},{96,80},{112,96},{128,112},... | collective-permute-start | bytes 491528 | tf_op jit(solution)/shard_map/ppermute | solution.py:29
  83.7 4.6 %collective-permute-start.6 = (bf16[320,256]{1,0:T(8,128)(2,1)}, bf16[320,256]{1,0:T(8,128)(2,1)}, u32[]{:S(2)}, u32[]{:S(2)}) collective-permute-start(bf16[320,256]{1,0:T(8,128)(2,1)} %collective-permute-done.5.rest_4_), channel_id=1, source_target_pairs={{16,0},{32,16},{48,32},{64,48},{80,64},{96,80},{112,96},{128,112},... | collective-permute-start | bytes 491528 | tf_op jit(solution)/shard_map/ppermute | solution.py:29
  90.4 4.6 %collective-permute-start.8 = (bf16[160,256]{1,0:T(8,128)(2,1)S(1)}, bf16[160,256]{1,0:T(8,128)(2,1)S(1)}, u32[]{:S(2)}, u32[]{:S(2)}) collective-permute-start(bf16[160,256]{1,0:T(8,128)(2,1)S(1)} %slice.28), channel_id=1, source_target_pairs={{16,0},{32,16},{48,32},{64,48},{80,64},{96,80},{112,96},{128,112},... | collective-permute-start | bytes 245768 | tf_op jit(solution)/shard_map/ppermute | solution.py:29
  99.8 5.9 %tile_product.2 = (bf16[8,2,128,256]{3,2,1,0:T(8,128)(2,1)S(1)}, bf16[8,2,128,256]{3,2,1,0:T(8,128)(2,1)S(1)}, bf16[1024,256]{1,0:T(8,128)(2,1)S(1)}) custom-call(s32[4,16]{1,0:T(4,128)S(1)} %bitcast.25, s32[16]{0:T(128)S(1)} %bitcast.28, s32[80]{0:T(128)S(1)} %bitcast_convert_fusion.theirs, s32[4]{0:T(128)S(1)} %pad_add_fusion.spot.spot_ref, ...), custom_call_target="tpu_custom_call" | custom-call | tf_op jit(solution)/shard_map/tile_product/pallas_call | solution.py:176
  105.7 5.3 %collective-permute-start.17 = (bf16[8,2,128,256]{3,2,1,0:T(8,128)(2,1)S(1)}, bf16[8,2,128,256]{3,2,1,0:T(8,128)(2,1)S(1)}, u32[]{:S(2)}, u32[]{:S(2)}) collective-permute-start(bf16[8,2,128,256]{3,2,1,0:T(8,128)(2,1)S(1)} %get-tuple-element.30), channel_id=1, source_target_pairs={{0,1},{1,0},{2,3},{3,2},{4,5},{5,4},{6,7},{7,6},{8,9},{9,8},{10,11... | collective-permute-start | bytes 3145736 | tf_op jit(solution)/shard_map/ppermute | solution.py:336
  114.6 6.8 %all-to-all-start.1 = ((bf16[8,2,128,256]{3,2,1,0:T(8,128)(2,1)}), bf16[8,2,128,256]{3,2,1,0:T(8,128)(2,1)S(1)}, u32[]{:S(2)}, u32[]{:S(2)}) async-start(bf16[8,2,128,256]{3,2,1,0:T(8,128)(2,1)} %add_convert_fusion.1), calls=%async_computation.1 | async-start | bytes 2097152 | tf_op jit(solution)/shard_map/all_to_all | solution.py:338
  124.1 11.8 %all-to-all-done.1.parts_ref = bf16[8,2,128,256]{3,2,1,0:T(8,128)(2,1)S(1)} async-done(((bf16[8,2,128,256]{3,2,1,0:T(8,128)(2,1)}), bf16[8,2,128,256]{3,2,1,0:T(8,128)(2,1)S(1)}, u32[]{:S(2)}, u32[]{:S(2)}) %all-to-all-start.1) | async-done | bytes 1048608 | tf_op jit(solution)/shard_map/all_to_all | solution.py:338
  136.1 12.0 %all-gather = bf16[4,128,256]{2,1,0:T(8,128)(2,1)S(1)} all-gather(bf16[2,128,256]{2,1,0:T(8,128)(2,1)S(1)} %add_parts.2), channel_id=2, replica_groups=mesh['x_lo'=2,'z'=16,'x_hi'=2,'y'=4,'core'=2] {'x_lo'}, dimensions={0}, use_global_device_ids=true | all-gather | bytes 393216 | tf_op jit(solution)/shard_map/all_gather | solution.py:389
  151.6 5.2 %collective-permute-start.18 = (bf16[256,256]{1,0:T(8,128)(2,1)S(1)}, bf16[256,256]{1,0:T(8,128)(2,1)S(1)}, u32[]{:S(2)}, u32[]{:S(2)}) collective-permute-start(bf16[256,256]{1,0:T(8,128)(2,1)S(1)} %get-tuple-element.32.rest_0_), channel_id=1, source_target_pairs={{16,0},{32,16},{48,32},{64,48},{80,64},{96,80},{112,96},{128,112},... | collective-permute-start | bytes 393224 | tf_op jit(solution)/shard_map/ppermute | solution.py:29
  159.1 4.6 %collective-permute-start.19 = (bf16[256,256]{1,0:T(8,128)(2,1)S(1)}, bf16[256,256]{1,0:T(8,128)(2,1)S(1)}, u32[]{:S(2)}, u32[]{:S(2)}) collective-permute-start(bf16[256,256]{1,0:T(8,128)(2,1)S(1)} %collective-permute-done.18.rest_1_), channel_id=1, source_target_pairs={{16,0},{32,16},{48,32},{64,48},{80,64},{96,80},{112,96},{128,112},... | collective-permute-start | bytes 393224 | tf_op jit(solution)/shard_map/ppermute | solution.py:29
  163.8 3.8 %history_term.1.rest_17_ = bf16[2048,128]{1,0:T(8,128)(2,1)S(1)} custom-call(s32[32,40]{1,0:T(8,128)S(1)} %copy-done.6, s32[40]{0:T(128)S(1)} %bitcast.30, s32[40]{0:T(128)S(1)} %bitcast.31, s32[4]{0:T(128)S(1)} %pad_add_fusion.1.spot, bf16[40,128,128]{2,1,0:T(8,128)(2,1)S(1)} %bitcast.22, bf16[1024,256]{1,0:T(8,128)(2,1)S(1)} %get-tuple-element.37.same, ...), custom_call_target="tpu_custom_call" | custom-call | tf_op jit(solution)/shard_map/history_term/pallas_call | solution.py:229
  170.2 5.3 %collective-permute-start.26 = (bf16[256,256]{1,0:T(8,128)(2,1)S(1)}, bf16[256,256]{1,0:T(8,128)(2,1)S(1)}, u32[]{:S(2)}, u32[]{:S(2)}) collective-permute-start(bf16[256,256]{1,0:T(8,128)(2,1)S(1)} %get-tuple-element.32.rest_0_), channel_id=1, source_target_pairs={{160,0},{176,16},{192,32},{208,48},{224,64},{240,80},{0,96},{16,11... | collective-permute-start | bytes 393224 | tf_op jit(solution)/shard_map/ppermute | solution.py:29
  178.9 5.4 %collective-permute-start.20 = (bf16[256,256]{1,0:T(8,128)(2,1)S(1)}, bf16[256,256]{1,0:T(8,128)(2,1)S(1)}, u32[]{:S(2)}, u32[]{:S(2)}) collective-permute-start(bf16[256,256]{1,0:T(8,128)(2,1)S(1)} %get-tuple-element.32.rest_0_), channel_id=1, source_target_pairs={{96,0},{112,16},{128,32},{144,48},{160,64},{176,80},{192,96},{208,... | collective-permute-start | bytes 393224 | tf_op jit(solution)/shard_map/ppermute | solution.py:29
  187.7 9.5 %collective-permute-done.29.rest_14_ = bf16[256,256]{1,0:T(8,128)(2,1)S(1)} collective-permute-done((bf16[256,256]{1,0:T(8,128)(2,1)S(1)}, bf16[256,256]{1,0:T(8,128)(2,1)S(1)}, u32[]{:S(2)}, u32[]{:S(2)}) %collective-permute-start.29) | collective-permute-done | bytes 131104 | tf_op jit(solution)/shard_map/ppermute | solution.py:29
  199.1 4.9 %collective-permute-done.21.rest_3_ = bf16[256,256]{1,0:T(8,128)(2,1)S(1)} collective-permute-done((bf16[256,256]{1,0:T(8,128)(2,1)S(1)}, bf16[256,256]{1,0:T(8,128)(2,1)S(1)}, u32[]{:S(2)}, u32[]{:S(2)}) %collective-permute-start.21) | collective-permute-done | bytes 131104 | tf_op jit(solution)/shard_map/ppermute | solution.py:29
  204.0 5.5 %collective-permute-start.22 = (bf16[256,256]{1,0:T(8,128)(2,1)S(1)}, bf16[256,256]{1,0:T(8,128)(2,1)S(1)}, u32[]{:S(2)}, u32[]{:S(2)}) collective-permute-start(bf16[256,256]{1,0:T(8,128)(2,1)S(1)} %collective-permute-done.21.rest_3_), channel_id=1, source_target_pairs={{16,0},{32,16},{48,32},{64,48},{80,64},{96,80},{112,96},{128,112},... | collective-permute-start | bytes 393224 | tf_op jit(solution)/shard_map/ppermute | solution.py:29
  211.4 4.6 %collective-permute-start.24 = (bf16[256,256]{1,0:T(8,128)(2,1)S(1)}, bf16[256,256]{1,0:T(8,128)(2,1)S(1)}, u32[]{:S(2)}, u32[]{:S(2)}) collective-permute-start(bf16[256,256]{1,0:T(8,128)(2,1)S(1)} %collective-permute-done.20.rest_6_), channel_id=1, source_target_pairs={{16,0},{32,16},{48,32},{64,48},{80,64},{96,80},{112,96},{128,112},... | collective-permute-start | bytes 393224 | tf_op jit(solution)/shard_map/ppermute | solution.py:29
  218.0 4.6 %collective-permute-start.23 = (bf16[256,256]{1,0:T(8,128)(2,1)S(1)}, bf16[256,256]{1,0:T(8,128)(2,1)S(1)}, u32[]{:S(2)}, u32[]{:S(2)}) collective-permute-start(bf16[256,256]{1,0:T(8,128)(2,1)S(1)} %collective-permute-done.22.rest_4_), channel_id=1, source_target_pairs={{16,0},{32,16},{48,32},{64,48},{80,64},{96,80},{112,96},{128,112},... | collective-permute-start | bytes 393224 | tf_op jit(solution)/shard_map/ppermute | solution.py:29
  224.5 4.6 %collective-permute-start.25 = (bf16[128,256]{1,0:T(8,128)(2,1)S(1)}, bf16[128,256]{1,0:T(8,128)(2,1)S(1)}, u32[]{:S(2)}, u32[]{:S(2)}) collective-permute-start(bf16[128,256]{1,0:T(8,128)(2,1)S(1)} %slice.30), channel_id=1, source_target_pairs={{16,0},{32,16},{48,32},{64,48},{80,64},{96,80},{112,96},{128,112},... | collective-permute-start | bytes 196616 | tf_op jit(solution)/shard_map/ppermute | solution.py:29
  230.4 7.5 %tile_product.3 = (bf16[8,2,128,256]{3,2,1,0:T(8,128)(2,1)S(1)}, bf16[8,2,128,256]{3,2,1,0:T(8,128)(2,1)S(1)}) custom-call(s32[4,16]{1,0:T(4,128)S(1)} %bitcast.26, s32[16]{0:T(128)S(1)} %bitcast.29, s32[80]{0:T(128)S(1)} %bitcast_convert_fusion.theirs, s32[4]{0:T(128)S(1)} %pad_add_fusion.spot.spot_ref, bf16[64,128,128]{2,1,0:T(8,128)(2,1)} %bitcast.34, ...), custom_call_target="tpu_custom_call" | custom-call | tf_op jit(solution)/shard_map/tile_product/pallas_call | solution.py:176
  237.9 4.9 %collective-permute-start.36 = (bf16[8,2,128,256]{3,2,1,0:T(8,128)(2,1)S(1)}, bf16[8,2,128,256]{3,2,1,0:T(8,128)(2,1)S(1)}, u32[]{:S(2)}, u32[]{:S(2)}) collective-permute-start(bf16[8,2,128,256]{3,2,1,0:T(8,128)(2,1)S(1)} %get-tuple-element.39), channel_id=1, source_target_pairs={{0,1},{1,0},{2,3},{3,2},{4,5},{5,4},{6,7},{7,6},{8,9},{9,8},{10,11... | collective-permute-start | bytes 3145736 | tf_op jit(solution)/shard_map/ppermute | solution.py:336
  245.5 22.2 %all_to_all.21.parts_ref = bf16[8,2,128,256]{3,2,1,0:T(8,128)(2,1)S(1)} all-to-all(bf16[8,2,128,256]{3,2,1,0:T(8,128)(2,1)S(1)} %add_convert_fusion), channel_id=1, replica_groups=mesh['x_lo'=2,'z'=16,'x_hi'=2,'y'=4,'core'=2] {'x_hi','y'}, dimensions={0} | all-to-all | bytes 2097152 | tf_op jit(solution)/shard_map/all_to_all | solution.py:338
  267.8 5.7 %all_to_all.22.halves_ref = bf16[2,128,256]{2,1,0:T(8,128)(2,1)S(1)} all-to-all(bf16[2,128,256]{2,1,0:T(8,128)(2,1)S(1)} %add_parts.3), channel_id=1, replica_groups=mesh['x_lo'=2,'z'=16,'x_hi'=2,'y'=4,'core'=2] {'x_lo'}, dimensions={0} | all-to-all | bytes 262144 | tf_op jit(solution)/shard_map/all_to_all | solution.py:395
  (120 shorter events, 66.4 us)
Async XLA Ops:
  10.0 86.5 %collective-permute-start = (bf16[64,128,128]{2,1,0:T(8,128)(2,1)}, bf16[64,128,128]{2,1,0:T(8,128)(2,1)S(1)}, u32[]{:S(2)}, u32[]{:S(2)}) collective-permute-start(bf16[64,128,128]{2,1,0:T(8,128)(2,1)} %bitcast.32), channel_id=1, source_target_pairs={{0,256},{256,0},{1,257},{257,1},{2,258},{258,2},{3,259},{259,3},{4... | collective-permute-start | bytes 6291464 | tf_op jit(solution)/shard_map/ppermute | solution.py:374
  12.0 13.9 %collective-permute-start.10 = (bf16[320,256]{1,0:T(8,128)(2,1)S(1)}, bf16[320,256]{1,0:T(8,128)(2,1)S(1)}, u32[]{:S(2)}, u32[]{:S(2)}) collective-permute-start(bf16[320,256]{1,0:T(8,128)(2,1)S(1)} %pad_maximum_fusion.rest_0_), channel_id=1, source_target_pairs={{240,0},{0,16},{16,32},{32,48},{48,64},{64,80},{80,96},{96,112},{1... | collective-permute-start | bytes 491528 | tf_op jit(solution)/shard_map/ppermute | solution.py:29
  15.6 12.2 %collective-permute-start.1 = (bf16[320,256]{1,0:T(8,128)(2,1)S(1)}, bf16[320,256]{1,0:T(8,128)(2,1)S(1)}, u32[]{:S(2)}, u32[]{:S(2)}) collective-permute-start(bf16[320,256]{1,0:T(8,128)(2,1)S(1)} %pad_maximum_fusion.rest_0_), channel_id=1, source_target_pairs={{16,0},{32,16},{48,32},{64,48},{80,64},{96,80},{112,96},{128,112},... | collective-permute-start | bytes 491528 | tf_op jit(solution)/shard_map/ppermute | solution.py:29
  25.9 10.9 %collective-permute-start.11 = (bf16[320,256]{1,0:T(8,128)(2,1)S(1)}, bf16[320,256]{1,0:T(8,128)(2,1)S(1)}, u32[]{:S(2)}, u32[]{:S(2)}) collective-permute-start(bf16[320,256]{1,0:T(8,128)(2,1)S(1)} %collective-permute-done.10.rest_16_), channel_id=1, source_target_pairs={{240,0},{0,16},{16,32},{32,48},{48,64},{64,80},{80,96},{96,112},{1... | collective-permute-start | bytes 491528 | tf_op jit(solution)/shard_map/ppermute | solution.py:29
  27.8 18.7 %collective-permute-start.2 = (bf16[320,256]{1,0:T(8,128)(2,1)S(1)}, bf16[320,256]{1,0:T(8,128)(2,1)S(1)}, u32[]{:S(2)}, u32[]{:S(2)}) collective-permute-start(bf16[320,256]{1,0:T(8,128)(2,1)S(1)} %collective-permute-done.1.rest_1_), channel_id=1, source_target_pairs={{16,0},{32,16},{48,32},{64,48},{80,64},{96,80},{112,96},{128,112},... | collective-permute-start | bytes 491528 | tf_op jit(solution)/shard_map/ppermute | solution.py:29
  32.4 24.1 %collective-permute-start.9 = (bf16[320,256]{1,0:T(8,128)(2,1)S(1)}, bf16[320,256]{1,0:T(8,128)(2,1)S(1)}, u32[]{:S(2)}, u32[]{:S(2)}) collective-permute-start(bf16[320,256]{1,0:T(8,128)(2,1)S(1)} %pad_maximum_fusion.rest_0_), channel_id=1, source_target_pairs={{160,0},{176,16},{192,32},{208,48},{224,64},{240,80},{0,96},{16,11... | collective-permute-start | bytes 491528 | tf_op jit(solution)/shard_map/ppermute | solution.py:29
  36.8 25.0 %collective-permute-start.12 = (bf16[320,256]{1,0:T(8,128)(2,1)S(1)}, bf16[320,256]{1,0:T(8,128)(2,1)S(1)}, u32[]{:S(2)}, u32[]{:S(2)}) collective-permute-start(bf16[320,256]{1,0:T(8,128)(2,1)S(1)} %collective-permute-done.11.rest_15_), channel_id=1, source_target_pairs={{240,0},{0,16},{16,32},{32,48},{48,64},{64,80},{80,96},{96,112},{1... | collective-permute-start | bytes 491528 | tf_op jit(solution)/shard_map/ppermute | solution.py:29
  41.1 24.2 %collective-permute-start.3 = (bf16[320,256]{1,0:T(8,128)(2,1)S(1)}, bf16[320,256]{1,0:T(8,128)(2,1)S(1)}, u32[]{:S(2)}, u32[]{:S(2)}) collective-permute-start(bf16[320,256]{1,0:T(8,128)(2,1)S(1)} %pad_maximum_fusion.rest_0_), channel_id=1, source_target_pairs={{96,0},{112,16},{128,32},{144,48},{160,64},{176,80},{192,96},{208,... | collective-permute-start | bytes 491528 | tf_op jit(solution)/shard_map/ppermute | solution.py:29
  46.6 24.8 %collective-permute-start.4 = (bf16[320,256]{1,0:T(8,128)(2,1)S(1)}, bf16[320,256]{1,0:T(8,128)(2,1)S(1)}, u32[]{:S(2)}, u32[]{:S(2)}) collective-permute-start(bf16[320,256]{1,0:T(8,128)(2,1)S(1)} %collective-permute-done.2.rest_2_), channel_id=1, source_target_pairs={{16,0},{32,16},{48,32},{64,48},{80,64},{96,80},{112,96},{128,112},... | collective-permute-start | bytes 491528 | tf_op jit(solution)/shard_map/ppermute | solution.py:29
  61.8 20.0 %collective-permute-start.15 = (bf16[320,256]{1,0:T(8,128)(2,1)S(1)}, bf16[320,256]{1,0:T(8,128)(2,1)}, u32[]{:S(2)}, u32[]{:S(2)}) collective-permute-start(bf16[320,256]{1,0:T(8,128)(2,1)S(1)} %collective-permute-done.12.rest_14_), channel_id=1, source_target_pairs={{240,0},{0,16},{16,32},{32,48},{48,64},{64,80},{80,96},{96,112},{1... | collective-permute-start | bytes 491528 | tf_op jit(solution)/shard_map/ppermute | solution.py:29
  71.4 12.4 %collective-permute-start.5 = (bf16[320,256]{1,0:T(8,128)(2,1)S(1)}, bf16[320,256]{1,0:T(8,128)(2,1)}, u32[]{:S(2)}, u32[]{:S(2)}) collective-permute-start(bf16[320,256]{1,0:T(8,128)(2,1)S(1)} %collective-permute-done.4.rest_3_), channel_id=1, source_target_pairs={{16,0},{32,16},{48,32},{64,48},{80,64},{96,80},{112,96},{128,112},... | collective-permute-start | bytes 491528 | tf_op jit(solution)/shard_map/ppermute | solution.py:29
  75.2 13.2 %collective-permute-start.13 = (bf16[320,256]{1,0:T(8,128)(2,1)S(1)}, bf16[320,256]{1,0:T(8,128)(2,1)S(1)}, u32[]{:S(2)}, u32[]{:S(2)}) collective-permute-start(bf16[320,256]{1,0:T(8,128)(2,1)S(1)} %collective-permute-done.9.rest_11_), channel_id=1, source_target_pairs={{240,0},{0,16},{16,32},{32,48},{48,64},{64,80},{80,96},{96,112},{1... | collective-permute-start | bytes 491528 | tf_op jit(solution)/shard_map/ppermute | solution.py:29
  77.1 13.2 %collective-permute-start.7 = (bf16[320,256]{1,0:T(8,128)(2,1)S(1)}, bf16[320,256]{1,0:T(8,128)(2,1)S(1)}, u32[]{:S(2)}, u32[]{:S(2)}) collective-permute-start(bf16[320,256]{1,0:T(8,128)(2,1)S(1)} %collective-permute-done.3.rest_6_), channel_id=1, source_target_pairs={{16,0},{32,16},{48,32},{64,48},{80,64},{96,80},{112,96},{128,112},... | collective-permute-start | bytes 491528 | tf_op jit(solution)/shard_map/ppermute | solution.py:29
  81.8 14.6 %collective-permute-start.16 = (bf16[320,256]{1,0:T(8,128)(2,1)}, bf16[320,256]{1,0:T(8,128)(2,1)}, u32[]{:S(2)}, u32[]{:S(2)}) collective-permute-start(bf16[320,256]{1,0:T(8,128)(2,1)} %collective-permute-done.15.rest_13_), channel_id=1, source_target_pairs={{240,0},{0,16},{16,32},{32,48},{48,64},{64,80},{80,96},{96,112},{1... | collective-permute-start | bytes 491528 | tf_op jit(solution)/shard_map/ppermute | solution.py:29
  83.7 12.7 %collective-permute-start.6 = (bf16[320,256]{1,0:T(8,128)(2,1)}, bf16[320,256]{1,0:T(8,128)(2,1)}, u32[]{:S(2)}, u32[]{:S(2)}) collective-permute-start(bf16[320,256]{1,0:T(8,128)(2,1)} %collective-permute-done.5.rest_4_), channel_id=1, source_target_pairs={{16,0},{32,16},{48,32},{64,48},{80,64},{96,80},{112,96},{128,112},... | collective-permute-start | bytes 491528 | tf_op jit(solution)/shard_map/ppermute | solution.py:29
  105.7 7.6 %collective-permute-start.17 = (bf16[8,2,128,256]{3,2,1,0:T(8,128)(2,1)S(1)}, bf16[8,2,128,256]{3,2,1,0:T(8,128)(2,1)S(1)}, u32[]{:S(2)}, u32[]{:S(2)}) collective-permute-start(bf16[8,2,128,256]{3,2,1,0:T(8,128)(2,1)S(1)} %get-tuple-element.30), channel_id=1, source_target_pairs={{0,1},{1,0},{2,3},{3,2},{4,5},{5,4},{6,7},{7,6},{8,9},{9,8},{10,11... | collective-permute-start | bytes 3145736 | tf_op jit(solution)/shard_map/ppermute | solution.py:336
  114.6 21.4 %all-to-all-start.1 = ((bf16[8,2,128,256]{3,2,1,0:T(8,128)(2,1)}), bf16[8,2,128,256]{3,2,1,0:T(8,128)(2,1)S(1)}, u32[]{:S(2)}, u32[]{:S(2)}) async-start(bf16[8,2,128,256]{3,2,1,0:T(8,128)(2,1)} %add_convert_fusion.1), calls=%async_computation.1 | async-start | bytes 2097152 | tf_op jit(solution)/shard_map/all_to_all | solution.py:338
  121.4 42.3 %collective-permute-start.34 = (bf16[1024,256]{1,0:T(8,128)(2,1)S(1)}, bf16[1024,256]{1,0:T(8,128)(2,1)}, u32[]{:S(2)}, u32[]{:S(2)}) collective-permute-start(bf16[1024,256]{1,0:T(8,128)(2,1)S(1)} %get-tuple-element.37.same), channel_id=1, source_target_pairs={{0,256},{256,0},{1,257},{257,1},{2,258},{258,2},{3,259},{259,3},{4... | collective-permute-start | bytes 1572872 | tf_op jit(solution)/shard_map/ppermute | solution.py:385
  151.6 7.6 %collective-permute-start.18 = (bf16[256,256]{1,0:T(8,128)(2,1)S(1)}, bf16[256,256]{1,0:T(8,128)(2,1)S(1)}, u32[]{:S(2)}, u32[]{:S(2)}) collective-permute-start(bf16[256,256]{1,0:T(8,128)(2,1)S(1)} %get-tuple-element.32.rest_0_), channel_id=1, source_target_pairs={{16,0},{32,16},{48,32},{64,48},{80,64},{96,80},{112,96},{128,112},... | collective-permute-start | bytes 393224 | tf_op jit(solution)/shard_map/ppermute | solution.py:29
  157.2 18.3 %collective-permute-start.28 = (bf16[256,256]{1,0:T(8,128)(2,1)S(1)}, bf16[256,256]{1,0:T(8,128)(2,1)S(1)}, u32[]{:S(2)}, u32[]{:S(2)}) collective-permute-start(bf16[256,256]{1,0:T(8,128)(2,1)S(1)} %collective-permute-done.27.rest_16_), channel_id=1, source_target_pairs={{240,0},{0,16},{16,32},{32,48},{48,64},{64,80},{80,96},{96,112},{1... | collective-permute-start | bytes 393224 | tf_op jit(solution)/shard_map/ppermute | solution.py:29
  159.1 25.2 %collective-permute-start.19 = (bf16[256,256]{1,0:T(8,128)(2,1)S(1)}, bf16[256,256]{1,0:T(8,128)(2,1)S(1)}, u32[]{:S(2)}, u32[]{:S(2)}) collective-permute-start(bf16[256,256]{1,0:T(8,128)(2,1)S(1)} %collective-permute-done.18.rest_1_), channel_id=1, source_target_pairs={{16,0},{32,16},{48,32},{64,48},{80,64},{96,80},{112,96},{128,112},... | collective-permute-start | bytes 393224 | tf_op jit(solution)/shard_map/ppermute | solution.py:29
  167.6 61.5 %collective-permute-start.35 = (bf16[2048,128]{1,0:T(8,128)(2,1)S(1)}, bf16[2048,128]{1,0:T(8,128)(2,1)S(1)}, u32[]{:S(2)}, u32[]{:S(2)}) collective-permute-start(bf16[2048,128]{1,0:T(8,128)(2,1)S(1)} %history_term.1.rest_17_), channel_id=1, source_target_pairs={{0,256},{256,0},{1,257},{257,1},{2,258},{258,2},{3,259},{259,3},{4... | collective-permute-start | bytes 1572872 | tf_op jit(solution)/shard_map/ppermute | solution.py:392
  170.2 17.5 %collective-permute-start.26 = (bf16[256,256]{1,0:T(8,128)(2,1)S(1)}, bf16[256,256]{1,0:T(8,128)(2,1)S(1)}, u32[]{:S(2)}, u32[]{:S(2)}) collective-permute-start(bf16[256,256]{1,0:T(8,128)(2,1)S(1)} %get-tuple-element.32.rest_0_), channel_id=1, source_target_pairs={{160,0},{176,16},{192,32},{208,48},{224,64},{240,80},{0,96},{16,11... | collective-permute-start | bytes 393224 | tf_op jit(solution)/shard_map/ppermute | solution.py:29
  175.5 21.7 %collective-permute-start.29 = (bf16[256,256]{1,0:T(8,128)(2,1)S(1)}, bf16[256,256]{1,0:T(8,128)(2,1)S(1)}, u32[]{:S(2)}, u32[]{:S(2)}) collective-permute-start(bf16[256,256]{1,0:T(8,128)(2,1)S(1)} %collective-permute-done.28.rest_15_), channel_id=1, source_target_pairs={{240,0},{0,16},{16,32},{32,48},{48,64},{64,80},{80,96},{96,112},{1... | collective-permute-start | bytes 393224 | tf_op jit(solution)/shard_map/ppermute | solution.py:29
  178.9 20.2 %collective-permute-start.20 = (bf16[256,256]{1,0:T(8,128)(2,1)S(1)}, bf16[256,256]{1,0:T(8,128)(2,1)S(1)}, u32[]{:S(2)}, u32[]{:S(2)}) collective-permute-start(bf16[256,256]{1,0:T(8,128)(2,1)S(1)} %get-tuple-element.32.rest_0_), channel_id=1, source_target_pairs={{96,0},{112,16},{128,32},{144,48},{160,64},{176,80},{192,96},{208,... | collective-permute-start | bytes 393224 | tf_op jit(solution)/shard_map/ppermute | solution.py:29
  184.3 19.7 %collective-permute-start.21 = (bf16[256,256]{1,0:T(8,128)(2,1)S(1)}, bf16[256,256]{1,0:T(8,128)(2,1)S(1)}, u32[]{:S(2)}, u32[]{:S(2)}) collective-permute-start(bf16[256,256]{1,0:T(8,128)(2,1)S(1)} %collective-permute-done.19.rest_2_), channel_id=1, source_target_pairs={{16,0},{32,16},{48,32},{64,48},{80,64},{96,80},{112,96},{128,112},... | collective-permute-start | bytes 393224 | tf_op jit(solution)/shard_map/ppermute | solution.py:29
  197.2 18.8 %collective-permute-start.32 = (bf16[256,256]{1,0:T(8,128)(2,1)S(1)}, bf16[256,256]{1,0:T(8,128)(2,1)S(1)}, u32[]{:S(2)}, u32[]{:S(2)}) collective-permute-start(bf16[256,256]{1,0:T(8,128)(2,1)S(1)} %collective-permute-done.29.rest_14_), channel_id=1, source_target_pairs={{240,0},{0,16},{16,32},{32,48},{48,64},{64,80},{80,96},{96,112},{1... | collective-permute-start | bytes 393224 | tf_op jit(solution)/shard_map/ppermute | solution.py:29
  204.0 13.9 %collective-permute-start.22 = (bf16[256,256]{1,0:T(8,128)(2,1)S(1)}, bf16[256,256]{1,0:T(8,128)(2,1)S(1)}, u32[]{:S(2)}, u32[]{:S(2)}) collective-permute-start(bf16[256,256]{1,0:T(8,128)(2,1)S(1)} %collective-permute-done.21.rest_3_), channel_id=1, source_target_pairs={{16,0},{32,16},{48,32},{64,48},{80,64},{96,80},{112,96},{128,112},... | collective-permute-start | bytes 393224 | tf_op jit(solution)/shard_map/ppermute | solution.py:29
  209.5 13.0 %collective-permute-start.30 = (bf16[256,256]{1,0:T(8,128)(2,1)S(1)}, bf16[256,256]{1,0:T(8,128)(2,1)S(1)}, u32[]{:S(2)}, u32[]{:S(2)}) collective-permute-start(bf16[256,256]{1,0:T(8,128)(2,1)S(1)} %collective-permute-done.26.rest_11_), channel_id=1, source_target_pairs={{240,0},{0,16},{16,32},{32,48},{48,64},{64,80},{80,96},{96,112},{1... | collective-permute-start | bytes 393224 | tf_op jit(solution)/shard_map/ppermute | solution.py:29
  211.4 13.1 %collective-permute-start.24 = (bf16[256,256]{1,0:T(8,128)(2,1)S(1)}, bf16[256,256]{1,0:T(8,128)(2,1)S(1)}, u32[]{:S(2)}, u32[]{:S(2)}) collective-permute-start(bf16[256,256]{1,0:T(8,128)(2,1)S(1)} %collective-permute-done.20.rest_6_), channel_id=1, source_target_pairs={{16,0},{32,16},{48,32},{64,48},{80,64},{96,80},{112,96},{128,112},... | collective-permute-start | bytes 393224 | tf_op jit(solution)/shard_map/ppermute | solution.py:29
  216.0 14.4 %collective-permute-start.33 = (bf16[256,256]{1,0:T(8,128)(2,1)S(1)}, bf16[256,256]{1,0:T(8,128)(2,1)S(1)}, u32[]{:S(2)}, u32[]{:S(2)}) collective-permute-start(bf16[256,256]{1,0:T(8,128)(2,1)S(1)} %collective-permute-done.32.rest_13_), channel_id=1, source_target_pairs={{240,0},{0,16},{16,32},{32,48},{48,64},{64,80},{80,96},{96,112},{1... | collective-permute-start | bytes 393224 | tf_op jit(solution)/shard_map/ppermute | solution.py:29
  218.0 12.5 %collective-permute-start.23 = (bf16[256,256]{1,0:T(8,128)(2,1)S(1)}, bf16[256,256]{1,0:T(8,128)(2,1)S(1)}, u32[]{:S(2)}, u32[]{:S(2)}) collective-permute-start(bf16[256,256]{1,0:T(8,128)(2,1)S(1)} %collective-permute-done.22.rest_4_), channel_id=1, source_target_pairs={{16,0},{32,16},{48,32},{64,48},{80,64},{96,80},{112,96},{128,112},... | collective-permute-start | bytes 393224 | tf_op jit(solution)/shard_map/ppermute | solution.py:29
  (32 other events, 901.3 us)

commit v5 on v4

v5 whole, which is shorter than its diff:
```python
import functools

import jax
import jax.numpy as jnp
from jax import lax
from jax.experimental import pallas as pl
from jax.experimental.pallas import tpu as pltpu
from jax.sharding import Mesh, PartitionSpec as P

F = 512
HALF = 256
BLOCK = 128
HOWN = 4
ROWS = 16
SLOTS = 4
FEAT = 32
LIST = 40
WIDE = 128
DOM = ("x_lo", "zq", "zr")
Z = ("zq", "zr")
GRID = ("x_hi", "y", "core")
SIDE = ("x_hi", "y")
SWAP = [(0, 1), (1, 0)]


def from_z(value, offset):
    return lax.ppermute(value, Z, [((z + offset) % 16, z) for z in range(16)])


def params(mib):
    return pltpu.CompilerParams(vmem_limit_bytes=mib << 20)


def tile_body(second, n_chunks, cols, counts, theirs, spot, *rest):
    n_parts = 2 if second else 1
    tiles = rest[:n_parts]
    chunks = rest[n_parts : n_parts + n_chunks]
    if second:
        extras = rest[n_parts + n_chunks : n_parts + n_chunks + 2]
        keep, send, panel, adj, sems, added = rest[-6:]
    else:
        keep, send, panel, adj, sems = rest[-5:]
    core = spot[1]
    moves = []

    def move(source, target):
        moves.append(pltpu.make_async_copy(source, target, sems.at[len(moves)]))
        moves[-1].start()

    start = 0
    for source in chunks:
        move(source, panel.at[pl.ds(start, source.shape[0])])
        start += source.shape[0]
    for k in range(n_parts):
        for c in range(4):
            move(tiles[k].at[pl.ds(16 * c, 16)], adj.at[pl.ds(64 * k + 16 * c, 16)])
    if second:
        for k in range(2):
            move(extras[k], added.at[k])

    def product(k, row):
        base = (ROWS * k + row) * SLOTS
        count = counts[row] if k == 0 else theirs[ROWS * SLOTS + row]
        left = []
        right = []
        for slot in range(SLOTS):
            block = adj[base + slot]
            left.append(jnp.where(slot < count, block, jnp.zeros_like(block)))
            col = cols[slot, row] if k == 0 else theirs[row * SLOTS + slot]
            z = col & 15
            index = ((z - spot[3]) & 3) * 4 + (z >> 2) if second else z
            start = pl.multiple_of((index * 2 + (col >> 4)) * BLOCK, BLOCK)
            right.append(panel[pl.ds(start, BLOCK), :])
        return jnp.dot(
            jnp.concatenate(left, axis=1),
            jnp.concatenate(right, axis=0),
            preferred_element_type=jnp.float32,
        )

    def with_history(k, row, value):
        piece = added[k, row * BLOCK : (row + 1) * BLOCK, :].astype(jnp.float32)
        zero = jnp.zeros_like(piece)
        wide = [jnp.where(spot[2] == group, piece, zero) for group in range(2)]
        return value + jnp.concatenate(wide, axis=1)

    def two_rows(k, j):
        pair = [product(k, 2 * j + side) for side in range(2)]
        if second:
            pair = [with_history(k, 2 * j + side, pair[side]) for side in range(2)]
        even, odd = [value.astype(jnp.bfloat16) for value in pair]
        part = spot[0] if k == 0 else 1 - spot[0]
        where = (j, part) if second else (j,)
        keep[where] = jnp.where(core == 0, even, odd)
        send[where] = jnp.where(core == 0, odd, even)

    for n in range(n_chunks):
        moves[n].wait()
    for k in range(n_parts):
        for c in range(4):
            moves[n_chunks + 4 * k + c].wait()
            if second and c == 0:
                moves[n_chunks + 8 + k].wait()
            two_rows(k, 2 * c)
            two_rows(k, 2 * c + 1)


def tile_product(cols, counts, theirs, spot, tiles, chunks, extras):
    operands = [*tiles, *chunks, *extras]
    second = bool(extras)
    width = chunks[0].shape[1]
    shape = (ROWS // 2, 2, BLOCK, width) if second else (ROWS // 2, BLOCK, width)
    half = jax.ShapeDtypeStruct(shape, jnp.bfloat16)
    scratch = [
        pltpu.VMEM((32 * BLOCK, width), jnp.bfloat16),
        pltpu.VMEM((len(tiles) * ROWS * SLOTS, BLOCK, BLOCK), jnp.bfloat16),
        pltpu.SemaphoreType.DMA((len(chunks) + 4 * len(tiles) + len(extras),)),
    ]
    if second:
        scratch.append(pltpu.VMEM((2, ROWS * BLOCK, WIDE), jnp.bfloat16))
    out_spec = pl.BlockSpec(shape, lambda i, *_: (0,) * len(shape))
    return pl.pallas_call(
        functools.partial(tile_body, second, len(chunks)),
        out_shape=(half, half),
        grid_spec=pltpu.PrefetchScalarGridSpec(
            num_scalar_prefetch=4,
            grid=(1,),
            in_specs=[pl.BlockSpec(memory_space=pltpu.HBM)] * len(operands),
            out_specs=(out_spec, out_spec),
            scratch_shapes=scratch,
        ),
        compiler_params=params(20),
        name="tile_product",
    )(cols, counts, theirs, spot, *operands)


def history_body(listed, order, rows, spot, adj, same, other, out, weights, store, total, sems):
    moves = [
        pltpu.make_async_copy(adj, weights, sems.at[0]),
        pltpu.make_async_copy(same, store.at[0], sems.at[1]),
        pltpu.make_async_copy(other, store.at[1], sems.at[2]),
    ]
    for move in moves:
        move.start()
    total[...] = jnp.zeros_like(total)
    for move in moves:
        move.wait()

    def one(slot):
        block = listed[spot[0], order[slot]]
        owner = block >> 2
        piece = block & 3
        source = pl.multiple_of((owner & 15) * FEAT, FEAT)
        lane = pl.multiple_of(piece * BLOCK, BLOCK)
        return lax.dot_general(
            weights[slot],
            store[(owner >> 4) ^ spot[2], pl.ds(source, FEAT), pl.ds(lane, BLOCK)],
            (((1,), (1,)), ((), ())),
            preferred_element_type=jnp.float32,
        )

    def step(n, carry):
        parts = [one(n * 5 + k) for k in range(5)]
        for k, part in enumerate(parts):
            target = pl.multiple_of(rows[n * 5 + k] * BLOCK, BLOCK)
            total[pl.ds(target, BLOCK), :FEAT] += part
        return carry

    lax.fori_loop(0, LIST // 5, step, 0)
    out[...] = pltpu.roll(total[...], spot[1] * FEAT, 1).astype(jnp.bfloat16)


def history_term(listed, order, rows, spot, adj, same, other):
    return pl.pallas_call(
        history_body,
        out_shape=jax.ShapeDtypeStruct((ROWS * BLOCK, WIDE), jnp.bfloat16),
        grid_spec=pltpu.PrefetchScalarGridSpec(
            num_scalar_prefetch=4,
            grid=(1,),
            in_specs=[pl.BlockSpec(memory_space=pltpu.HBM)] * 3,
            out_specs=pl.BlockSpec((ROWS * BLOCK, WIDE), lambda i, *_: (0, 0)),
            scratch_shapes=[
                pltpu.VMEM(adj.shape, jnp.bfloat16),
                pltpu.VMEM((2, *same.shape), jnp.bfloat16),
                pltpu.VMEM((ROWS * BLOCK, WIDE), jnp.float32),
                pltpu.SemaphoreType.DMA((3,)),
            ],
        ),
        compiler_params=params(16),
        name="history_term",
    )(listed, order, rows, spot, adj, same, other)


def add_parts(parts):
    def body(parts_ref, out):
        total = parts_ref[0].astype(jnp.float32)
        for k in range(1, parts.shape[0]):
            total = total + parts_ref[k].astype(jnp.float32)
        out[...] = total.astype(jnp.bfloat16)

    return pl.pallas_call(
        body,
        out_shape=jax.ShapeDtypeStruct(parts.shape[1:], jnp.bfloat16),
        compiler_params=params(8),
        name="add_parts",
    )(parts)


def first_dense(parts, weight):
    def body(parts_ref, weight_ref, hidden, halves):
        total = parts_ref[0].astype(jnp.float32)
        for k in range(1, parts.shape[0]):
            total = total + parts_ref[k].astype(jnp.float32)
        value = jnp.dot(
            total.astype(jnp.bfloat16), weight_ref[...], preferred_element_type=jnp.float32
        )
        value = jnp.maximum(value, 0.0).astype(jnp.bfloat16)
        hidden[...] = value
        halves[0] = value[:, :HALF]
        halves[1] = value[:, HALF:]

    return pl.pallas_call(
        body,
        out_shape=(
            jax.ShapeDtypeStruct((BLOCK, F), jnp.bfloat16),
            jax.ShapeDtypeStruct((2, BLOCK, HALF), jnp.bfloat16),
        ),
        compiler_params=params(8),
        name="first_dense",
    )(parts, weight)


def second_dense(halves, weight):
    def body(halves_ref, weight_ref, out):
        rows = jnp.concatenate([halves_ref[0], halves_ref[1]], axis=1)
        value = jnp.dot(rows, weight_ref[...], preferred_element_type=jnp.float32)
        out[...] = value.astype(jnp.bfloat16)

    return pl.pallas_call(
        body,
        out_shape=jax.ShapeDtypeStruct((BLOCK, F), jnp.bfloat16),
        compiler_params=params(8),
        name="second_dense",
    )(halves, weight)


def gather_quads(chunk):
    same = lax.all_gather(chunk, "zq", axis=0, tiled=True)
    above = from_z(same, 1)
    below = from_z(same, -1)
    half = same.shape[0] // 2
    across = [from_z(above[:half], 1), from_z(below[half:], -1)]
    return [same, above, *across, below]


def reduce_rows(keep, send):
    other = lax.ppermute(send, "core", SWAP)
    both = (keep.astype(jnp.float32) + other.astype(jnp.float32)).astype(jnp.bfloat16)
    return lax.all_to_all(both, SIDE, 0, 0, tiled=True)


def local(
    node_feats,
    adj_vals,
    adj_col,
    adj_count,
    hist_store,
    hist_list,
    hist_adj,
    hist_row,
    hist_col,
    w_first,
    w_second,
):
    adj = adj_vals[0, 0].reshape(ROWS * SLOTS, BLOCK, BLOCK)
    cols = adj_col[0, 0].T
    counts = adj_count[0, 0]
    x_lo = lax.axis_index("x_lo")
    x_hi = lax.axis_index("x_hi")
    grid_index = lax.axis_index(GRID)
    group = jnp.where(x_lo == x_hi, (grid_index // 4) % 2, -1)
    spot = jnp.stack([x_lo, lax.axis_index("core"), group, lax.axis_index(Z)])
    spot = spot.astype(jnp.int32)
    hist_spot = jnp.stack([lax.axis_index(DOM), grid_index % 4, x_lo]).astype(jnp.int32)

    pair = lax.all_gather(node_feats, "x_lo", axis=0, tiled=True)
    panel = lax.all_gather(pair, Z, axis=0, tiled=True)

    numbers = jnp.concatenate([adj_col[0, 0].reshape(-1), counts])
    pair, numbers = lax.optimization_barrier((pair, numbers))
    both = lax.all_gather(numbers, "x_lo", axis=0, tiled=False)
    theirs = lax.dynamic_index_in_dim(both, 1 - x_lo, 0, keepdims=False)
    adj_held, theirs = lax.optimization_barrier((adj, theirs))
    partner = lax.ppermute(adj_held, "x_lo", SWAP)

    store = lax.all_gather(hist_store, Z, axis=0, tiled=True)
    store, partner = lax.optimization_barrier((store, partner))
    other_store = lax.ppermute(store, "x_lo", SWAP)
    mine = history_term(
        hist_list, hist_col[0], hist_row[0], hist_spot, hist_adj[0], store, other_store
    )
    extras = (mine, lax.ppermute(mine, "x_lo", SWAP))
    panel, extras = lax.optimization_barrier((panel, extras))

    adj = pltpu.with_memory_space_constraint(adj, pltpu.HBM)
    panel = pltpu.with_memory_space_constraint(panel, pltpu.HBM)
    tables = (cols, counts, theirs, spot)
    parts = reduce_rows(*tile_product(*tables, (adj,), (panel,), ()))
    hidden, halves = first_dense(parts, w_first)

    chunk = lax.all_to_all(halves, "x_lo", 0, 0, tiled=True).reshape(2 * BLOCK, HALF)
    chunks = gather_quads(chunk)
    parts = reduce_rows(*tile_product(*tables, (adj, partner), chunks, extras))
    halves = lax.all_to_all(add_parts(parts), "x_lo", 0, 0, tiled=True)
    return hidden, second_dense(halves, w_second)


def solution(mesh):
    fine = Mesh(
        mesh.devices.reshape(2, 4, 4, 2, 4, 2), ("x_lo", "zq", "zr", "x_hi", "y", "core")
    )
    placed = (
        P(DOM + GRID, None),
        P(DOM, GRID),
        P(DOM, GRID),
        P(DOM, GRID),
        P(GRID, DOM),
        P(),
        P(DOM),
        P(DOM),
        P(DOM),
        P(),
        P(),
    )
    return jax.shard_map(
        local,
        mesh=fine,
        in_specs=placed,
        out_specs=(P(DOM + GRID, None), P(DOM + GRID, None)),
        check_vma=False,
    )
```

time: 278 us -> 248 us (0.89)
  starting transfers between devices: 146 us -> 40.2 us
  blocking collectives: 46.4 us -> 126 us
  between operations: 1.51 us -> 14.9 us
  waiting for transfers between devices: 52.5 us -> 40.3 us
  Pallas kernels: 21.4 us -> 14.2 us
  local copies, waits for them, and re-layouts: 4.68 us -> 7.72 us
    ppermute x32 -> x4, starting transfers between devices: 122 us -> 13.3 us  [from_z(): return lax.ppermute(value, Z, [((z + offset) % 16, z) for z in range(16)])]
    all_gather x1 -> x3, blocking collectives: 12 us -> 70.7 us  [the longest x1 35.3 us: local(): store = lax.all_gather(hist_store, Z, axis=0, tiled=True)]
    ppermute x32 -> x4, waiting for transfers between devices: 36.1 us -> 11.2 us  [from_z(): return lax.ppermute(value, Z, [((z + offset) % 16, z) for z in range(16)])]
    all_to_all x3 -> x4, blocking collectives: 34.4 us -> 52.4 us  [the longest x2 41 us: reduce_rows(): return lax.all_to_all(both, SIDE, 0, 0, tiled=True)]
    all_to_all x1 -> x0, waiting for transfers between devices: 11.8 us -> none  [reduce_rows(): return add_parts(lax.all_to_all(both, SIDE, 0, 0, tiled=True))]
    ppermute x1, waiting for transfers between devices: 0.01 us -> 11.2 us  [local(): other_store = lax.ppermute(store, 'x_lo', SWAP)]
    ppermute x2, starting transfers between devices: 10.2 us -> 21.1 us  [reduce_rows(): other = lax.ppermute(send, 'core', SWAP)]
    ppermute x1, waiting for transfers between devices: 0.01 us -> 8.28 us  [local(): extras = (mine, lax.ppermute(mine, 'x_lo', SWAP))]
  transfers between devices with their start and end apart: 38 -> 10, of which waited for: 12 -> 8; matrix products, arithmetic and copies ran while one was open for 0% -> 1% of each run, Pallas kernels for 2% -> 1%
where the time goes in v5:
time: 248 us; the launch traced here: 245 us
  blocking collectives  126 us (51%)
  waiting for transfers between devices  40.3 us (16%)
  starting transfers between devices  40.2 us (16%)
  between operations  14.9 us (6%)
  Pallas kernels  14.2 us (6%)
  local copies, waits for them, and re-layouts  7.72 us (3%)
    all_to_all x2, blocking collectives, reduce_rows(): return lax.all_to_all(both, SIDE, 0, 0, tiled=True)  41 us
    all_gather x1, blocking collectives, local(): store = lax.all_gather(hist_store, Z, axis=0, tiled=True)  35.3 us
    all_gather x1, blocking collectives, gather_quads(): same = lax.all_gather(chunk, 'zq', axis=0, tiled=True)  28.5 us
    ppermute x2, starting transfers between devices, reduce_rows(): other = lax.ppermute(send, 'core', SWAP)  21.1 us
    ppermute x4, starting transfers between devices, from_z(): return lax.ppermute(value, Z, [((z + offset) % 16, z) for z in range(16)])  13.3 us
    ppermute x1, waiting for transfers between devices, local(): other_store = lax.ppermute(store, 'x_lo', SWAP)  11.2 us
    ppermute x4, waiting for transfers between devices, from_z(): return lax.ppermute(value, Z, [((z + offset) % 16, z) for z in range(16)])  11.2 us
    pallas_call x2, Pallas kernels, tile_product(): pl.pallas_call(functools.partial(tile_body, second, len(chunks)), out_sha...  9.32 us
  transfers between devices with their start and end apart: 10, of which 8 were waited for; matrix products, arithmetic and copies ran while one was open for 1% of the time, Pallas kernels for 1%

profile of v5, /device:TPU:1, one launch (start us, length us, event | category | flops | bytes accessed | tf_op | source)
XLA Modules:
  0.0 245.1 jit_solution(712746700636773559)
XLA Ops:
  7.2 6.9 %all_gather.18 = bf16[256,512]{1,0:T(8,128)(2,1)} all-gather(bf16[128,512]{1,0:T(8,128)(2,1)} %param.11), channel_id=1, replica_groups=mesh['x_lo'=2,'zq'=4,'zr'=4,'x_hi'=2,'y'=4,'core'=2] {'x_lo'}, dimensions={0}, use_global_device_ids=true | all-gather | bytes 393216 | tf_op jit(solution)/shard_map/all_gather | solution.py:285
  15.8 1.3 dynamic-slice
  18.0 3.1 %all-reduce.1 = s32[2,80]{1,0:T(2,128)S(1)} all-reduce(s32[2,80]{1,0:T(2,128)S(1)} %reshape.8), channel_id=2, replica_groups=mesh['x_lo'=2,'zq'=4,'zr'=4,'x_hi'=2,'y'=4,'core'=2] {'x_lo'}, use_global_device_ids=true, to_apply=%add | all-reduce | flops 160 | bytes 1280
  21.2 1.9 collective-permute-start
  23.1 35.3 %all_gather.22.same = bf16[512,512]{1,0:T(8,128)(2,1)S(1)} all-gather(bf16[32,512]{1,0:T(8,128)(2,1)} %param.15), channel_id=1, replica_groups=mesh['x_lo'=2,'zq'=4,'zr'=4,'x_hi'=2,'y'=4,'core'=2] {'zq','zr'}, dimensions={0}, use_global_device_ids=true | all-gather | bytes 557056 | tf_op jit(solution)/shard_map/all_gather | solution.py:295
  58.4 5.0 %collective-permute-done.rest_1_ = bf16[64,128,128]{2,1,0:T(8,128)(2,1)S(1)} collective-permute-done((bf16[64,128,128]{2,1,0:T(8,128)(2,1)}, bf16[64,128,128]{2,1,0:T(8,128)(2,1)S(1)}, u32[]{:S(2)}, u32[]{:S(2)}) %collective-permute-start) | collective-permute-done | bytes 2097184 | tf_op jit(solution)/shard_map/ppermute | solution.py:293
  63.4 1.9 collective-permute-start.1
  65.4 11.2 %collective-permute-done.1.other = bf16[512,512]{1,0:T(8,128)(2,1)S(1)} collective-permute-done((bf16[512,512]{1,0:T(8,128)(2,1)S(1)}, bf16[512,512]{1,0:T(8,128)(2,1)S(1)}, u32[]{:S(2)}, u32[]{:S(2)}) %collective-permute-start.1) | collective-permute-done | bytes 524320 | tf_op jit(solution)/shard_map/ppermute | solution.py:297
  77.5 1.3 copy-done
  78.8 1.1 copy-done.4
  81.9 2.9 %history_term.1.rest_7_ = bf16[2048,128]{1,0:T(8,128)(2,1)S(1)} custom-call(s32[32,40]{1,0:T(8,128)S(1)} %copy-done.6, s32[40]{0:T(128)S(1)} %bitcast.26, s32[40]{0:T(128)S(1)} %bitcast.27, s32[3]{0:T(128)S(1)} %pad_add_fusion.2.spot, bf16[40,128,128]{2,1,0:T(8,128)(2,1)S(1)} %bitcast.20, bf16[512,512]{1,0:T(8,128)(2,1)S(1)} %all_gather.22.same, ...), custom_call_target="tpu_custom_call" | custom-call | tf_op jit(solution)/shard_map/history_term/pallas_call | solution.py:173
  84.8 1.9 collective-permute-start.2
  86.8 8.3 %collective-permute-done.2.rest_8_ = bf16[2048,128]{1,0:T(8,128)(2,1)S(1)} collective-permute-done((bf16[2048,128]{1,0:T(8,128)(2,1)S(1)}, bf16[2048,128]{1,0:T(8,128)(2,1)S(1)}, u32[]{:S(2)}, u32[]{:S(2)}) %collective-permute-start.2) | collective-permute-done | bytes 524320 | tf_op jit(solution)/shard_map/ppermute | solution.py:301
  95.1 4.8 %tile_product.2 = (bf16[8,128,512]{2,1,0:T(8,128)(2,1)S(1)}, bf16[8,128,512]{2,1,0:T(8,128)(2,1)S(1)}) custom-call(s32[4,16]{1,0:T(4,128)S(1)} %bitcast.21, s32[16]{0:T(128)S(1)} %bitcast.24, s32[80]{0:T(128)S(1)} %dynamic-slice_bitcast_fusion.theirs, s32[4]{0:T(128)S(1)} %pad_add_fusion.1.spot, bf16[64,128,128]{2,1,0:T(8,128)(2,1)} %bitcast.29, ...), custom_call_target="tpu_custom_call" | custom-call | tf_op jit(solution)/shard_map/tile_product/pallas_call | solution.py:121
  99.9 11.3 %collective-permute-start.3 = (bf16[8,128,512]{2,1,0:T(8,128)(2,1)S(1)}, bf16[8,128,512]{2,1,0:T(8,128)(2,1)S(1)}, u32[]{:S(2)}, u32[]{:S(2)}) collective-permute-start(bf16[8,128,512]{2,1,0:T(8,128)(2,1)S(1)} %get-tuple-element.22), channel_id=1, source_target_pairs={{0,1},{1,0},{2,3},{3,2},{4,5},{5,4},{6,7},{7,6},{8,9},{9,8},{10,11... | collective-permute-start | bytes 3145736 | tf_op jit(solution)/shard_map/ppermute | solution.py:256
  111.2 2.3 collective-permute-done.3
  113.8 22.8 %all_to_all.20.parts_ref = bf16[8,128,512]{2,1,0:T(8,128)(2,1)S(1)} all-to-all(bf16[8,128,512]{2,1,0:T(8,128)(2,1)S(1)} %add_convert_fusion.1), channel_id=1, replica_groups=mesh['x_lo'=2,'zq'=4,'zr'=4,'x_hi'=2,'y'=4,'core'=2] {'x_hi','y'}, dimensions={0} | all-to-all | bytes 2097152 | tf_op jit(solution)/shard_map/all_to_all | solution.py:258
  136.6 1.0 first_dense.1
  137.6 5.7 %all_to_all.21 = bf16[2,128,256]{2,1,0:T(8,128)(2,1)S(1)} all-to-all(bf16[2,128,256]{2,1,0:T(8,128)(2,1)S(1)} %get-tuple-element.25), channel_id=1, replica_groups=mesh['x_lo'=2,'zq'=4,'zr'=4,'x_hi'=2,'y'=4,'core'=2] {'x_lo'}, dimensions={0} | all-to-all | bytes 262144 | tf_op jit(solution)/shard_map/all_to_all | solution.py:310
  143.3 28.5 %all_gather.23.rest_2_ = bf16[1024,256]{1,0:T(8,128)(2,1)S(1)} all-gather(bf16[256,256]{1,0:T(8,128)(2,1)S(1)} %bitcast.31), channel_id=1, replica_groups=mesh['x_lo'=2,'zq'=4,'zr'=4,'x_hi'=2,'y'=4,'core'=2] {'zq'}, dimensions={0}, use_global_device_ids=true | all-gather | bytes 655360 | tf_op jit(solution)/shard_map/all_gather | solution.py:247
  171.8 4.9 %collective-permute-start.6 = (bf16[1024,256]{1,0:T(8,128)(2,1)S(1)}, bf16[1024,256]{1,0:T(8,128)(2,1)S(1)}, u32[]{:S(2)}, u32[]{:S(2)}) collective-permute-start(bf16[1024,256]{1,0:T(8,128)(2,1)S(1)} %all_gather.23.rest_2_), channel_id=1, source_target_pairs={{240,0},{0,16},{16,32},{32,48},{48,64},{64,80},{80,96},{96,112},{1... | collective-permute-start | bytes 1572872 | tf_op jit(solution)/shard_map/ppermute | solution.py:27
  176.7 1.9 collective-permute-start.4
  178.6 5.7 %collective-permute-done.6.rest_6_ = bf16[1024,256]{1,0:T(8,128)(2,1)S(1)} collective-permute-done((bf16[1024,256]{1,0:T(8,128)(2,1)S(1)}, bf16[1024,256]{1,0:T(8,128)(2,1)S(1)}, u32[]{:S(2)}, u32[]{:S(2)}) %collective-permute-start.6) | collective-permute-done | bytes 524320 | tf_op jit(solution)/shard_map/ppermute | solution.py:27
  184.3 3.1 %collective-permute-start.7 = (bf16[512,256]{1,0:T(8,128)(2,1)S(1)}, bf16[512,256]{1,0:T(8,128)(2,1)S(1)}, u32[]{:S(2)}, u32[]{:S(2)}) collective-permute-start(bf16[512,256]{1,0:T(8,128)(2,1)S(1)} %slice.9), channel_id=1, source_target_pairs={{240,0},{0,16},{16,32},{32,48},{48,64},{64,80},{80,96},{96,112},{1... | collective-permute-start | bytes 786440 | tf_op jit(solution)/shard_map/ppermute | solution.py:27
  187.5 3.4 %collective-permute-start.5 = (bf16[512,256]{1,0:T(8,128)(2,1)S(1)}, bf16[512,256]{1,0:T(8,128)(2,1)S(1)}, u32[]{:S(2)}, u32[]{:S(2)}) collective-permute-start(bf16[512,256]{1,0:T(8,128)(2,1)S(1)} %slice.8), channel_id=1, source_target_pairs={{16,0},{32,16},{48,32},{64,48},{80,64},{96,80},{112,96},{128,112},... | collective-permute-start | bytes 786440 | tf_op jit(solution)/shard_map/ppermute | solution.py:27
  190.8 2.3 collective-permute-done.7.rest_5_
  193.1 3.3 %collective-permute-done.5.rest_4_ = bf16[512,256]{1,0:T(8,128)(2,1)S(1)} collective-permute-done((bf16[512,256]{1,0:T(8,128)(2,1)S(1)}, bf16[512,256]{1,0:T(8,128)(2,1)S(1)}, u32[]{:S(2)}, u32[]{:S(2)}) %collective-permute-start.5) | collective-permute-done | bytes 262176 | tf_op jit(solution)/shard_map/ppermute | solution.py:27
  196.3 4.5 %tile_product.3 = (bf16[8,2,128,256]{3,2,1,0:T(8,128)(2,1)S(1)}, bf16[8,2,128,256]{3,2,1,0:T(8,128)(2,1)S(1)}) custom-call(s32[4,16]{1,0:T(4,128)S(1)} %bitcast.22, s32[16]{0:T(128)S(1)} %bitcast.25, s32[80]{0:T(128)S(1)} %dynamic-slice_bitcast_fusion.theirs, s32[4]{0:T(128)S(1)} %pad_add_fusion.1.spot, bf16[64,128,128]{2,1,0:T(8,128)(2,1)} %bitcast.30, ...), custom_call_target="tpu_custom_call" | custom-call | tf_op jit(solution)/shard_map/tile_product/pallas_call | solution.py:121
  200.9 9.8 %collective-permute-start.8 = (bf16[8,2,128,256]{3,2,1,0:T(8,128)(2,1)S(1)}, bf16[8,2,128,256]{3,2,1,0:T(8,128)(2,1)S(1)}, u32[]{:S(2)}, u32[]{:S(2)}) collective-permute-start(bf16[8,2,128,256]{3,2,1,0:T(8,128)(2,1)S(1)} %get-tuple-element.29), channel_id=1, source_target_pairs={{0,1},{1,0},{2,3},{3,2},{4,5},{5,4},{6,7},{7,6},{8,9},{9,8},{10,11... | collective-permute-start | bytes 3145736 | tf_op jit(solution)/shard_map/ppermute | solution.py:256
  210.7 2.3 collective-permute-done.8
  213.3 18.2 %all_to_all.22.parts_ref = bf16[8,2,128,256]{3,2,1,0:T(8,128)(2,1)S(1)} all-to-all(bf16[8,2,128,256]{3,2,1,0:T(8,128)(2,1)S(1)} %add_convert_fusion), channel_id=1, replica_groups=mesh['x_lo'=2,'zq'=4,'zr'=4,'x_hi'=2,'y'=4,'core'=2] {'x_hi','y'}, dimensions={0} | all-to-all | bytes 2097152 | tf_op jit(solution)/shard_map/all_to_all | solution.py:258
  231.7 5.7 %all_to_all.23.halves_ref = bf16[2,128,256]{2,1,0:T(8,128)(2,1)S(1)} all-to-all(bf16[2,128,256]{2,1,0:T(8,128)(2,1)S(1)} %add_parts.1), channel_id=1, replica_groups=mesh['x_lo'=2,'zq'=4,'zr'=4,'x_hi'=2,'y'=4,'core'=2] {'x_lo'}, dimensions={0} | all-to-all | bytes 262144 | tf_op jit(solution)/shard_map/all_to_all | solution.py:313
  (37 shorter events, 6.7 us)
Async XLA Ops:
  7.2 87.9 %copy-start.5 = (s32[1,1,16,4]{2,3,1,0:T(4,128)S(1)}, s32[1,1,16,4]{2,3,1,0:T(4,128)}, u32[]{:S(2)}) copy-start(s32[1,1,16,4]{2,3,1,0:T(4,128)} %param.13) | copy-start | bytes 772
  7.2 87.9 %copy-start.7 = (s32[1,1,16]{2,1,0:T(1,128)S(1)}, s32[1,1,16]{2,1,0:T(1,128)}, u32[]{:S(2)}) copy-start(s32[1,1,16]{2,1,0:T(1,128)} %param.14) | copy-start | bytes 196
  7.2 87.9 %all-gather.3.cloned.1.call-start = ((), (), s32[]{:S(2)}) async-start(), calls=%async_computation.4 | async-start | bytes 4456448 | tf_op jit(solution)/shard_map/all_gather | solution.py:286
  21.2 42.3 %collective-permute-start = (bf16[64,128,128]{2,1,0:T(8,128)(2,1)}, bf16[64,128,128]{2,1,0:T(8,128)(2,1)S(1)}, u32[]{:S(2)}, u32[]{:S(2)}) collective-permute-start(bf16[64,128,128]{2,1,0:T(8,128)(2,1)} %bitcast.28), channel_id=1, source_target_pairs={{0,256},{256,0},{1,257},{257,1},{2,258},{258,2},{3,259},{259,3},{4... | collective-permute-start | bytes 6291464 | tf_op jit(solution)/shard_map/ppermute | solution.py:293
  63.4 13.3 %collective-permute-start.1 = (bf16[512,512]{1,0:T(8,128)(2,1)S(1)}, bf16[512,512]{1,0:T(8,128)(2,1)S(1)}, u32[]{:S(2)}, u32[]{:S(2)}) collective-permute-start(bf16[512,512]{1,0:T(8,128)(2,1)S(1)} %all_gather.22.same), channel_id=1, source_target_pairs={{0,256},{256,0},{1,257},{257,1},{2,258},{258,2},{3,259},{259,3},{4... | collective-permute-start | bytes 1572872 | tf_op jit(solution)/shard_map/ppermute | solution.py:297
  76.7 0.8 copy-start.3
  77.5 1.3 copy-start
  78.8 1.1 copy-start.4
  79.9 0.7 copy-start.6
  80.6 0.7 copy-start.8
  81.2 0.7 copy-start.9
  84.8 10.3 %collective-permute-start.2 = (bf16[2048,128]{1,0:T(8,128)(2,1)S(1)}, bf16[2048,128]{1,0:T(8,128)(2,1)S(1)}, u32[]{:S(2)}, u32[]{:S(2)}) collective-permute-start(bf16[2048,128]{1,0:T(8,128)(2,1)S(1)} %history_term.1.rest_7_), channel_id=1, source_target_pairs={{0,256},{256,0},{1,257},{257,1},{2,258},{258,2},{3,259},{259,3},{4... | collective-permute-start | bytes 1572872 | tf_op jit(solution)/shard_map/ppermute | solution.py:301
  99.9 13.5 %collective-permute-start.3 = (bf16[8,128,512]{2,1,0:T(8,128)(2,1)S(1)}, bf16[8,128,512]{2,1,0:T(8,128)(2,1)S(1)}, u32[]{:S(2)}, u32[]{:S(2)}) collective-permute-start(bf16[8,128,512]{2,1,0:T(8,128)(2,1)S(1)} %get-tuple-element.22), channel_id=1, source_target_pairs={{0,1},{1,0},{2,3},{3,2},{4,5},{5,4},{6,7},{7,6},{8,9},{9,8},{10,11... | collective-permute-start | bytes 3145736 | tf_op jit(solution)/shard_map/ppermute | solution.py:256
  113.5 23.2 %copy-start.1 = (bf16[512,512]{1,0:T(8,128)(2,1)S(1)}, bf16[512,512]{1,0:T(8,128)(2,1)}, u32[]{:S(2)}) copy-start(bf16[512,512]{1,0:T(8,128)(2,1)} %weight_ref.2) | copy-start | bytes 1572868
  171.8 12.5 %collective-permute-start.6 = (bf16[1024,256]{1,0:T(8,128)(2,1)S(1)}, bf16[1024,256]{1,0:T(8,128)(2,1)S(1)}, u32[]{:S(2)}, u32[]{:S(2)}) collective-permute-start(bf16[1024,256]{1,0:T(8,128)(2,1)S(1)} %all_gather.23.rest_2_), channel_id=1, source_target_pairs={{240,0},{0,16},{16,32},{32,48},{48,64},{64,80},{80,96},{96,112},{1... | collective-permute-start | bytes 1572872 | tf_op jit(solution)/shard_map/ppermute | solution.py:27
  176.7 10.8 %collective-permute-start.4 = (bf16[1024,256]{1,0:T(8,128)(2,1)S(1)}, bf16[1024,256]{1,0:T(8,128)(2,1)S(1)}, u32[]{:S(2)}, u32[]{:S(2)}) collective-permute-start(bf16[1024,256]{1,0:T(8,128)(2,1)S(1)} %all_gather.23.rest_2_), channel_id=1, source_target_pairs={{16,0},{32,16},{48,32},{64,48},{80,64},{96,80},{112,96},{128,112},... | collective-permute-start | bytes 1572872 | tf_op jit(solution)/shard_map/ppermute | solution.py:27
  184.3 8.8 %collective-permute-start.7 = (bf16[512,256]{1,0:T(8,128)(2,1)S(1)}, bf16[512,256]{1,0:T(8,128)(2,1)S(1)}, u32[]{:S(2)}, u32[]{:S(2)}) collective-permute-start(bf16[512,256]{1,0:T(8,128)(2,1)S(1)} %slice.9), channel_id=1, source_target_pairs={{240,0},{0,16},{16,32},{32,48},{48,64},{64,80},{80,96},{96,112},{1... | collective-permute-start | bytes 786440 | tf_op jit(solution)/shard_map/ppermute | solution.py:27
  187.5 8.9 %collective-permute-start.5 = (bf16[512,256]{1,0:T(8,128)(2,1)S(1)}, bf16[512,256]{1,0:T(8,128)(2,1)S(1)}, u32[]{:S(2)}, u32[]{:S(2)}) collective-permute-start(bf16[512,256]{1,0:T(8,128)(2,1)S(1)} %slice.8), channel_id=1, source_target_pairs={{16,0},{32,16},{48,32},{64,48},{80,64},{96,80},{112,96},{128,112},... | collective-permute-start | bytes 786440 | tf_op jit(solution)/shard_map/ppermute | solution.py:27
  200.9 12.1 %collective-permute-start.8 = (bf16[8,2,128,256]{3,2,1,0:T(8,128)(2,1)S(1)}, bf16[8,2,128,256]{3,2,1,0:T(8,128)(2,1)S(1)}, u32[]{:S(2)}, u32[]{:S(2)}) collective-permute-start(bf16[8,2,128,256]{3,2,1,0:T(8,128)(2,1)S(1)} %get-tuple-element.29), channel_id=1, source_target_pairs={{0,1},{1,0},{2,3},{3,2},{4,5},{5,4},{6,7},{7,6},{8,9},{9,8},{10,11... | collective-permute-start | bytes 3145736 | tf_op jit(solution)/shard_map/ppermute | solution.py:256
  213.3 24.1 %copy-start.2 = (bf16[512,512]{1,0:T(8,128)(2,1)S(1)}, bf16[512,512]{1,0:T(8,128)(2,1)}, u32[]{:S(2)}) copy-start(bf16[512,512]{1,0:T(8,128)(2,1)} %weight_ref.3) | copy-start | bytes 1572868
Sparse Core Ops, SparseCore 0:
  14.3 80.0 all-gather.2

commit v6 on v3

--- a/solution.py
+++ b/solution.py
@@ -19,12 +19,16 @@
 META = 16
 CARRY = BLOCK + 2 * FEAT
 PAY = CARRY + META
-DOM = ("x_lo", "z")
+DOM = ("x_lo", "zq", "zr")
+Z = ("zq", "zr")
 GRID = ("x_hi", "y", "core")
 SIDE = ("x_hi", "y")
+ALL_SIDE = ("x_lo", "x_hi", "y")
 SWAP = [(0, 1), (1, 0)]
-UP = [(z, (z + 1) % 16) for z in range(16)]
-DOWN = [(z, (z + 15) % 16) for z in range(16)]
+
+
+def from_z(value, offset):
+    return lax.ppermute(value, Z, [((z + offset) % 16, z) for z in range(16)])
 
 
 def params(mib):
@@ -75,28 +79,31 @@
     )(cols, counts, feats, hist)
 
 
-def tile_body(n_chunks, stride, with_extra, cols, counts, theirs, spot, own, partner, *rest):
-    chunks = rest[:n_chunks]
-    extras = rest[n_chunks : n_chunks + 2] if with_extra else ()
-    keep, send, panel, adj, sems = rest[-5:]
+def tile_body(second, stride, n_chunks, cols, counts, theirs, spot, *rest):
+    tiles = rest[:2]
+    chunks = rest[2 : 2 + n_chunks]
+    if second:
+        extras = rest[2 + n_chunks : 4 + n_chunks]
+        keep, send, panel, adj, sems, added = rest[-6:]
+    else:
+        keep, send, panel, adj, sems = rest[-5:]
     core = spot[1]
     moves = []
+
+    def move(source, target):
+        moves.append(pltpu.make_async_copy(source, target, sems.at[len(moves)]))
+        moves[-1].start()
+
     start = 0
     for source in chunks:
-        size = source.shape[0]
-        target = panel.at[pl.ds(start, size)]
-        moves.append(pltpu.make_async_copy(source, target, sems.at[len(moves)]))
-        start += size
-    for k, source in enumerate((own, partner)):
+        move(source, panel.at[pl.ds(start, source.shape[0])])
+        start += source.shape[0]
+    for k in range(2):
         for c in range(4):
-            target = adj.at[pl.ds(64 * k + 16 * c, 16)]
-            moves.append(
-                pltpu.make_async_copy(
-                    source.at[pl.ds(16 * c, 16)], target, sems.at[len(moves)]
-                )
-            )
-    for move in moves:
-        move.start()
+            move(tiles[k].at[pl.ds(16 * c, 16)], adj.at[pl.ds(64 * k + 16 * c, 16)])
+    if second:
+        for k in range(2):
+            move(extras[k], added.at[k])
 
     def product(k, row):
         base = (ROWS * k + row) * SLOTS
@@ -107,8 +114,11 @@
             block = adj[base + slot]
             left.append(jnp.where(slot < count, block, jnp.zeros_like(block)))
             col = cols[slot, row] if k == 0 else theirs[row * SLOTS + slot]
-            place = (((col & 15) - spot[3]) & 15) * 2 + (col >> 4)
-            right.append(panel[pl.ds(pl.multiple_of(place * stride, 2 * FEAT), BLOCK), :])
+            z = col & 15
+            ahead = z - spot[3]
+            index = (ahead & 3) * 4 + (z >> 2) if second else ahead & 15
+            start = pl.multiple_of((index * 2 + (col >> 4)) * stride, 2 * FEAT)
+            right.append(panel[pl.ds(start, BLOCK), :])
         return jnp.dot(
             jnp.concatenate(left, axis=1),
             jnp.concatenate(right, axis=0),
@@ -116,52 +126,55 @@
         )
 
     def with_history(k, row, value):
-        start = pl.multiple_of(row * BLOCK, BLOCK)
-        piece = extras[k][pl.ds(start, BLOCK), :].astype(jnp.float32)
+        piece = added[k, row * BLOCK : (row + 1) * BLOCK, :].astype(jnp.float32)
         zero = jnp.zeros_like(piece)
         wide = [jnp.where(spot[2] == group, piece, zero) for group in range(2)]
         return value + jnp.concatenate(wide, axis=1)
 
     def two_rows(k, j):
-        part = spot[0] if k == 0 else 1 - spot[0]
         pair = [product(k, 2 * j + side) for side in range(2)]
-        if with_extra:
+        if second:
             pair = [with_history(k, 2 * j + side, pair[side]) for side in range(2)]
         even, odd = [value.astype(jnp.bfloat16) for value in pair]
-        keep[j, part] = jnp.where(core == 0, even, odd)
-        send[j, part] = jnp.where(core == 0, odd, even)
+        part = spot[0] if k == 0 else 1 - spot[0]
+        where = (part, j) if second else (j, part)
+        keep[where] = jnp.where(core == 0, even, odd)
+        send[where] = jnp.where(core == 0, odd, even)
 
     for n in range(n_chunks):
         moves[n].wait()
     for k in range(2):
         for c in range(4):
             moves[n_chunks + 4 * k + c].wait()
+            if second and c == 0:
+                moves[n_chunks + 8 + k].wait()
             two_rows(k, 2 * c)
             two_rows(k, 2 * c + 1)
 
 
-def tile_product(cols, counts, theirs, spot, own, partner, chunks, extras):
-    operands = [own, partner, *chunks]
-    specs = [pl.BlockSpec(memory_space=pltpu.HBM)] * len(operands)
-    stride = chunks[0].shape[0] // 2
-    for extra in extras:
-        operands.append(extra)
-        specs.append(pl.BlockSpec(extra.shape, lambda i, *_: (0, 0)))
-    half = jax.ShapeDtypeStruct((ROWS // 2, 2, BLOCK, HALF), jnp.bfloat16)
-    out_spec = pl.BlockSpec(half.shape, lambda i, *_: (0, 0, 0, 0))
-    return pl.pallas_call(
-        functools.partial(tile_body, len(chunks), stride, bool(extras)),
+def tile_product(cols, counts, theirs, spot, tiles, chunks, extras):
+    operands = [*tiles, *chunks, *extras]
+    second = bool(extras)
+    stride = sum(chunk.shape[0] for chunk in chunks) // 32
+    shape = (2, ROWS // 2, BLOCK, HALF) if second else (ROWS // 2, 2, BLOCK, HALF)
+    half = jax.ShapeDtypeStruct(shape, jnp.bfloat16)
+    scratch = [
+        pltpu.VMEM((32 * stride, HALF), jnp.bfloat16),
+        pltpu.VMEM((2 * ROWS * SLOTS, BLOCK, BLOCK), jnp.bfloat16),
+        pltpu.SemaphoreType.DMA((len(chunks) + 8 + len(extras),)),
+    ]
+    if second:
+        scratch.append(pltpu.VMEM((2, ROWS * BLOCK, WIDE), jnp.bfloat16))
+    out_spec = pl.BlockSpec(shape, lambda i, *_: (0,) * len(shape))
+    return pl.pallas_call(
+        functools.partial(tile_body, second, stride, len(chunks)),
         out_shape=(half, half),
         grid_spec=pltpu.PrefetchScalarGridSpec(
             num_scalar_prefetch=4,
             grid=(1,),
-            in_specs=specs,
+            in_specs=[pl.BlockSpec(memory_space=pltpu.HBM)] * len(operands),
             out_specs=(out_spec, out_spec),
-            scratch_shapes=[
-                pltpu.VMEM((32 * stride, HALF), jnp.bfloat16),
-                pltpu.VMEM((2 * ROWS * SLOTS, BLOCK, BLOCK), jnp.bfloat16),
-                pltpu.SemaphoreType.DMA((len(chunks) + 8,)),
-            ],
+            scratch_shapes=scratch,
         ),
         compiler_params=params(20),
         name="tile_product",
@@ -287,10 +300,17 @@
     )(spot, halves, weight)
 
 
-def second_dense(halves, weight):
-    def body(halves_ref, weight_ref, out):
-        rows = jnp.concatenate([halves_ref[0], halves_ref[1]], axis=1)
-        value = jnp.dot(rows, weight_ref[...], preferred_element_type=jnp.float32)
+def second_dense(parts, weight):
+    def body(parts_ref, weight_ref, out):
+        halves = []
+        for part in range(2):
+            total = parts_ref[part, 0].astype(jnp.float32)
+            for k in range(1, parts.shape[1]):
+                total = total + parts_ref[part, k].astype(jnp.float32)
+            halves.append(total.astype(jnp.bfloat16))
+        value = jnp.dot(
+            jnp.concatenate(halves, axis=1), weight_ref[...], preferred_element_type=jnp.float32
+        )
         out[...] = value.astype(jnp.bfloat16)
 
     return pl.pallas_call(
@@ -298,27 +318,32 @@
         out_shape=jax.ShapeDtypeStruct((BLOCK, F), jnp.bfloat16),
         compiler_params=params(8),
         name="second_dense",
-    )(halves, weight)
+    )(parts, weight)
 
 
 def gather_ring(chunk):
-    up = [chunk]
-    down = [chunk]
+    ahead = [chunk]
+    behind = [chunk]
     for _ in range(7):
-        up.append(lax.ppermute(up[-1], "z", UP))
-        down.append(lax.ppermute(down[-1], "z", DOWN))
+        ahead.append(from_z(ahead[-1], 1))
+        behind.append(from_z(behind[-1], -1))
     half = chunk.shape[0] // 2
-    far = [
-        lax.ppermute(down[7][:half], "z", DOWN),
-        lax.ppermute(up[7][half:], "z", UP),
-    ]
-    return down + far + up[:0:-1]
-
-
-def reduce_rows(keep, send):
+    across = [from_z(ahead[7][:half], 1), from_z(behind[7][half:], -1)]
+    return [*ahead, *across, *behind[:0:-1]]
+
+
+def gather_quads(chunk):
+    same = lax.all_gather(chunk, "zq", axis=0, tiled=True)
+    above = from_z(same, 1)
+    below = from_z(same, -1)
+    half = same.shape[0] // 2
+    across = [from_z(above[:half], 1), from_z(below[half:], -1)]
+    return [same, above, *across, below]
+
+
+def swap_cores(keep, send):
     other = lax.ppermute(send, "core", SWAP)
-    both = (keep.astype(jnp.float32) + other.astype(jnp.float32)).astype(jnp.bfloat16)
-    return add_parts(lax.all_to_all(both, SIDE, 0, 0, tiled=True))
+    return (keep.astype(jnp.float32) + other.astype(jnp.float32)).astype(jnp.bfloat16)
 
 
 def local(
@@ -341,9 +366,9 @@
     x_hi = lax.axis_index("x_hi")
     grid_index = lax.axis_index(GRID)
     group = jnp.where(x_lo == x_hi, (grid_index // 4) % 2, -1)
-    spot = jnp.stack([x_lo, lax.axis_index("core"), group, lax.axis_index("z")])
+    spot = jnp.stack([x_lo, lax.axis_index("core"), group, lax.axis_index(Z)])
     spot = spot.astype(jnp.int32)
-    hist_spot = jnp.stack([lax.axis_index(DOM), grid_index % 4, lax.axis_index("z")]).astype(jnp.int32)
+    hist_spot = jnp.stack([lax.axis_index(DOM), grid_index % 4, lax.axis_index(Z)]).astype(jnp.int32)
 
     payload = make_payload(
         cols,
@@ -356,28 +381,29 @@
     partner = lax.ppermute(adj_held, "x_lo", SWAP)
     chunks = gather_ring(received[:, :CARRY].reshape(2 * CARRY, HALF))
     chunks = [pltpu.with_memory_space_constraint(chunk, pltpu.HBM) for chunk in chunks]
-    partner = pltpu.with_memory_space_constraint(partner, pltpu.HBM)
     adj = pltpu.with_memory_space_constraint(adj, pltpu.HBM)
     theirs = lax.dynamic_index_in_dim(received[:, CARRY, :80], 1 - x_lo, 0, False)
     theirs = theirs.astype(jnp.int32)
     mine = history_term(hist_list, hist_col[0], hist_row[0], hist_spot, hist_adj[0], chunks)
 
     tables = (cols, counts, theirs, spot)
-    agg = reduce_rows(*tile_product(*tables, adj, partner, chunks, ()))
+    both = swap_cores(*tile_product(*tables, (adj, partner), chunks, ()))
+    agg = add_parts(lax.all_to_all(both, SIDE, 0, 0, tiled=True))
     halves = lax.all_gather(agg, "x_lo", axis=0, tiled=False)
     hidden, chunk = first_dense(halves, w_first, spot)
 
     chunk, mine = lax.optimization_barrier((chunk, mine))
     extras = (mine, lax.ppermute(mine, "x_lo", SWAP))
-    chunks = gather_ring(chunk)
-    agg = reduce_rows(*tile_product(*tables, adj, partner, chunks, extras))
-    embedding = second_dense(lax.all_to_all(agg, "x_lo", 0, 0, tiled=True), w_second)
+    chunks = gather_quads(chunk)
+    both = swap_cores(*tile_product(*tables, (adj, partner), chunks, extras))
+    parts = lax.all_to_all(both.reshape(16, BLOCK, HALF), ALL_SIDE, 0, 0, tiled=True)
+    embedding = second_dense(parts.reshape(2, 8, BLOCK, HALF), w_second)
     return hidden, embedding
 
 
 def solution(mesh):
     fine = Mesh(
-        mesh.devices.reshape(2, 16, 2, 4, 2), ("x_lo", "z", "x_hi", "y", "core")
+        mesh.devices.reshape(2, 4, 4, 2, 4, 2), ("x_lo", "zq", "zr", "x_hi", "y", "core")
     )
     placed = (
         P(DOM + GRID, None),

time: 251 us -> 227 us (0.904)
  starting transfers between devices: 149 us -> 104 us
  blocking collectives: 38.8 us -> 58.5 us
  waiting for transfers between devices: 32.2 us -> 35.2 us
  Pallas kernels: 21.1 us -> 18.2 us
    ppermute x34 -> x22, starting transfers between devices: 137 us -> 92.6 us  [the longest x20 73.8 us: from_z(): return lax.ppermute(value, Z, [((z + offset) % 16, z) for z in range(16)])]
    all_gather x0 -> x1, blocking collectives: none -> 22.6 us  [gather_quads(): same = lax.all_gather(chunk, 'zq', axis=0, tiled=True)]
    ppermute x34 -> x22, waiting for transfers between devices: 22 us -> 27.1 us  [the longest x20 22.5 us: from_z(): return lax.ppermute(value, Z, [((z + offset) % 16, z) for z in range(16)])]
    all_to_all x2 -> x1, blocking collectives: 27 us -> 24 us  [local(): lax.all_to_all(both.reshape(16, BLOCK, HALF), ALL_SIDE, 0, 0, tiled=True)]
    pallas_call x2, Pallas kernels: 12.8 us -> 9.95 us  [tile_product(): pl.pallas_call(functools.partial(tile_body, second, stride, len(chunks)),...]
    unnamed x56 -> x58, local copies, waits for them, and re-layouts: 4.68 us -> 6.48 us
  transfers between devices with their start and end apart: 37 -> 25, of which waited for: 19 -> 15; matrix products, arithmetic and copies ran while one was open for 0% -> 0% of each run, Pallas kernels for 2% -> 2%
where the time goes in v6:
time: 227 us; the launch traced here: 226 us
  starting transfers between devices  104 us (46%)
  blocking collectives  58.5 us (26%)
  waiting for transfers between devices  35.2 us (16%)
  Pallas kernels  18.2 us (8%)
  local copies, waits for them, and re-layouts  6.55 us (3%)
    ppermute x20, starting transfers between devices, from_z(): return lax.ppermute(value, Z, [((z + offset) % 16, z) for z in range(16)])  73.8 us
    all_to_all x1, blocking collectives, local(): lax.all_to_all(both.reshape(16, BLOCK, HALF), ALL_SIDE, 0, 0, tiled=True)  24 us
    all_gather x1, blocking collectives, gather_quads(): same = lax.all_gather(chunk, 'zq', axis=0, tiled=True)  22.6 us
    ppermute x20, waiting for transfers between devices, from_z(): return lax.ppermute(value, Z, [((z + offset) % 16, z) for z in range(16)])  22.5 us
    ppermute x2, starting transfers between devices, swap_cores(): other = lax.ppermute(send, 'core', SWAP)  18.8 us
    pallas_call x2, Pallas kernels, tile_product(): pl.pallas_call(functools.partial(tile_body, second, stride, len(chunks)),...  9.95 us
    all_to_all x1, waiting for transfers between devices, local(): agg = add_parts(lax.all_to_all(both, SIDE, 0, 0, tiled=True))  8.14 us
    all_to_all x1, blocking collectives, local(): received = lax.all_to_all(payload, 'x_lo', 0, 0, tiled=True)  6.87 us
  transfers between devices with their start and end apart: 25, of which 15 were waited for; matrix products, arithmetic and copies ran while one was open for 0% of the time, Pallas kernels for 2%

profile of v6, /device:TPU:1, one launch (start us, length us, event | category | flops | bytes accessed | tf_op | source)
XLA Modules:
  0.0 225.6 jit_solution(7697652756573023178)
XLA Ops:
  3.5 6.9 %all_to_all.15 = bf16[2,208,256]{2,1,0:T(8,128)(2,1)S(1)} all-to-all(bf16[2,208,256]{2,1,0:T(8,128)(2,1)S(1)} %payload.1), channel_id=1, replica_groups=mesh['x_lo'=2,'zq'=4,'zr'=4,'x_hi'=2,'y'=4,'core'=2] {'x_lo'}, dimensions={0} | all-to-all | bytes 425984 | tf_op jit(solution)/shard_map/all_to_all | solution.py:379
  10.3 1.9 collective-permute-start
  12.3 4.0 %collective-permute-start.9 = (bf16[384,256]{1,0:T(8,128)(2,1)S(1)}, bf16[384,256]{1,0:T(8,128)(2,1)S(1)}, u32[]{:S(2)}, u32[]{:S(2)}) collective-permute-start(bf16[384,256]{1,0:T(8,128)(2,1)S(1)} %bitcast.36), channel_id=1, source_target_pairs={{240,0},{0,16},{16,32},{32,48},{48,64},{64,80},{80,96},{96,112},{1... | collective-permute-start | bytes 589832 | tf_op jit(solution)/shard_map/ppermute | solution.py:31
  16.3 9.5 %collective-permute-start.1 = (bf16[384,256]{1,0:T(8,128)(2,1)S(1)}, bf16[384,256]{1,0:T(8,128)(2,1)S(1)}, u32[]{:S(2)}, u32[]{:S(2)}) collective-permute-start(bf16[384,256]{1,0:T(8,128)(2,1)S(1)} %bitcast.37), channel_id=1, source_target_pairs={{16,0},{32,16},{48,32},{64,48},{80,64},{96,80},{112,96},{128,112},... | collective-permute-start | bytes 589832 | tf_op jit(solution)/shard_map/ppermute | solution.py:31
  29.3 4.6 %collective-permute-start.2 = (bf16[384,256]{1,0:T(8,128)(2,1)S(1)}, bf16[384,256]{1,0:T(8,128)(2,1)S(1)}, u32[]{:S(2)}, u32[]{:S(2)}) collective-permute-start(bf16[384,256]{1,0:T(8,128)(2,1)S(1)} %collective-permute-done.1.rest_3_.rest_1_), channel_id=1, source_target_pairs={{16,0},{32,16},{48,32},{64,48},{80,64},{96,80},{112,96},{128,112},... | collective-permute-start | bytes 589832 | tf_op jit(solution)/shard_map/ppermute | solution.py:31
  36.9 4.6 %collective-permute-start.3 = (bf16[384,256]{1,0:T(8,128)(2,1)S(1)}, bf16[384,256]{1,0:T(8,128)(2,1)S(1)}, u32[]{:S(2)}, u32[]{:S(2)}) collective-permute-start(bf16[384,256]{1,0:T(8,128)(2,1)S(1)} %collective-permute-done.2.rest_4_.rest_2_), channel_id=1, source_target_pairs={{16,0},{32,16},{48,32},{64,48},{80,64},{96,80},{112,96},{128,112},... | collective-permute-start | bytes 589832 | tf_op jit(solution)/shard_map/ppermute | solution.py:31
  44.5 4.6 %collective-permute-start.4 = (bf16[384,256]{1,0:T(8,128)(2,1)S(1)}, bf16[384,256]{1,0:T(8,128)(2,1)S(1)}, u32[]{:S(2)}, u32[]{:S(2)}) collective-permute-start(bf16[384,256]{1,0:T(8,128)(2,1)S(1)} %collective-permute-done.3.rest_5_.rest_3_), channel_id=1, source_target_pairs={{16,0},{32,16},{48,32},{64,48},{80,64},{96,80},{112,96},{128,112},... | collective-permute-start | bytes 589832 | tf_op jit(solution)/shard_map/ppermute | solution.py:31
  52.2 4.6 %collective-permute-start.5 = (bf16[384,256]{1,0:T(8,128)(2,1)S(1)}, bf16[384,256]{1,0:T(8,128)(2,1)S(1)}, u32[]{:S(2)}, u32[]{:S(2)}) collective-permute-start(bf16[384,256]{1,0:T(8,128)(2,1)S(1)} %collective-permute-done.4.rest_6_.rest_4_), channel_id=1, source_target_pairs={{16,0},{32,16},{48,32},{64,48},{80,64},{96,80},{112,96},{128,112},... | collective-permute-start | bytes 589832 | tf_op jit(solution)/shard_map/ppermute | solution.py:31
  59.8 4.6 %collective-permute-start.6 = (bf16[384,256]{1,0:T(8,128)(2,1)S(1)}, bf16[384,256]{1,0:T(8,128)(2,1)}, u32[]{:S(2)}, u32[]{:S(2)}) collective-permute-start(bf16[384,256]{1,0:T(8,128)(2,1)S(1)} %collective-permute-done.5.rest_7_.rest_5_), channel_id=1, source_target_pairs={{16,0},{32,16},{48,32},{64,48},{80,64},{96,80},{112,96},{128,112},... | collective-permute-start | bytes 589832 | tf_op jit(solution)/shard_map/ppermute | solution.py:31
  64.4 2.0 collective-permute-done.14.rest_13_.rest_11_
  68.3 4.8 %collective-permute-start.7 = (bf16[384,256]{1,0:T(8,128)(2,1)}, bf16[384,256]{1,0:T(8,128)(2,1)S(1)}, u32[]{:S(2)}, u32[]{:S(2)}) collective-permute-start(bf16[384,256]{1,0:T(8,128)(2,1)} %collective-permute-done.6.rest_8_.rest_6_), channel_id=1, source_target_pairs={{16,0},{32,16},{48,32},{64,48},{80,64},{96,80},{112,96},{128,112},... | collective-permute-start | bytes 589832 | tf_op jit(solution)/shard_map/ppermute | solution.py:31
  73.3 2.4 %collective-permute-done.15.rest_12_.rest_10_ = bf16[384,256]{1,0:T(8,128)(2,1)S(1)} collective-permute-done((bf16[384,256]{1,0:T(8,128)(2,1)}, bf16[384,256]{1,0:T(8,128)(2,1)S(1)}, u32[]{:S(2)}, u32[]{:S(2)}) %collective-permute-start.15) | collective-permute-done | bytes 196640 | tf_op jit(solution)/shard_map/ppermute | solution.py:31
  75.7 1.9 collective-permute-start.16
  77.9 5.1 %collective-permute-start.8 = (bf16[192,256]{1,0:T(8,128)(2,1)S(1)}, bf16[192,256]{1,0:T(8,128)(2,1)S(1)}, u32[]{:S(2)}, u32[]{:S(2)}) collective-permute-start(bf16[192,256]{1,0:T(8,128)(2,1)S(1)} %slice.24), channel_id=1, source_target_pairs={{16,0},{32,16},{48,32},{64,48},{80,64},{96,80},{112,96},{128,112},... | collective-permute-start | bytes 294920 | tf_op jit(solution)/shard_map/ppermute | solution.py:31
  86.6 5.4 %tile_product.2 = (bf16[8,2,128,256]{3,2,1,0:T(8,128)(2,1)S(1)}, bf16[8,2,128,256]{3,2,1,0:T(8,128)(2,1)S(1)}) custom-call(s32[4,16]{1,0:T(4,128)S(1)} %bitcast.25, s32[16]{0:T(128)S(1)} %bitcast.28, s32[80]{0:T(128)S(1)} %bitcast_convert_fusion.theirs, s32[4]{0:T(128)S(1)} %pad_add_fusion.spot.spot_ref, bf16[64,128,128]{2,1,0:T(8,128)(2,1)} %bitcast.33, ...), custom_call_target="tpu_custom_call" | custom-call | tf_op jit(solution)/shard_map/tile_product/pallas_call | solution.py:169
  92.1 12.2 %collective-permute-start.17 = (bf16[8,2,128,256]{3,2,1,0:T(8,128)(2,1)S(1)}, bf16[8,2,128,256]{3,2,1,0:T(8,128)(2,1)S(1)}, u32[]{:S(2)}, u32[]{:S(2)}) collective-permute-start(bf16[8,2,128,256]{3,2,1,0:T(8,128)(2,1)S(1)} %get-tuple-element.15), channel_id=1, source_target_pairs={{0,1},{1,0},{2,3},{3,2},{4,5},{5,4},{6,7},{7,6},{8,9},{9,8},{10,11... | collective-permute-start | bytes 3145736 | tf_op jit(solution)/shard_map/ppermute | solution.py:345
  104.2 2.3 %collective-permute-done.17 = bf16[8,2,128,256]{3,2,1,0:T(8,128)(2,1)S(1)} collective-permute-done((bf16[8,2,128,256]{3,2,1,0:T(8,128)(2,1)S(1)}, bf16[8,2,128,256]{3,2,1,0:T(8,128)(2,1)S(1)}, u32[]{:S(2)}, u32[]{:S(2)}) %collective-permute-start.17) | collective-permute-done | bytes 1048608 | tf_op jit(solution)/shard_map/ppermute | solution.py:345
  107.8 6.5 %all-to-all-start.1 = ((bf16[8,2,128,256]{3,2,1,0:T(8,128)(2,1)}), bf16[8,2,128,256]{3,2,1,0:T(8,128)(2,1)S(1)}, u32[]{:S(2)}, u32[]{:S(2)}) async-start(bf16[8,2,128,256]{3,2,1,0:T(8,128)(2,1)} %add_convert_fusion.1), calls=%async_computation.1 | async-start | bytes 2097152 | tf_op jit(solution)/shard_map/all_to_all | solution.py:391
  115.7 4.2 %history_term.1.rest_7_ = bf16[2048,128]{1,0:T(8,128)(2,1)S(1)} custom-call(s32[32,40]{1,0:T(8,128)S(1)} %copy-done.8, s32[40]{0:T(128)S(1)} %bitcast.30, s32[40]{0:T(128)S(1)} %bitcast.31, s32[3]{0:T(128)S(1)} %pad_add_fusion.1.spot, bf16[40,128,128]{2,1,0:T(8,128)(2,1)S(1)} %bitcast.22, bf16[384,256]{1,0:T(8,128)(2,1)} %bitcast.39, ...), custom_call_target="tpu_custom_call" | custom-call | tf_op jit(solution)/shard_map/history_term/pallas_call | solution.py:231
  120.7 8.1 %all-to-all-done.1.parts_ref = bf16[8,2,128,256]{3,2,1,0:T(8,128)(2,1)S(1)} async-done(((bf16[8,2,128,256]{3,2,1,0:T(8,128)(2,1)}), bf16[8,2,128,256]{3,2,1,0:T(8,128)(2,1)S(1)}, u32[]{:S(2)}, u32[]{:S(2)}) %all-to-all-start.1) | async-done | bytes 1048608 | tf_op jit(solution)/shard_map/all_to_all | solution.py:391
  129.0 5.1 %all-gather = bf16[4,128,256]{2,1,0:T(8,128)(2,1)S(1)} all-gather(bf16[2,128,256]{2,1,0:T(8,128)(2,1)S(1)} %add_parts.1), channel_id=2, replica_groups=mesh['x_lo'=2,'zq'=4,'zr'=4,'x_hi'=2,'y'=4,'core'=2] {'x_lo'}, dimensions={0}, use_global_device_ids=true | all-gather | bytes 393216 | tf_op jit(solution)/shard_map/all_gather | solution.py:392
  136.7 22.6 %all_gather.11.rest_2_ = bf16[1024,256]{1,0:T(8,128)(2,1)S(1)} all-gather(bf16[256,256]{1,0:T(8,128)(2,1)S(1)} %get-tuple-element.18), channel_id=1, replica_groups=mesh['x_lo'=2,'zq'=4,'zr'=4,'x_hi'=2,'y'=4,'core'=2] {'zq'}, dimensions={0}, use_global_device_ids=true | all-gather | bytes 655360 | tf_op jit(solution)/shard_map/all_gather | solution.py:336
  161.1 5.8 %collective-permute-start.18 = (bf16[1024,256]{1,0:T(8,128)(2,1)S(1)}, bf16[1024,256]{1,0:T(8,128)(2,1)S(1)}, u32[]{:S(2)}, u32[]{:S(2)}) collective-permute-start(bf16[1024,256]{1,0:T(8,128)(2,1)S(1)} %all_gather.11.rest_2_), channel_id=1, source_target_pairs={{16,0},{32,16},{48,32},{64,48},{80,64},{96,80},{112,96},{128,112},... | collective-permute-start | bytes 1572872 | tf_op jit(solution)/shard_map/ppermute | solution.py:31
  166.9 3.1 %collective-permute-start.22 = (bf16[2048,128]{1,0:T(8,128)(2,1)S(1)}, bf16[2048,128]{1,0:T(8,128)(2,1)S(1)}, u32[]{:S(2)}, u32[]{:S(2)}) collective-permute-start(bf16[2048,128]{1,0:T(8,128)(2,1)S(1)} %copy-done.1), channel_id=1, source_target_pairs={{0,256},{256,0},{1,257},{257,1},{2,258},{258,2},{3,259},{259,3},{4... | collective-permute-start | bytes 1572872 | tf_op jit(solution)/shard_map/ppermute | solution.py:396
  171.6 3.5 %collective-permute-start.21 = (bf16[512,256]{1,0:T(8,128)(2,1)S(1)}, bf16[512,256]{1,0:T(8,128)(2,1)S(1)}, u32[]{:S(2)}, u32[]{:S(2)}) collective-permute-start(bf16[512,256]{1,0:T(8,128)(2,1)S(1)} %slice.27), channel_id=1, source_target_pairs={{240,0},{0,16},{16,32},{32,48},{48,64},{64,80},{80,96},{96,112},{1... | collective-permute-start | bytes 786440 | tf_op jit(solution)/shard_map/ppermute | solution.py:31
  175.1 3.0 %collective-permute-start.19 = (bf16[512,256]{1,0:T(8,128)(2,1)S(1)}, bf16[512,256]{1,0:T(8,128)(2,1)S(1)}, u32[]{:S(2)}, u32[]{:S(2)}) collective-permute-start(bf16[512,256]{1,0:T(8,128)(2,1)S(1)} %slice.26), channel_id=1, source_target_pairs={{16,0},{32,16},{48,32},{64,48},{80,64},{96,80},{112,96},{128,112},... | collective-permute-start | bytes 786440 | tf_op jit(solution)/shard_map/ppermute | solution.py:31
  178.2 3.1 %collective-permute-done.21.rest_5_ = bf16[512,256]{1,0:T(8,128)(2,1)S(1)} collective-permute-done((bf16[512,256]{1,0:T(8,128)(2,1)S(1)}, bf16[512,256]{1,0:T(8,128)(2,1)S(1)}, u32[]{:S(2)}, u32[]{:S(2)}) %collective-permute-start.21) | collective-permute-done | bytes 262176 | tf_op jit(solution)/shard_map/ppermute | solution.py:31
  181.3 5.7 %collective-permute-done.19.rest_4_ = bf16[512,256]{1,0:T(8,128)(2,1)S(1)} collective-permute-done((bf16[512,256]{1,0:T(8,128)(2,1)S(1)}, bf16[512,256]{1,0:T(8,128)(2,1)S(1)}, u32[]{:S(2)}, u32[]{:S(2)}) %collective-permute-start.19) | collective-permute-done | bytes 262176 | tf_op jit(solution)/shard_map/ppermute | solution.py:31
  187.0 4.5 %tile_product.3 = (bf16[2,8,128,256]{3,2,1,0:T(8,128)(2,1)S(1)}, bf16[2,8,128,256]{3,2,1,0:T(8,128)(2,1)S(1)}) custom-call(s32[4,16]{1,0:T(4,128)S(1)} %bitcast.26, s32[16]{0:T(128)S(1)} %bitcast.29, s32[80]{0:T(128)S(1)} %bitcast_convert_fusion.theirs, s32[4]{0:T(128)S(1)} %pad_add_fusion.spot.spot_ref, bf16[64,128,128]{2,1,0:T(8,128)(2,1)} %bitcast.34, ...), custom_call_target="tpu_custom_call" | custom-call | tf_op jit(solution)/shard_map/tile_product/pallas_call | solution.py:169
  191.5 6.6 %collective-permute-start.23 = (bf16[2,8,128,256]{3,2,1,0:T(8,128)(2,1)S(1)}, bf16[2,8,128,256]{3,2,1,0:T(8,128)(2,1)S(1)}, u32[]{:S(2)}, u32[]{:S(2)}) collective-permute-start(bf16[2,8,128,256]{3,2,1,0:T(8,128)(2,1)S(1)} %get-tuple-element.21), channel_id=1, source_target_pairs={{0,1},{1,0},{2,3},{3,2},{4,5},{5,4},{6,7},{7,6},{8,9},{9,8},{10,11... | collective-permute-start | bytes 3145736 | tf_op jit(solution)/shard_map/ppermute | solution.py:345
  198.1 2.3 %collective-permute-done.23 = bf16[2,8,128,256]{3,2,1,0:T(8,128)(2,1)S(1)} collective-permute-done((bf16[2,8,128,256]{3,2,1,0:T(8,128)(2,1)S(1)}, bf16[2,8,128,256]{3,2,1,0:T(8,128)(2,1)S(1)}, u32[]{:S(2)}, u32[]{:S(2)}) %collective-permute-start.23) | collective-permute-done | bytes 1048608 | tf_op jit(solution)/shard_map/ppermute | solution.py:345
  200.7 24.0 %all_to_all.16 = bf16[16,128,256]{2,1,0:T(8,128)(2,1)S(1)} all-to-all(bf16[16,128,256]{2,1,0:T(8,128)(2,1)S(1)} %bitcast.35), channel_id=1, replica_groups=mesh['x_lo'=2,'zq'=4,'zr'=4,'x_hi'=2,'y'=4,'core'=2] {'x_lo','x_hi','y'}, dimensions={0} | all-to-all | bytes 2097152 | tf_op jit(solution)/shard_map/all_to_all | solution.py:399
  (98 shorter events, 35.2 us)
Async XLA Ops:
  10.3 74.3 %collective-permute-start = (bf16[64,128,128]{2,1,0:T(8,128)(2,1)}, bf16[64,128,128]{2,1,0:T(8,128)(2,1)S(1)}, u32[]{:S(2)}, u32[]{:S(2)}) collective-permute-start(bf16[64,128,128]{2,1,0:T(8,128)(2,1)} %bitcast.32), channel_id=1, source_target_pairs={{0,256},{256,0},{1,257},{257,1},{2,258},{258,2},{3,259},{259,3},{4... | collective-permute-start | bytes 6291464 | tf_op jit(solution)/shard_map/ppermute | solution.py:381
  12.3 72.3 %copy-start.14 = (bf16[2,192,256]{2,1,0:T(8,128)(2,1)}, bf16[2,192,256]{2,1,0:T(8,128)(2,1)S(1)}, u32[]{:S(2)}) copy-start(bf16[2,192,256]{2,1,0:T(8,128)(2,1)S(1)} %slice.19) | copy-start | bytes 589828
  12.3 15.1 %collective-permute-start.9 = (bf16[384,256]{1,0:T(8,128)(2,1)S(1)}, bf16[384,256]{1,0:T(8,128)(2,1)S(1)}, u32[]{:S(2)}, u32[]{:S(2)}) collective-permute-start(bf16[384,256]{1,0:T(8,128)(2,1)S(1)} %bitcast.36), channel_id=1, source_target_pairs={{240,0},{0,16},{16,32},{32,48},{48,64},{64,80},{80,96},{96,112},{1... | collective-permute-start | bytes 589832 | tf_op jit(solution)/shard_map/ppermute | solution.py:31
  16.3 13.0 %collective-permute-start.1 = (bf16[384,256]{1,0:T(8,128)(2,1)S(1)}, bf16[384,256]{1,0:T(8,128)(2,1)S(1)}, u32[]{:S(2)}, u32[]{:S(2)}) collective-permute-start(bf16[384,256]{1,0:T(8,128)(2,1)S(1)} %bitcast.37), channel_id=1, source_target_pairs={{16,0},{32,16},{48,32},{64,48},{80,64},{96,80},{112,96},{128,112},... | collective-permute-start | bytes 589832 | tf_op jit(solution)/shard_map/ppermute | solution.py:31
  27.4 57.3 %copy-start.17 = (bf16[384,256]{1,0:T(8,128)(2,1)}, bf16[384,256]{1,0:T(8,128)(2,1)S(1)}, u32[]{:S(2)}) copy-start(bf16[384,256]{1,0:T(8,128)(2,1)S(1)} %collective-permute-done.9.rest_18_.rest_16_) | copy-start | bytes 589828
  27.4 7.6 %collective-permute-start.10 = (bf16[384,256]{1,0:T(8,128)(2,1)S(1)}, bf16[384,256]{1,0:T(8,128)(2,1)S(1)}, u32[]{:S(2)}, u32[]{:S(2)}) collective-permute-start(bf16[384,256]{1,0:T(8,128)(2,1)S(1)} %collective-permute-done.9.rest_18_.rest_16_), channel_id=1, source_target_pairs={{240,0},{0,16},{16,32},{32,48},{48,64},{64,80},{80,96},{96,112},{1... | collective-permute-start | bytes 589832 | tf_op jit(solution)/shard_map/ppermute | solution.py:31
  29.3 55.3 %copy-start.18 = (bf16[384,256]{1,0:T(8,128)(2,1)}, bf16[384,256]{1,0:T(8,128)(2,1)S(1)}, u32[]{:S(2)}) copy-start(bf16[384,256]{1,0:T(8,128)(2,1)S(1)} %collective-permute-done.1.rest_3_.rest_1_) | copy-start | bytes 589828
  29.3 7.6 %collective-permute-start.2 = (bf16[384,256]{1,0:T(8,128)(2,1)S(1)}, bf16[384,256]{1,0:T(8,128)(2,1)S(1)}, u32[]{:S(2)}, u32[]{:S(2)}) collective-permute-start(bf16[384,256]{1,0:T(8,128)(2,1)S(1)} %collective-permute-done.1.rest_3_.rest_1_), channel_id=1, source_target_pairs={{16,0},{32,16},{48,32},{64,48},{80,64},{96,80},{112,96},{128,112},... | collective-permute-start | bytes 589832 | tf_op jit(solution)/shard_map/ppermute | solution.py:31
  35.0 33.3 %copy-start.19 = (bf16[384,256]{1,0:T(8,128)(2,1)}, bf16[384,256]{1,0:T(8,128)(2,1)S(1)}, u32[]{:S(2)}) copy-start(bf16[384,256]{1,0:T(8,128)(2,1)S(1)} %collective-permute-done.10.rest_17_.rest_15_) | copy-start | bytes 589828
  35.0 7.6 %collective-permute-start.11 = (bf16[384,256]{1,0:T(8,128)(2,1)S(1)}, bf16[384,256]{1,0:T(8,128)(2,1)S(1)}, u32[]{:S(2)}, u32[]{:S(2)}) collective-permute-start(bf16[384,256]{1,0:T(8,128)(2,1)S(1)} %collective-permute-done.10.rest_17_.rest_15_), channel_id=1, source_target_pairs={{240,0},{0,16},{16,32},{32,48},{48,64},{64,80},{80,96},{96,112},{1... | collective-permute-start | bytes 589832 | tf_op jit(solution)/shard_map/ppermute | solution.py:31
  36.9 7.6 %collective-permute-start.3 = (bf16[384,256]{1,0:T(8,128)(2,1)S(1)}, bf16[384,256]{1,0:T(8,128)(2,1)S(1)}, u32[]{:S(2)}, u32[]{:S(2)}) collective-permute-start(bf16[384,256]{1,0:T(8,128)(2,1)S(1)} %collective-permute-done.2.rest_4_.rest_2_), channel_id=1, source_target_pairs={{16,0},{32,16},{48,32},{64,48},{80,64},{96,80},{112,96},{128,112},... | collective-permute-start | bytes 589832 | tf_op jit(solution)/shard_map/ppermute | solution.py:31
  42.6 7.6 %collective-permute-start.12 = (bf16[384,256]{1,0:T(8,128)(2,1)S(1)}, bf16[384,256]{1,0:T(8,128)(2,1)S(1)}, u32[]{:S(2)}, u32[]{:S(2)}) collective-permute-start(bf16[384,256]{1,0:T(8,128)(2,1)S(1)} %collective-permute-done.11.rest_16_.rest_14_), channel_id=1, source_target_pairs={{240,0},{0,16},{16,32},{32,48},{48,64},{64,80},{80,96},{96,112},{1... | collective-permute-start | bytes 589832 | tf_op jit(solution)/shard_map/ppermute | solution.py:31
  44.5 7.6 %collective-permute-start.4 = (bf16[384,256]{1,0:T(8,128)(2,1)S(1)}, bf16[384,256]{1,0:T(8,128)(2,1)S(1)}, u32[]{:S(2)}, u32[]{:S(2)}) collective-permute-start(bf16[384,256]{1,0:T(8,128)(2,1)S(1)} %collective-permute-done.3.rest_5_.rest_3_), channel_id=1, source_target_pairs={{16,0},{32,16},{48,32},{64,48},{80,64},{96,80},{112,96},{128,112},... | collective-permute-start | bytes 589832 | tf_op jit(solution)/shard_map/ppermute | solution.py:31
  50.2 7.6 %collective-permute-start.13 = (bf16[384,256]{1,0:T(8,128)(2,1)S(1)}, bf16[384,256]{1,0:T(8,128)(2,1)S(1)}, u32[]{:S(2)}, u32[]{:S(2)}) collective-permute-start(bf16[384,256]{1,0:T(8,128)(2,1)S(1)} %collective-permute-done.12.rest_15_.rest_13_), channel_id=1, source_target_pairs={{240,0},{0,16},{16,32},{32,48},{48,64},{64,80},{80,96},{96,112},{1... | collective-permute-start | bytes 589832 | tf_op jit(solution)/shard_map/ppermute | solution.py:31
  52.2 7.6 %collective-permute-start.5 = (bf16[384,256]{1,0:T(8,128)(2,1)S(1)}, bf16[384,256]{1,0:T(8,128)(2,1)S(1)}, u32[]{:S(2)}, u32[]{:S(2)}) collective-permute-start(bf16[384,256]{1,0:T(8,128)(2,1)S(1)} %collective-permute-done.4.rest_6_.rest_4_), channel_id=1, source_target_pairs={{16,0},{32,16},{48,32},{64,48},{80,64},{96,80},{112,96},{128,112},... | collective-permute-start | bytes 589832 | tf_op jit(solution)/shard_map/ppermute | solution.py:31
  57.8 8.5 %collective-permute-start.14 = (bf16[384,256]{1,0:T(8,128)(2,1)S(1)}, bf16[384,256]{1,0:T(8,128)(2,1)}, u32[]{:S(2)}, u32[]{:S(2)}) collective-permute-start(bf16[384,256]{1,0:T(8,128)(2,1)S(1)} %collective-permute-done.13.rest_14_.rest_12_), channel_id=1, source_target_pairs={{240,0},{0,16},{16,32},{32,48},{48,64},{64,80},{80,96},{96,112},{1... | collective-permute-start | bytes 589832 | tf_op jit(solution)/shard_map/ppermute | solution.py:31
  59.8 8.5 %collective-permute-start.6 = (bf16[384,256]{1,0:T(8,128)(2,1)S(1)}, bf16[384,256]{1,0:T(8,128)(2,1)}, u32[]{:S(2)}, u32[]{:S(2)}) collective-permute-start(bf16[384,256]{1,0:T(8,128)(2,1)S(1)} %collective-permute-done.5.rest_7_.rest_5_), channel_id=1, source_target_pairs={{16,0},{32,16},{48,32},{64,48},{80,64},{96,80},{112,96},{128,112},... | collective-permute-start | bytes 589832 | tf_op jit(solution)/shard_map/ppermute | solution.py:31
  66.3 9.4 %collective-permute-start.15 = (bf16[384,256]{1,0:T(8,128)(2,1)}, bf16[384,256]{1,0:T(8,128)(2,1)S(1)}, u32[]{:S(2)}, u32[]{:S(2)}) collective-permute-start(bf16[384,256]{1,0:T(8,128)(2,1)} %collective-permute-done.14.rest_13_.rest_11_), channel_id=1, source_target_pairs={{240,0},{0,16},{16,32},{32,48},{48,64},{64,80},{80,96},{96,112},{1... | collective-permute-start | bytes 589832 | tf_op jit(solution)/shard_map/ppermute | solution.py:31
  68.3 9.6 %collective-permute-start.7 = (bf16[384,256]{1,0:T(8,128)(2,1)}, bf16[384,256]{1,0:T(8,128)(2,1)S(1)}, u32[]{:S(2)}, u32[]{:S(2)}) collective-permute-start(bf16[384,256]{1,0:T(8,128)(2,1)} %collective-permute-done.6.rest_8_.rest_6_), channel_id=1, source_target_pairs={{16,0},{32,16},{48,32},{64,48},{80,64},{96,80},{112,96},{128,112},... | collective-permute-start | bytes 589832 | tf_op jit(solution)/shard_map/ppermute | solution.py:31
  75.7 7.3 %collective-permute-start.16 = (bf16[192,256]{1,0:T(8,128)(2,1)S(1)}, bf16[192,256]{1,0:T(8,128)(2,1)S(1)}, u32[]{:S(2)}, u32[]{:S(2)}) collective-permute-start(bf16[192,256]{1,0:T(8,128)(2,1)S(1)} %slice.25), channel_id=1, source_target_pairs={{240,0},{0,16},{16,32},{32,48},{48,64},{64,80},{80,96},{96,112},{1... | collective-permute-start | bytes 294920 | tf_op jit(solution)/shard_map/ppermute | solution.py:31
  77.9 6.7 %collective-permute-start.8 = (bf16[192,256]{1,0:T(8,128)(2,1)S(1)}, bf16[192,256]{1,0:T(8,128)(2,1)S(1)}, u32[]{:S(2)}, u32[]{:S(2)}) collective-permute-start(bf16[192,256]{1,0:T(8,128)(2,1)S(1)} %slice.24), channel_id=1, source_target_pairs={{16,0},{32,16},{48,32},{64,48},{80,64},{96,80},{112,96},{128,112},... | collective-permute-start | bytes 294920 | tf_op jit(solution)/shard_map/ppermute | solution.py:31
  92.1 14.4 %collective-permute-start.17 = (bf16[8,2,128,256]{3,2,1,0:T(8,128)(2,1)S(1)}, bf16[8,2,128,256]{3,2,1,0:T(8,128)(2,1)S(1)}, u32[]{:S(2)}, u32[]{:S(2)}) collective-permute-start(bf16[8,2,128,256]{3,2,1,0:T(8,128)(2,1)S(1)} %get-tuple-element.15), channel_id=1, source_target_pairs={{0,1},{1,0},{2,3},{3,2},{4,5},{5,4},{6,7},{7,6},{8,9},{9,8},{10,11... | collective-permute-start | bytes 3145736 | tf_op jit(solution)/shard_map/ppermute | solution.py:345
  107.8 21.0 %all-to-all-start.1 = ((bf16[8,2,128,256]{3,2,1,0:T(8,128)(2,1)}), bf16[8,2,128,256]{3,2,1,0:T(8,128)(2,1)S(1)}, u32[]{:S(2)}, u32[]{:S(2)}) async-start(bf16[8,2,128,256]{3,2,1,0:T(8,128)(2,1)} %add_convert_fusion.1), calls=%async_computation.1 | async-start | bytes 2097152 | tf_op jit(solution)/shard_map/all_to_all | solution.py:391
  120.7 66.3 %copy-start.7 = (s32[1,1,16,4]{2,3,1,0:T(4,128)S(1)}, s32[1,1,16,4]{2,3,1,0:T(4,128)}, u32[]{:S(2)}) copy-start(s32[1,1,16,4]{2,3,1,0:T(4,128)} %param.13) | copy-start | bytes 772
  120.7 66.3 %copy-start.11 = (s32[1,1,16]{2,1,0:T(1,128)S(1)}, s32[1,1,16]{2,1,0:T(1,128)}, u32[]{:S(2)}) copy-start(s32[1,1,16]{2,1,0:T(1,128)} %param.14) | copy-start | bytes 196
  128.8 38.1 %copy-start.1 = (bf16[2048,128]{1,0:T(8,128)(2,1)S(1)}, bf16[2048,128]{1,0:T(8,128)(2,1)}, u32[]{:S(2)}) copy-start(bf16[2048,128]{1,0:T(8,128)(2,1)} %copy-done) | copy-start | bytes 1572868
  159.2 12.4 %collective-permute-start.20 = (bf16[1024,256]{1,0:T(8,128)(2,1)S(1)}, bf16[1024,256]{1,0:T(8,128)(2,1)S(1)}, u32[]{:S(2)}, u32[]{:S(2)}) collective-permute-start(bf16[1024,256]{1,0:T(8,128)(2,1)S(1)} %all_gather.11.rest_2_), channel_id=1, source_target_pairs={{240,0},{0,16},{16,32},{32,48},{48,64},{64,80},{80,96},{96,112},{1... | collective-permute-start | bytes 1572872 | tf_op jit(solution)/shard_map/ppermute | solution.py:31
  161.1 14.0 %collective-permute-start.18 = (bf16[1024,256]{1,0:T(8,128)(2,1)S(1)}, bf16[1024,256]{1,0:T(8,128)(2,1)S(1)}, u32[]{:S(2)}, u32[]{:S(2)}) collective-permute-start(bf16[1024,256]{1,0:T(8,128)(2,1)S(1)} %all_gather.11.rest_2_), channel_id=1, source_target_pairs={{16,0},{32,16},{48,32},{64,48},{80,64},{96,80},{112,96},{128,112},... | collective-permute-start | bytes 1572872 | tf_op jit(solution)/shard_map/ppermute | solution.py:31
  166.9 11.3 %collective-permute-start.22 = (bf16[2048,128]{1,0:T(8,128)(2,1)S(1)}, bf16[2048,128]{1,0:T(8,128)(2,1)S(1)}, u32[]{:S(2)}, u32[]{:S(2)}) collective-permute-start(bf16[2048,128]{1,0:T(8,128)(2,1)S(1)} %copy-done.1), channel_id=1, source_target_pairs={{0,256},{256,0},{1,257},{257,1},{2,258},{258,2},{3,259},{259,3},{4... | collective-permute-start | bytes 1572872 | tf_op jit(solution)/shard_map/ppermute | solution.py:396
  171.6 9.7 %collective-permute-start.21 = (bf16[512,256]{1,0:T(8,128)(2,1)S(1)}, bf16[512,256]{1,0:T(8,128)(2,1)S(1)}, u32[]{:S(2)}, u32[]{:S(2)}) collective-permute-start(bf16[512,256]{1,0:T(8,128)(2,1)S(1)} %slice.27), channel_id=1, source_target_pairs={{240,0},{0,16},{16,32},{32,48},{48,64},{64,80},{80,96},{96,112},{1... | collective-permute-start | bytes 786440 | tf_op jit(solution)/shard_map/ppermute | solution.py:31
  175.1 11.8 %collective-permute-start.19 = (bf16[512,256]{1,0:T(8,128)(2,1)S(1)}, bf16[512,256]{1,0:T(8,128)(2,1)S(1)}, u32[]{:S(2)}, u32[]{:S(2)}) collective-permute-start(bf16[512,256]{1,0:T(8,128)(2,1)S(1)} %slice.26), channel_id=1, source_target_pairs={{16,0},{32,16},{48,32},{64,48},{80,64},{96,80},{112,96},{128,112},... | collective-permute-start | bytes 786440 | tf_op jit(solution)/shard_map/ppermute | solution.py:31
  191.5 8.9 %collective-permute-start.23 = (bf16[2,8,128,256]{3,2,1,0:T(8,128)(2,1)S(1)}, bf16[2,8,128,256]{3,2,1,0:T(8,128)(2,1)S(1)}, u32[]{:S(2)}, u32[]{:S(2)}) collective-permute-start(bf16[2,8,128,256]{3,2,1,0:T(8,128)(2,1)S(1)} %get-tuple-element.21), channel_id=1, source_target_pairs={{0,1},{1,0},{2,3},{3,2},{4,5},{5,4},{6,7},{7,6},{8,9},{9,8},{10,11... | collective-permute-start | bytes 3145736 | tf_op jit(solution)/shard_map/ppermute | solution.py:345
  (22 other events, 230.0 us)

commit v7 on v6

--- a/solution.py
+++ b/solution.py
@@ -79,7 +79,7 @@
     )(cols, counts, feats, hist)
 
 
-def tile_body(second, stride, n_chunks, cols, counts, theirs, spot, *rest):
+def tile_body(second, stride, n_chunks, numbers, spot, *rest):
     tiles = rest[:2]
     chunks = rest[2 : 2 + n_chunks]
     if second:
@@ -107,16 +107,17 @@
 
     def product(k, row):
         base = (ROWS * k + row) * SLOTS
-        count = counts[row] if k == 0 else theirs[ROWS * SLOTS + row]
+        part = spot[0] if k == 0 else 1 - spot[0]
+        count = numbers[part, ROWS * SLOTS + row]
         left = []
         right = []
         for slot in range(SLOTS):
             block = adj[base + slot]
             left.append(jnp.where(slot < count, block, jnp.zeros_like(block)))
-            col = cols[slot, row] if k == 0 else theirs[row * SLOTS + slot]
+            col = numbers[part, row * SLOTS + slot]
             z = col & 15
             ahead = z - spot[3]
-            index = (ahead & 3) * 4 + (z >> 2) if second else ahead & 15
+            index = (ahead & 3) * 4 + (z >> 2)
             start = pl.multiple_of((index * 2 + (col >> 4)) * stride, 2 * FEAT)
             right.append(panel[pl.ds(start, BLOCK), :])
         return jnp.dot(
@@ -152,7 +153,7 @@
             two_rows(k, 2 * c + 1)
 
 
-def tile_product(cols, counts, theirs, spot, tiles, chunks, extras):
+def tile_product(numbers, spot, tiles, chunks, extras):
     operands = [*tiles, *chunks, *extras]
     second = bool(extras)
     stride = sum(chunk.shape[0] for chunk in chunks) // 32
@@ -170,7 +171,7 @@
         functools.partial(tile_body, second, stride, len(chunks)),
         out_shape=(half, half),
         grid_spec=pltpu.PrefetchScalarGridSpec(
-            num_scalar_prefetch=4,
+            num_scalar_prefetch=2,
             grid=(1,),
             in_specs=[pl.BlockSpec(memory_space=pltpu.HBM)] * len(operands),
             out_specs=(out_spec, out_spec),
@@ -178,7 +179,7 @@
         ),
         compiler_params=params(20),
         name="tile_product",
-    )(cols, counts, theirs, spot, *operands)
+    )(numbers, spot, *operands)
 
 
 def history_body(n_chunks, listed, order, rows, spot, adj, *rest):
@@ -206,7 +207,8 @@
         block = listed[spot[0], order[slot]]
         owner = block >> 2
         piece = block & 3
-        place = (((owner & 15) - spot[2]) & 15) * 2 + (owner >> 4)
+        z = owner & 15
+        place = (((z - spot[2]) & 3) * 4 + (z >> 2)) * 2 + (owner >> 4)
         source = pl.multiple_of(place * (2 * FEAT) + (piece >> 1) * FEAT, FEAT)
         lane = pl.multiple_of((piece & 1) * BLOCK, BLOCK)
         return lax.dot_general(
@@ -319,17 +321,6 @@
         compiler_params=params(8),
         name="second_dense",
     )(parts, weight)
-
-
-def gather_ring(chunk):
-    ahead = [chunk]
-    behind = [chunk]
-    for _ in range(7):
-        ahead.append(from_z(ahead[-1], 1))
-        behind.append(from_z(behind[-1], -1))
-    half = chunk.shape[0] // 2
-    across = [from_z(ahead[7][:half], 1), from_z(behind[7][half:], -1)]
-    return [*ahead, *across, *behind[:0:-1]]
 
 
 def gather_quads(chunk):
@@ -379,14 +370,13 @@
     received = lax.all_to_all(payload, "x_lo", 0, 0, tiled=True)
     adj_held, received = lax.optimization_barrier((adj, received))
     partner = lax.ppermute(adj_held, "x_lo", SWAP)
-    chunks = gather_ring(received[:, :CARRY].reshape(2 * CARRY, HALF))
+    chunks = gather_quads(received[:, :CARRY].reshape(2 * CARRY, HALF))
     chunks = [pltpu.with_memory_space_constraint(chunk, pltpu.HBM) for chunk in chunks]
     adj = pltpu.with_memory_space_constraint(adj, pltpu.HBM)
-    theirs = lax.dynamic_index_in_dim(received[:, CARRY, :80], 1 - x_lo, 0, False)
-    theirs = theirs.astype(jnp.int32)
+    numbers = received[:, CARRY, :80].astype(jnp.int32)
     mine = history_term(hist_list, hist_col[0], hist_row[0], hist_spot, hist_adj[0], chunks)
 
-    tables = (cols, counts, theirs, spot)
+    tables = (numbers, spot)
     both = swap_cores(*tile_product(*tables, (adj, partner), chunks, ()))
     agg = add_parts(lax.all_to_all(both, SIDE, 0, 0, tiled=True))
     halves = lax.all_gather(agg, "x_lo", axis=0, tiled=False)

time: 227 us -> 217 us (0.956)
  starting transfers between devices: 104 us -> 53.5 us
  blocking collectives: 58.5 us -> 97.3 us
  waiting for transfers between devices: 35.2 us -> 37.8 us
    ppermute x20 -> x8, starting transfers between devices: 73.8 us -> 28 us  [from_z(): return lax.ppermute(value, Z, [((z + offset) % 16, z) for z in range(16)])]
    all_gather x1 -> x2, blocking collectives: 22.6 us -> 61 us  [gather_quads(): same = lax.all_gather(chunk, 'zq', axis=0, tiled=True)]
    ppermute x2, starting transfers between devices: 18.8 us -> 14.7 us  [swap_cores(): other = lax.ppermute(send, 'core', SWAP)]
    ppermute x20 -> x8, waiting for transfers between devices: 22.5 us -> 25.1 us  [from_z(): return lax.ppermute(value, Z, [((z + offset) % 16, z) for z in range(16)])]
    unnamed x58 -> x30, local copies, waits for them, and re-layouts: 6.48 us -> 5.42 us
  transfers between devices with their start and end apart: 25 -> 13, of which waited for: 15 -> 9; matrix products, arithmetic and copies ran while one was open for 0% -> 1% of each run, Pallas kernels for 2% -> 2%
where the time goes in v7:
time: 217 us; the launch traced here: 216 us
  blocking collectives  97.3 us (45%)
  starting transfers between devices  53.5 us (25%)
  waiting for transfers between devices  37.8 us (17%)
  Pallas kernels  17.9 us (8%)
  local copies, waits for them, and re-layouts  6.54 us (3%)
    all_gather x2, blocking collectives, gather_quads(): same = lax.all_gather(chunk, 'zq', axis=0, tiled=True)  61 us
    ppermute x8, starting transfers between devices, from_z(): return lax.ppermute(value, Z, [((z + offset) % 16, z) for z in range(16)])  28 us
    ppermute x8, waiting for transfers between devices, from_z(): return lax.ppermute(value, Z, [((z + offset) % 16, z) for z in range(16)])  25.1 us
    all_to_all x1, blocking collectives, local(): lax.all_to_all(both.reshape(16, BLOCK, HALF), ALL_SIDE, 0, 0, tiled=True)  23.6 us
    ppermute x2, starting transfers between devices, swap_cores(): other = lax.ppermute(send, 'core', SWAP)  14.7 us
    pallas_call x2, Pallas kernels, tile_product(): pl.pallas_call(functools.partial(tile_body, second, stride, len(chunks)),...  9.7 us
    all_to_all x1, waiting for transfers between devices, local(): agg = add_parts(lax.all_to_all(both, SIDE, 0, 0, tiled=True))  8.17 us
    all_to_all x1, starting transfers between devices, local(): agg = add_parts(lax.all_to_all(both, SIDE, 0, 0, tiled=True))  6.88 us
  transfers between devices with their start and end apart: 13, of which 9 were waited for; matrix products, arithmetic and copies ran while one was open for 1% of the time, Pallas kernels for 2%

profile of v7, /device:TPU:1, one launch (start us, length us, event | category | flops | bytes accessed | tf_op | source)
XLA Modules:
  0.0 215.7 jit_solution(4246619740585286922)
XLA Ops:
  2.0 1.5 payload.1
  3.5 6.9 %all_to_all.15 = bf16[2,208,256]{2,1,0:T(8,128)(2,1)S(1)} all-to-all(bf16[2,208,256]{2,1,0:T(8,128)(2,1)S(1)} %payload.1), channel_id=1, replica_groups=mesh['x_lo'=2,'zq'=4,'zr'=4,'x_hi'=2,'y'=4,'core'=2] {'x_lo'}, dimensions={0} | all-to-all | bytes 425984 | tf_op jit(solution)/shard_map/all_to_all | solution.py:370
  10.3 1.9 collective-permute-start
  12.3 38.5 %all_gather.12.rest_2_.rest_0_ = bf16[1536,256]{1,0:T(8,128)(2,1)S(1)} all-gather(bf16[384,256]{1,0:T(8,128)(2,1)S(1)} %bitcast.34), channel_id=1, replica_groups=mesh['x_lo'=2,'zq'=4,'zr'=4,'x_hi'=2,'y'=4,'core'=2] {'zq'}, dimensions={0}, use_global_device_ids=true | all-gather | bytes 983040 | tf_op jit(solution)/shard_map/all_gather | solution.py:327
  50.8 2.5 %collective-permute-start.3 = (bf16[1536,256]{1,0:T(8,128)(2,1)S(1)}, bf16[1536,256]{1,0:T(8,128)(2,1)S(1)}, u32[]{:S(2)}, u32[]{:S(2)}) collective-permute-start(bf16[1536,256]{1,0:T(8,128)(2,1)S(1)} %all_gather.12.rest_2_.rest_0_), channel_id=1, source_target_pairs={{240,0},{0,16},{16,32},{32,48},{48,64},{64,80},{80,96},{96,112},{1... | collective-permute-start | bytes 2359304 | tf_op jit(solution)/shard_map/ppermute | solution.py:31
  53.3 4.2 %collective-permute-start.1 = (bf16[1536,256]{1,0:T(8,128)(2,1)S(1)}, bf16[1536,256]{1,0:T(8,128)(2,1)S(1)}, u32[]{:S(2)}, u32[]{:S(2)}) collective-permute-start(bf16[1536,256]{1,0:T(8,128)(2,1)S(1)} %all_gather.12.rest_2_.rest_0_), channel_id=1, source_target_pairs={{16,0},{32,16},{48,32},{64,48},{80,64},{96,80},{112,96},{128,112},... | collective-permute-start | bytes 2359304 | tf_op jit(solution)/shard_map/ppermute | solution.py:31
  57.6 12.7 %collective-permute-done.3.rest_6_.rest_4_ = bf16[1536,256]{1,0:T(8,128)(2,1)S(1)} collective-permute-done((bf16[1536,256]{1,0:T(8,128)(2,1)S(1)}, bf16[1536,256]{1,0:T(8,128)(2,1)S(1)}, u32[]{:S(2)}, u32[]{:S(2)}) %collective-permute-start.3) | collective-permute-done | bytes 786464 | tf_op jit(solution)/shard_map/ppermute | solution.py:31
  70.3 1.9 collective-permute-start.4
  73.3 4.6 %collective-permute-start.2 = (bf16[768,256]{1,0:T(8,128)(2,1)}, bf16[768,256]{1,0:T(8,128)(2,1)S(1)}, u32[]{:S(2)}, u32[]{:S(2)}) collective-permute-start(bf16[768,256]{1,0:T(8,128)(2,1)} %slice.25), channel_id=1, source_target_pairs={{16,0},{32,16},{48,32},{64,48},{80,64},{96,80},{112,96},{128,112},... | collective-permute-start | bytes 1179656 | tf_op jit(solution)/shard_map/ppermute | solution.py:31
  78.2 1.9 collective-permute-done.4.rest_5_.rest_3_
  80.1 2.8 %collective-permute-done.2.rest_4_.rest_2_ = bf16[768,256]{1,0:T(8,128)(2,1)S(1)} collective-permute-done((bf16[768,256]{1,0:T(8,128)(2,1)}, bf16[768,256]{1,0:T(8,128)(2,1)S(1)}, u32[]{:S(2)}, u32[]{:S(2)}) %collective-permute-start.2) | collective-permute-done | bytes 393248 | tf_op jit(solution)/shard_map/ppermute | solution.py:31
  83.7 5.2 %tile_product.2 = (bf16[8,2,128,256]{3,2,1,0:T(8,128)(2,1)S(1)}, bf16[8,2,128,256]{3,2,1,0:T(8,128)(2,1)S(1)}) custom-call(s32[2,80]{1,0:T(2,128)S(1)} %fusion.numbers, s32[4]{0:T(128)S(1)} %pad_add_fusion.spot.spot_ref, bf16[64,128,128]{2,1,0:T(8,128)(2,1)} %bitcast.31, bf16[64,128,128]{2,1,0:T(8,128)(2,1)S(1)} %collective-permute-done.rest_1_, ...), custom_call_target="tpu_custom_call" | custom-call | tf_op jit(solution)/shard_map/tile_product/pallas_call | solution.py:170
  88.9 6.8 %collective-permute-start.5 = (bf16[8,2,128,256]{3,2,1,0:T(8,128)(2,1)S(1)}, bf16[8,2,128,256]{3,2,1,0:T(8,128)(2,1)S(1)}, u32[]{:S(2)}, u32[]{:S(2)}) collective-permute-start(bf16[8,2,128,256]{3,2,1,0:T(8,128)(2,1)S(1)} %get-tuple-element.15), channel_id=1, source_target_pairs={{0,1},{1,0},{2,3},{3,2},{4,5},{5,4},{6,7},{7,6},{8,9},{9,8},{10,11... | collective-permute-start | bytes 3145736 | tf_op jit(solution)/shard_map/ppermute | solution.py:336
  95.7 2.3 %collective-permute-done.5 = bf16[8,2,128,256]{3,2,1,0:T(8,128)(2,1)S(1)} collective-permute-done((bf16[8,2,128,256]{3,2,1,0:T(8,128)(2,1)S(1)}, bf16[8,2,128,256]{3,2,1,0:T(8,128)(2,1)S(1)}, u32[]{:S(2)}, u32[]{:S(2)}) %collective-permute-start.5) | collective-permute-done | bytes 1048608 | tf_op jit(solution)/shard_map/ppermute | solution.py:336
  99.3 6.9 %all-to-all-start.1 = ((bf16[8,2,128,256]{3,2,1,0:T(8,128)(2,1)}), bf16[8,2,128,256]{3,2,1,0:T(8,128)(2,1)S(1)}, u32[]{:S(2)}, u32[]{:S(2)}) async-start(bf16[8,2,128,256]{3,2,1,0:T(8,128)(2,1)} %add_convert_fusion.1), calls=%async_computation.1 | async-start | bytes 2097152 | tf_op jit(solution)/shard_map/all_to_all | solution.py:381
  107.6 4.1 %history_term.1.rest_7_ = bf16[2048,128]{1,0:T(8,128)(2,1)S(1)} custom-call(s32[32,40]{1,0:T(8,128)S(1)} %copy-done.5, s32[40]{0:T(128)S(1)} %bitcast.28, s32[40]{0:T(128)S(1)} %bitcast.29, s32[3]{0:T(128)S(1)} %pad_add_fusion.1.spot, bf16[40,128,128]{2,1,0:T(8,128)(2,1)S(1)} %bitcast.24, bf16[1536,256]{1,0:T(8,128)(2,1)} %copy-done.10, ...), custom_call_target="tpu_custom_call" | custom-call | tf_op jit(solution)/shard_map/history_term/pallas_call | solution.py:233
  112.5 8.2 %all-to-all-done.1.parts_ref = bf16[8,2,128,256]{3,2,1,0:T(8,128)(2,1)S(1)} async-done(((bf16[8,2,128,256]{3,2,1,0:T(8,128)(2,1)}), bf16[8,2,128,256]{3,2,1,0:T(8,128)(2,1)S(1)}, u32[]{:S(2)}, u32[]{:S(2)}) %all-to-all-start.1) | async-done | bytes 1048608 | tf_op jit(solution)/shard_map/all_to_all | solution.py:381
  120.8 5.8 %all-gather = bf16[4,128,256]{2,1,0:T(8,128)(2,1)S(1)} all-gather(bf16[2,128,256]{2,1,0:T(8,128)(2,1)S(1)} %add_parts.1), channel_id=2, replica_groups=mesh['x_lo'=2,'zq'=4,'zr'=4,'x_hi'=2,'y'=4,'core'=2] {'x_lo'}, dimensions={0}, use_global_device_ids=true | all-gather | bytes 393216 | tf_op jit(solution)/shard_map/all_gather | solution.py:382
  127.7 1.5 first_dense.1
  129.2 22.5 %all_gather.15.rest_2_ = bf16[1024,256]{1,0:T(8,128)(2,1)S(1)} all-gather(bf16[256,256]{1,0:T(8,128)(2,1)S(1)} %get-tuple-element.18), channel_id=1, replica_groups=mesh['x_lo'=2,'zq'=4,'zr'=4,'x_hi'=2,'y'=4,'core'=2] {'zq'}, dimensions={0}, use_global_device_ids=true | all-gather | bytes 655360 | tf_op jit(solution)/shard_map/all_gather | solution.py:327
  151.7 1.9 collective-permute-start.8
  153.6 6.4 %collective-permute-start.6 = (bf16[1024,256]{1,0:T(8,128)(2,1)S(1)}, bf16[1024,256]{1,0:T(8,128)(2,1)S(1)}, u32[]{:S(2)}, u32[]{:S(2)}) collective-permute-start(bf16[1024,256]{1,0:T(8,128)(2,1)S(1)} %all_gather.15.rest_2_), channel_id=1, source_target_pairs={{16,0},{32,16},{48,32},{64,48},{80,64},{96,80},{112,96},{128,112},... | collective-permute-start | bytes 1572872 | tf_op jit(solution)/shard_map/ppermute | solution.py:31
  160.0 1.9 collective-permute-start.10
  161.9 4.3 %collective-permute-done.8.rest_6_ = bf16[1024,256]{1,0:T(8,128)(2,1)S(1)} collective-permute-done((bf16[1024,256]{1,0:T(8,128)(2,1)S(1)}, bf16[1024,256]{1,0:T(8,128)(2,1)S(1)}, u32[]{:S(2)}, u32[]{:S(2)}) %collective-permute-start.8) | collective-permute-done | bytes 524320 | tf_op jit(solution)/shard_map/ppermute | solution.py:31
  166.3 1.9 collective-permute-start.9
  168.2 4.6 %collective-permute-start.7 = (bf16[512,256]{1,0:T(8,128)(2,1)S(1)}, bf16[512,256]{1,0:T(8,128)(2,1)S(1)}, u32[]{:S(2)}, u32[]{:S(2)}) collective-permute-start(bf16[512,256]{1,0:T(8,128)(2,1)S(1)} %slice.27), channel_id=1, source_target_pairs={{16,0},{32,16},{48,32},{64,48},{80,64},{96,80},{112,96},{128,112},... | collective-permute-start | bytes 786440 | tf_op jit(solution)/shard_map/ppermute | solution.py:31
  172.8 1.8 collective-permute-done.9.rest_5_
  174.6 1.5 collective-permute-done.7.rest_4_
  176.1 4.5 %tile_product.3 = (bf16[2,8,128,256]{3,2,1,0:T(8,128)(2,1)S(1)}, bf16[2,8,128,256]{3,2,1,0:T(8,128)(2,1)S(1)}) custom-call(s32[2,80]{1,0:T(2,128)S(1)} %fusion.numbers, s32[4]{0:T(128)S(1)} %pad_add_fusion.spot.spot_ref, bf16[64,128,128]{2,1,0:T(8,128)(2,1)} %bitcast.32, bf16[64,128,128]{2,1,0:T(8,128)(2,1)S(1)} %collective-permute-done.rest_1_, ...), custom_call_target="tpu_custom_call" | custom-call | tf_op jit(solution)/shard_map/tile_product/pallas_call | solution.py:170
  180.6 7.9 %collective-permute-start.11 = (bf16[2,8,128,256]{3,2,1,0:T(8,128)(2,1)S(1)}, bf16[2,8,128,256]{3,2,1,0:T(8,128)(2,1)S(1)}, u32[]{:S(2)}, u32[]{:S(2)}) collective-permute-start(bf16[2,8,128,256]{3,2,1,0:T(8,128)(2,1)S(1)} %get-tuple-element.21), channel_id=1, source_target_pairs={{0,1},{1,0},{2,3},{3,2},{4,5},{5,4},{6,7},{7,6},{8,9},{9,8},{10,11... | collective-permute-start | bytes 3145736 | tf_op jit(solution)/shard_map/ppermute | solution.py:336
  188.5 2.3 %collective-permute-done.11 = bf16[2,8,128,256]{3,2,1,0:T(8,128)(2,1)S(1)} collective-permute-done((bf16[2,8,128,256]{3,2,1,0:T(8,128)(2,1)S(1)}, bf16[2,8,128,256]{3,2,1,0:T(8,128)(2,1)S(1)}, u32[]{:S(2)}, u32[]{:S(2)}) %collective-permute-start.11) | collective-permute-done | bytes 1048608 | tf_op jit(solution)/shard_map/ppermute | solution.py:336
  191.1 23.6 %all_to_all.16 = bf16[16,128,256]{2,1,0:T(8,128)(2,1)S(1)} all-to-all(bf16[16,128,256]{2,1,0:T(8,128)(2,1)S(1)} %bitcast.33), channel_id=1, replica_groups=mesh['x_lo'=2,'zq'=4,'zr'=4,'x_hi'=2,'y'=4,'core'=2] {'x_lo','x_hi','y'}, dimensions={0} | all-to-all | bytes 2097152 | tf_op jit(solution)/shard_map/all_to_all | solution.py:389
  (47 shorter events, 9.4 us)
Async XLA Ops:
  0.6 0.7 copy-start.6
  1.3 0.7 copy-start.7
  10.3 72.6 %collective-permute-start = (bf16[64,128,128]{2,1,0:T(8,128)(2,1)}, bf16[64,128,128]{2,1,0:T(8,128)(2,1)S(1)}, u32[]{:S(2)}, u32[]{:S(2)}) collective-permute-start(bf16[64,128,128]{2,1,0:T(8,128)(2,1)} %bitcast.30), channel_id=1, source_target_pairs={{0,256},{256,0},{1,257},{257,1},{2,258},{258,2},{3,259},{259,3},{4... | collective-permute-start | bytes 6291464 | tf_op jit(solution)/shard_map/ppermute | solution.py:372
  50.8 2.5 %copy-start.10 = (bf16[1536,256]{1,0:T(8,128)(2,1)}, bf16[1536,256]{1,0:T(8,128)(2,1)S(1)}, u32[]{:S(2)}) copy-start(bf16[1536,256]{1,0:T(8,128)(2,1)S(1)} %all_gather.12.rest_2_.rest_0_) | copy-start | bytes 2359300
  50.8 19.5 %collective-permute-start.3 = (bf16[1536,256]{1,0:T(8,128)(2,1)S(1)}, bf16[1536,256]{1,0:T(8,128)(2,1)S(1)}, u32[]{:S(2)}, u32[]{:S(2)}) collective-permute-start(bf16[1536,256]{1,0:T(8,128)(2,1)S(1)} %all_gather.12.rest_2_.rest_0_), channel_id=1, source_target_pairs={{240,0},{0,16},{16,32},{32,48},{48,64},{64,80},{80,96},{96,112},{1... | collective-permute-start | bytes 2359304 | tf_op jit(solution)/shard_map/ppermute | solution.py:31
  53.3 19.0 %collective-permute-start.1 = (bf16[1536,256]{1,0:T(8,128)(2,1)S(1)}, bf16[1536,256]{1,0:T(8,128)(2,1)S(1)}, u32[]{:S(2)}, u32[]{:S(2)}) collective-permute-start(bf16[1536,256]{1,0:T(8,128)(2,1)S(1)} %all_gather.12.rest_2_.rest_0_), channel_id=1, source_target_pairs={{16,0},{32,16},{48,32},{64,48},{80,64},{96,80},{112,96},{128,112},... | collective-permute-start | bytes 2359304 | tf_op jit(solution)/shard_map/ppermute | solution.py:31
  70.3 2.0 copy-start.11
  70.3 9.7 %collective-permute-start.4 = (bf16[768,256]{1,0:T(8,128)(2,1)S(1)}, bf16[768,256]{1,0:T(8,128)(2,1)S(1)}, u32[]{:S(2)}, u32[]{:S(2)}) collective-permute-start(bf16[768,256]{1,0:T(8,128)(2,1)S(1)} %slice.26), channel_id=1, source_target_pairs={{240,0},{0,16},{16,32},{32,48},{48,64},{64,80},{80,96},{96,112},{1... | collective-permute-start | bytes 1179656 | tf_op jit(solution)/shard_map/ppermute | solution.py:31
  72.3 1.0 copy-start.12
  73.3 9.6 %collective-permute-start.2 = (bf16[768,256]{1,0:T(8,128)(2,1)}, bf16[768,256]{1,0:T(8,128)(2,1)S(1)}, u32[]{:S(2)}, u32[]{:S(2)}) collective-permute-start(bf16[768,256]{1,0:T(8,128)(2,1)} %slice.25), channel_id=1, source_target_pairs={{16,0},{32,16},{48,32},{64,48},{80,64},{96,80},{112,96},{128,112},... | collective-permute-start | bytes 1179656 | tf_op jit(solution)/shard_map/ppermute | solution.py:31
  80.1 2.9 %copy-start.13 = (bf16[768,256]{1,0:T(8,128)(2,1)}, bf16[768,256]{1,0:T(8,128)(2,1)S(1)}, u32[]{:S(2)}) copy-start(bf16[768,256]{1,0:T(8,128)(2,1)S(1)} %collective-permute-done.4.rest_5_.rest_3_) | copy-start | bytes 1179652
  82.9 0.7 copy-start.14
  88.9 9.1 %collective-permute-start.5 = (bf16[8,2,128,256]{3,2,1,0:T(8,128)(2,1)S(1)}, bf16[8,2,128,256]{3,2,1,0:T(8,128)(2,1)S(1)}, u32[]{:S(2)}, u32[]{:S(2)}) collective-permute-start(bf16[8,2,128,256]{3,2,1,0:T(8,128)(2,1)S(1)} %get-tuple-element.15), channel_id=1, source_target_pairs={{0,1},{1,0},{2,3},{3,2},{4,5},{5,4},{6,7},{7,6},{8,9},{9,8},{10,11... | collective-permute-start | bytes 3145736 | tf_op jit(solution)/shard_map/ppermute | solution.py:336
  98.0 8.3 %copy-start.5 = (s32[32,40]{1,0:T(8,128)S(1)}, s32[32,40]{1,0:T(8,128)}, u32[]{:S(2)}) copy-start(s32[32,40]{1,0:T(8,128)} %listed.1) | copy-start | bytes 15364
  98.0 8.3 %copy-start.8 = (s32[1,40]{1,0:T(1,128)S(1)}, s32[1,40]{1,0:T(1,128)}, u32[]{:S(2)}) copy-start(s32[1,40]{1,0:T(1,128)} %param.19) | copy-start | bytes 484
  98.0 8.3 %copy-start.9 = (s32[1,40]{1,0:T(1,128)S(1)}, s32[1,40]{1,0:T(1,128)}, u32[]{:S(2)}) copy-start(s32[1,40]{1,0:T(1,128)} %param.18) | copy-start | bytes 484
  99.3 21.4 %all-to-all-start.1 = ((bf16[8,2,128,256]{3,2,1,0:T(8,128)(2,1)}), bf16[8,2,128,256]{3,2,1,0:T(8,128)(2,1)S(1)}, u32[]{:S(2)}, u32[]{:S(2)}) async-start(bf16[8,2,128,256]{3,2,1,0:T(8,128)(2,1)} %add_convert_fusion.1), calls=%async_computation.1 | async-start | bytes 2097152 | tf_op jit(solution)/shard_map/all_to_all | solution.py:381
  106.3 1.3 copy-start.2
  111.7 0.8 copy-start
  120.7 39.3 %copy-start.1 = (bf16[2048,128]{1,0:T(8,128)(2,1)S(1)}, bf16[2048,128]{1,0:T(8,128)(2,1)}, u32[]{:S(2)}) copy-start(bf16[2048,128]{1,0:T(8,128)(2,1)} %copy-done) | copy-start | bytes 1572868
  126.6 1.0 copy-start.3
  151.7 14.6 %collective-permute-start.8 = (bf16[1024,256]{1,0:T(8,128)(2,1)S(1)}, bf16[1024,256]{1,0:T(8,128)(2,1)S(1)}, u32[]{:S(2)}, u32[]{:S(2)}) collective-permute-start(bf16[1024,256]{1,0:T(8,128)(2,1)S(1)} %all_gather.15.rest_2_), channel_id=1, source_target_pairs={{240,0},{0,16},{16,32},{32,48},{48,64},{64,80},{80,96},{96,112},{1... | collective-permute-start | bytes 1572872 | tf_op jit(solution)/shard_map/ppermute | solution.py:31
  153.6 14.6 %collective-permute-start.6 = (bf16[1024,256]{1,0:T(8,128)(2,1)S(1)}, bf16[1024,256]{1,0:T(8,128)(2,1)S(1)}, u32[]{:S(2)}, u32[]{:S(2)}) collective-permute-start(bf16[1024,256]{1,0:T(8,128)(2,1)S(1)} %all_gather.15.rest_2_), channel_id=1, source_target_pairs={{16,0},{32,16},{48,32},{64,48},{80,64},{96,80},{112,96},{128,112},... | collective-permute-start | bytes 1572872 | tf_op jit(solution)/shard_map/ppermute | solution.py:31
  160.0 12.8 %collective-permute-start.10 = (bf16[2048,128]{1,0:T(8,128)(2,1)S(1)}, bf16[2048,128]{1,0:T(8,128)(2,1)S(1)}, u32[]{:S(2)}, u32[]{:S(2)}) collective-permute-start(bf16[2048,128]{1,0:T(8,128)(2,1)S(1)} %copy-done.1), channel_id=1, source_target_pairs={{0,256},{256,0},{1,257},{257,1},{2,258},{258,2},{3,259},{259,3},{4... | collective-permute-start | bytes 1572872 | tf_op jit(solution)/shard_map/ppermute | solution.py:386
  166.3 8.3 %collective-permute-start.9 = (bf16[512,256]{1,0:T(8,128)(2,1)S(1)}, bf16[512,256]{1,0:T(8,128)(2,1)S(1)}, u32[]{:S(2)}, u32[]{:S(2)}) collective-permute-start(bf16[512,256]{1,0:T(8,128)(2,1)S(1)} %slice.28), channel_id=1, source_target_pairs={{240,0},{0,16},{16,32},{32,48},{48,64},{64,80},{80,96},{96,112},{1... | collective-permute-start | bytes 786440 | tf_op jit(solution)/shard_map/ppermute | solution.py:31
  168.2 7.9 %collective-permute-start.7 = (bf16[512,256]{1,0:T(8,128)(2,1)S(1)}, bf16[512,256]{1,0:T(8,128)(2,1)S(1)}, u32[]{:S(2)}, u32[]{:S(2)}) collective-permute-start(bf16[512,256]{1,0:T(8,128)(2,1)S(1)} %slice.27), channel_id=1, source_target_pairs={{16,0},{32,16},{48,32},{64,48},{80,64},{96,80},{112,96},{128,112},... | collective-permute-start | bytes 786440 | tf_op jit(solution)/shard_map/ppermute | solution.py:31
  180.6 10.2 %collective-permute-start.11 = (bf16[2,8,128,256]{3,2,1,0:T(8,128)(2,1)S(1)}, bf16[2,8,128,256]{3,2,1,0:T(8,128)(2,1)S(1)}, u32[]{:S(2)}, u32[]{:S(2)}) collective-permute-start(bf16[2,8,128,256]{3,2,1,0:T(8,128)(2,1)S(1)} %get-tuple-element.21), channel_id=1, source_target_pairs={{0,1},{1,0},{2,3},{3,2},{4,5},{5,4},{6,7},{7,6},{8,9},{9,8},{10,11... | collective-permute-start | bytes 3145736 | tf_op jit(solution)/shard_map/ppermute | solution.py:336
  190.8 24.0 %copy-start.4 = (bf16[512,512]{1,0:T(8,128)(2,1)S(1)}, bf16[512,512]{1,0:T(8,128)(2,1)}, u32[]{:S(2)}) copy-start(bf16[512,512]{1,0:T(8,128)(2,1)} %weight_ref.3) | copy-start | bytes 1572868

commit v8 on v7

--- a/solution.py
+++ b/solution.py
@@ -351,8 +351,8 @@
     w_second,
 ):
     adj = adj_vals[0, 0].reshape(ROWS * SLOTS, BLOCK, BLOCK)
-    cols = adj_col[0, 0].T
-    counts = adj_count[0, 0]
+    cols = pltpu.with_memory_space_constraint(adj_col[0, 0].T, pltpu.HBM)
+    counts = pltpu.with_memory_space_constraint(adj_count[0, 0], pltpu.HBM)
     x_lo = lax.axis_index("x_lo")
     x_hi = lax.axis_index("x_hi")
     grid_index = lax.axis_index(GRID)
@@ -380,7 +380,9 @@
     both = swap_cores(*tile_product(*tables, (adj, partner), chunks, ()))
     agg = add_parts(lax.all_to_all(both, SIDE, 0, 0, tiled=True))
     halves = lax.all_gather(agg, "x_lo", axis=0, tiled=False)
-    hidden, chunk = first_dense(halves, w_first, spot)
+    hidden, chunk = first_dense(
+        halves, pltpu.with_memory_space_constraint(w_first, pltpu.HBM), spot
+    )
 
     chunk, mine = lax.optimization_barrier((chunk, mine))
     extras = (mine, lax.ppermute(mine, "x_lo", SWAP))

time: 217 us -> 215 us (level)
  local copies, waits for them, and re-layouts: 6.54 us -> 4.12 us
    unnamed x30 -> x24, local copies, waits for them, and re-layouts: 5.42 us -> 3.05 us
where the time goes in v8:
time: 215 us; the launch traced here: 214 us
  blocking collectives  96.9 us (45%)
  starting transfers between devices  53.7 us (25%)
  waiting for transfers between devices  37.7 us (18%)
  Pallas kernels  19.1 us (9%)
  local copies, waits for them, and re-layouts  4.12 us (2%)
    all_gather x2, blocking collectives, gather_quads(): same = lax.all_gather(chunk, 'zq', axis=0, tiled=True)  61 us
    ppermute x8, starting transfers between devices, from_z(): return lax.ppermute(value, Z, [((z + offset) % 16, z) for z in range(16)])  28.1 us
    ppermute x8, waiting for transfers between devices, from_z(): return lax.ppermute(value, Z, [((z + offset) % 16, z) for z in range(16)])  25 us
    all_to_all x1, blocking collectives, local(): lax.all_to_all(both.reshape(16, BLOCK, HALF), ALL_SIDE, 0, 0, tiled=True)  23.3 us
    ppermute x2, starting transfers between devices, swap_cores(): other = lax.ppermute(send, 'core', SWAP)  14.9 us
    pallas_call x2, Pallas kernels, tile_product(): pl.pallas_call(functools.partial(tile_body, second, stride, len(chunks)),...  9.7 us
    all_to_all x1, waiting for transfers between devices, local(): agg = add_parts(lax.all_to_all(both, SIDE, 0, 0, tiled=True))  8.2 us
    all_to_all x1, blocking collectives, local(): received = lax.all_to_all(payload, 'x_lo', 0, 0, tiled=True)  6.87 us
  transfers between devices with their start and end apart: 13, of which 9 were waited for; matrix products, arithmetic and copies ran while one was open for 1% of the time, Pallas kernels for 2%

profile of v8, /device:TPU:1, one launch (start us, length us, event | category | flops | bytes accessed | tf_op | source)
XLA Modules:
  0.0 214.3 jit_solution(7047138611750591911)
XLA Ops:
  0.6 1.6 payload.1
  2.3 6.9 %all_to_all.15 = bf16[2,208,256]{2,1,0:T(8,128)(2,1)S(1)} all-to-all(bf16[2,208,256]{2,1,0:T(8,128)(2,1)S(1)} %payload.1), channel_id=1, replica_groups=mesh['x_lo'=2,'zq'=4,'zr'=4,'x_hi'=2,'y'=4,'core'=2] {'x_lo'}, dimensions={0} | all-to-all | bytes 425984 | tf_op jit(solution)/shard_map/all_to_all | solution.py:370
  9.1 1.9 collective-permute-start
  11.1 38.5 %all_gather.12.rest_2_.rest_0_ = bf16[1536,256]{1,0:T(8,128)(2,1)S(1)} all-gather(bf16[384,256]{1,0:T(8,128)(2,1)S(1)} %bitcast.32), channel_id=1, replica_groups=mesh['x_lo'=2,'zq'=4,'zr'=4,'x_hi'=2,'y'=4,'core'=2] {'zq'}, dimensions={0}, use_global_device_ids=true | all-gather | bytes 983040 | tf_op jit(solution)/shard_map/all_gather | solution.py:327
  49.6 2.5 %collective-permute-start.3 = (bf16[1536,256]{1,0:T(8,128)(2,1)S(1)}, bf16[1536,256]{1,0:T(8,128)(2,1)S(1)}, u32[]{:S(2)}, u32[]{:S(2)}) collective-permute-start(bf16[1536,256]{1,0:T(8,128)(2,1)S(1)} %all_gather.12.rest_2_.rest_0_), channel_id=1, source_target_pairs={{240,0},{0,16},{16,32},{32,48},{48,64},{64,80},{80,96},{96,112},{1... | collective-permute-start | bytes 2359304 | tf_op jit(solution)/shard_map/ppermute | solution.py:31
  52.1 4.2 %collective-permute-start.1 = (bf16[1536,256]{1,0:T(8,128)(2,1)S(1)}, bf16[1536,256]{1,0:T(8,128)(2,1)S(1)}, u32[]{:S(2)}, u32[]{:S(2)}) collective-permute-start(bf16[1536,256]{1,0:T(8,128)(2,1)S(1)} %all_gather.12.rest_2_.rest_0_), channel_id=1, source_target_pairs={{16,0},{32,16},{48,32},{64,48},{80,64},{96,80},{112,96},{128,112},... | collective-permute-start | bytes 2359304 | tf_op jit(solution)/shard_map/ppermute | solution.py:31
  56.4 12.7 %collective-permute-done.3.rest_6_.rest_4_ = bf16[1536,256]{1,0:T(8,128)(2,1)S(1)} collective-permute-done((bf16[1536,256]{1,0:T(8,128)(2,1)S(1)}, bf16[1536,256]{1,0:T(8,128)(2,1)S(1)}, u32[]{:S(2)}, u32[]{:S(2)}) %collective-permute-start.3) | collective-permute-done | bytes 786464 | tf_op jit(solution)/shard_map/ppermute | solution.py:31
  69.1 1.9 collective-permute-start.4
  72.1 4.6 %collective-permute-start.2 = (bf16[768,256]{1,0:T(8,128)(2,1)}, bf16[768,256]{1,0:T(8,128)(2,1)S(1)}, u32[]{:S(2)}, u32[]{:S(2)}) collective-permute-start(bf16[768,256]{1,0:T(8,128)(2,1)} %slice.25), channel_id=1, source_target_pairs={{16,0},{32,16},{48,32},{64,48},{80,64},{96,80},{112,96},{128,112},... | collective-permute-start | bytes 1179656 | tf_op jit(solution)/shard_map/ppermute | solution.py:31
  77.0 1.9 collective-permute-done.4.rest_5_.rest_3_
  78.9 2.8 %collective-permute-done.2.rest_4_.rest_2_ = bf16[768,256]{1,0:T(8,128)(2,1)S(1)} collective-permute-done((bf16[768,256]{1,0:T(8,128)(2,1)}, bf16[768,256]{1,0:T(8,128)(2,1)S(1)}, u32[]{:S(2)}, u32[]{:S(2)}) %collective-permute-start.2) | collective-permute-done | bytes 393248 | tf_op jit(solution)/shard_map/ppermute | solution.py:31
  82.4 5.2 %tile_product.2 = (bf16[8,2,128,256]{3,2,1,0:T(8,128)(2,1)S(1)}, bf16[8,2,128,256]{3,2,1,0:T(8,128)(2,1)S(1)}) custom-call(s32[2,80]{1,0:T(2,128)S(1)} %fusion.numbers, s32[4]{0:T(128)S(1)} %pad_add_fusion.spot.spot_ref, bf16[64,128,128]{2,1,0:T(8,128)(2,1)} %bitcast.29, bf16[64,128,128]{2,1,0:T(8,128)(2,1)S(1)} %collective-permute-done.rest_1_, ...), custom_call_target="tpu_custom_call" | custom-call | tf_op jit(solution)/shard_map/tile_product/pallas_call | solution.py:170
  87.6 6.9 %collective-permute-start.5 = (bf16[8,2,128,256]{3,2,1,0:T(8,128)(2,1)S(1)}, bf16[8,2,128,256]{3,2,1,0:T(8,128)(2,1)S(1)}, u32[]{:S(2)}, u32[]{:S(2)}) collective-permute-start(bf16[8,2,128,256]{3,2,1,0:T(8,128)(2,1)S(1)} %get-tuple-element.15), channel_id=1, source_target_pairs={{0,1},{1,0},{2,3},{3,2},{4,5},{5,4},{6,7},{7,6},{8,9},{9,8},{10,11... | collective-permute-start | bytes 3145736 | tf_op jit(solution)/shard_map/ppermute | solution.py:336
  94.5 2.3 %collective-permute-done.5 = bf16[8,2,128,256]{3,2,1,0:T(8,128)(2,1)S(1)} collective-permute-done((bf16[8,2,128,256]{3,2,1,0:T(8,128)(2,1)S(1)}, bf16[8,2,128,256]{3,2,1,0:T(8,128)(2,1)S(1)}, u32[]{:S(2)}, u32[]{:S(2)}) %collective-permute-start.5) | collective-permute-done | bytes 1048608 | tf_op jit(solution)/shard_map/ppermute | solution.py:336
  98.1 6.9 %all-to-all-start.1 = ((bf16[8,2,128,256]{3,2,1,0:T(8,128)(2,1)}), bf16[8,2,128,256]{3,2,1,0:T(8,128)(2,1)S(1)}, u32[]{:S(2)}, u32[]{:S(2)}) async-start(bf16[8,2,128,256]{3,2,1,0:T(8,128)(2,1)} %add_convert_fusion.1), calls=%async_computation.1 | async-start | bytes 2097152 | tf_op jit(solution)/shard_map/all_to_all | solution.py:381
  106.4 4.1 %history_term.1.rest_7_ = bf16[2048,128]{1,0:T(8,128)(2,1)S(1)} custom-call(s32[32,40]{1,0:T(8,128)S(1)} %copy-done.4, s32[40]{0:T(128)S(1)} %bitcast.26, s32[40]{0:T(128)S(1)} %bitcast.27, s32[3]{0:T(128)S(1)} %pad_add_fusion.1.spot, bf16[40,128,128]{2,1,0:T(8,128)(2,1)S(1)} %bitcast.24, bf16[1536,256]{1,0:T(8,128)(2,1)} %copy-done.7, ...), custom_call_target="tpu_custom_call" | custom-call | tf_op jit(solution)/shard_map/history_term/pallas_call | solution.py:233
  111.3 8.2 %all-to-all-done.1.parts_ref = bf16[8,2,128,256]{3,2,1,0:T(8,128)(2,1)S(1)} async-done(((bf16[8,2,128,256]{3,2,1,0:T(8,128)(2,1)}), bf16[8,2,128,256]{3,2,1,0:T(8,128)(2,1)S(1)}, u32[]{:S(2)}, u32[]{:S(2)}) %all-to-all-start.1) | async-done | bytes 1048608 | tf_op jit(solution)/shard_map/all_to_all | solution.py:381
  119.6 5.8 %all-gather = bf16[4,128,256]{2,1,0:T(8,128)(2,1)S(1)} all-gather(bf16[2,128,256]{2,1,0:T(8,128)(2,1)S(1)} %add_parts.1), channel_id=2, replica_groups=mesh['x_lo'=2,'zq'=4,'zr'=4,'x_hi'=2,'y'=4,'core'=2] {'x_lo'}, dimensions={0}, use_global_device_ids=true | all-gather | bytes 393216 | tf_op jit(solution)/shard_map/all_gather | solution.py:382
  125.4 2.5 %first_dense.1 = (bf16[128,512]{1,0:T(8,128)(2,1)}, bf16[256,256]{1,0:T(8,128)(2,1)S(1)}) custom-call(s32[4]{0:T(128)S(1)} %pad_add_fusion.spot.spot_ref, bf16[2,2,128,256]{3,2,1,0:T(8,128)(2,1)S(1)} %bitcast.25, bf16[512,512]{1,0:T(8,128)(2,1)} %weight_ref.2), custom_call_target="tpu_custom_call" | custom-call | tf_op jit(solution)/shard_map/first_dense/pallas_call | solution.py:282
  128.0 22.5 %all_gather.15.rest_2_ = bf16[1024,256]{1,0:T(8,128)(2,1)S(1)} all-gather(bf16[256,256]{1,0:T(8,128)(2,1)S(1)} %get-tuple-element.18), channel_id=1, replica_groups=mesh['x_lo'=2,'zq'=4,'zr'=4,'x_hi'=2,'y'=4,'core'=2] {'zq'}, dimensions={0}, use_global_device_ids=true | all-gather | bytes 655360 | tf_op jit(solution)/shard_map/all_gather | solution.py:327
  150.4 1.9 collective-permute-start.8
  152.3 6.5 %collective-permute-start.6 = (bf16[1024,256]{1,0:T(8,128)(2,1)S(1)}, bf16[1024,256]{1,0:T(8,128)(2,1)S(1)}, u32[]{:S(2)}, u32[]{:S(2)}) collective-permute-start(bf16[1024,256]{1,0:T(8,128)(2,1)S(1)} %all_gather.15.rest_2_), channel_id=1, source_target_pairs={{16,0},{32,16},{48,32},{64,48},{80,64},{96,80},{112,96},{128,112},... | collective-permute-start | bytes 1572872 | tf_op jit(solution)/shard_map/ppermute | solution.py:31
  158.8 1.9 collective-permute-start.10
  160.8 4.2 %collective-permute-done.8.rest_6_ = bf16[1024,256]{1,0:T(8,128)(2,1)S(1)} collective-permute-done((bf16[1024,256]{1,0:T(8,128)(2,1)S(1)}, bf16[1024,256]{1,0:T(8,128)(2,1)S(1)}, u32[]{:S(2)}, u32[]{:S(2)}) %collective-permute-start.8) | collective-permute-done | bytes 524320 | tf_op jit(solution)/shard_map/ppermute | solution.py:31
  165.0 1.9 collective-permute-start.9
  167.0 4.6 %collective-permute-start.7 = (bf16[512,256]{1,0:T(8,128)(2,1)S(1)}, bf16[512,256]{1,0:T(8,128)(2,1)S(1)}, u32[]{:S(2)}, u32[]{:S(2)}) collective-permute-start(bf16[512,256]{1,0:T(8,128)(2,1)S(1)} %slice.27), channel_id=1, source_target_pairs={{16,0},{32,16},{48,32},{64,48},{80,64},{96,80},{112,96},{128,112},... | collective-permute-start | bytes 786440 | tf_op jit(solution)/shard_map/ppermute | solution.py:31
  171.6 1.8 collective-permute-done.9.rest_5_
  173.4 1.5 collective-permute-done.7.rest_4_
  174.9 4.5 %tile_product.3 = (bf16[2,8,128,256]{3,2,1,0:T(8,128)(2,1)S(1)}, bf16[2,8,128,256]{3,2,1,0:T(8,128)(2,1)S(1)}) custom-call(s32[2,80]{1,0:T(2,128)S(1)} %fusion.numbers, s32[4]{0:T(128)S(1)} %pad_add_fusion.spot.spot_ref, bf16[64,128,128]{2,1,0:T(8,128)(2,1)} %bitcast.30, bf16[64,128,128]{2,1,0:T(8,128)(2,1)S(1)} %collective-permute-done.rest_1_, ...), custom_call_target="tpu_custom_call" | custom-call | tf_op jit(solution)/shard_map/tile_product/pallas_call | solution.py:170
  179.4 8.1 %collective-permute-start.11 = (bf16[2,8,128,256]{3,2,1,0:T(8,128)(2,1)S(1)}, bf16[2,8,128,256]{3,2,1,0:T(8,128)(2,1)S(1)}, u32[]{:S(2)}, u32[]{:S(2)}) collective-permute-start(bf16[2,8,128,256]{3,2,1,0:T(8,128)(2,1)S(1)} %get-tuple-element.21), channel_id=1, source_target_pairs={{0,1},{1,0},{2,3},{3,2},{4,5},{5,4},{6,7},{7,6},{8,9},{9,8},{10,11... | collective-permute-start | bytes 3145736 | tf_op jit(solution)/shard_map/ppermute | solution.py:336
  187.5 2.3 %collective-permute-done.11 = bf16[2,8,128,256]{3,2,1,0:T(8,128)(2,1)S(1)} collective-permute-done((bf16[2,8,128,256]{3,2,1,0:T(8,128)(2,1)S(1)}, bf16[2,8,128,256]{3,2,1,0:T(8,128)(2,1)S(1)}, u32[]{:S(2)}, u32[]{:S(2)}) %collective-permute-start.11) | collective-permute-done | bytes 1048608 | tf_op jit(solution)/shard_map/ppermute | solution.py:336
  190.0 23.3 %all_to_all.16 = bf16[16,128,256]{2,1,0:T(8,128)(2,1)S(1)} all-to-all(bf16[16,128,256]{2,1,0:T(8,128)(2,1)S(1)} %bitcast.31), channel_id=1, replica_groups=mesh['x_lo'=2,'zq'=4,'zr'=4,'x_hi'=2,'y'=4,'core'=2] {'x_lo','x_hi','y'}, dimensions={0} | all-to-all | bytes 2097152 | tf_op jit(solution)/shard_map/all_to_all | solution.py:391
  (41 shorter events, 7.0 us)
Async XLA Ops:
  9.1 72.6 %collective-permute-start = (bf16[64,128,128]{2,1,0:T(8,128)(2,1)}, bf16[64,128,128]{2,1,0:T(8,128)(2,1)S(1)}, u32[]{:S(2)}, u32[]{:S(2)}) collective-permute-start(bf16[64,128,128]{2,1,0:T(8,128)(2,1)} %bitcast.28), channel_id=1, source_target_pairs={{0,256},{256,0},{1,257},{257,1},{2,258},{258,2},{3,259},{259,3},{4... | collective-permute-start | bytes 6291464 | tf_op jit(solution)/shard_map/ppermute | solution.py:372
  49.6 2.5 %copy-start.7 = (bf16[1536,256]{1,0:T(8,128)(2,1)}, bf16[1536,256]{1,0:T(8,128)(2,1)S(1)}, u32[]{:S(2)}) copy-start(bf16[1536,256]{1,0:T(8,128)(2,1)S(1)} %all_gather.12.rest_2_.rest_0_) | copy-start | bytes 2359300
  49.6 19.5 %collective-permute-start.3 = (bf16[1536,256]{1,0:T(8,128)(2,1)S(1)}, bf16[1536,256]{1,0:T(8,128)(2,1)S(1)}, u32[]{:S(2)}, u32[]{:S(2)}) collective-permute-start(bf16[1536,256]{1,0:T(8,128)(2,1)S(1)} %all_gather.12.rest_2_.rest_0_), channel_id=1, source_target_pairs={{240,0},{0,16},{16,32},{32,48},{48,64},{64,80},{80,96},{96,112},{1... | collective-permute-start | bytes 2359304 | tf_op jit(solution)/shard_map/ppermute | solution.py:31
  52.1 19.0 %collective-permute-start.1 = (bf16[1536,256]{1,0:T(8,128)(2,1)S(1)}, bf16[1536,256]{1,0:T(8,128)(2,1)S(1)}, u32[]{:S(2)}, u32[]{:S(2)}) collective-permute-start(bf16[1536,256]{1,0:T(8,128)(2,1)S(1)} %all_gather.12.rest_2_.rest_0_), channel_id=1, source_target_pairs={{16,0},{32,16},{48,32},{64,48},{80,64},{96,80},{112,96},{128,112},... | collective-permute-start | bytes 2359304 | tf_op jit(solution)/shard_map/ppermute | solution.py:31
  69.1 2.0 copy-start.8
  69.1 9.7 %collective-permute-start.4 = (bf16[768,256]{1,0:T(8,128)(2,1)S(1)}, bf16[768,256]{1,0:T(8,128)(2,1)S(1)}, u32[]{:S(2)}, u32[]{:S(2)}) collective-permute-start(bf16[768,256]{1,0:T(8,128)(2,1)S(1)} %slice.26), channel_id=1, source_target_pairs={{240,0},{0,16},{16,32},{32,48},{48,64},{64,80},{80,96},{96,112},{1... | collective-permute-start | bytes 1179656 | tf_op jit(solution)/shard_map/ppermute | solution.py:31
  71.1 1.0 copy-start.9
  72.1 9.6 %collective-permute-start.2 = (bf16[768,256]{1,0:T(8,128)(2,1)}, bf16[768,256]{1,0:T(8,128)(2,1)S(1)}, u32[]{:S(2)}, u32[]{:S(2)}) collective-permute-start(bf16[768,256]{1,0:T(8,128)(2,1)} %slice.25), channel_id=1, source_target_pairs={{16,0},{32,16},{48,32},{64,48},{80,64},{96,80},{112,96},{128,112},... | collective-permute-start | bytes 1179656 | tf_op jit(solution)/shard_map/ppermute | solution.py:31
  78.9 2.8 %copy-start.10 = (bf16[768,256]{1,0:T(8,128)(2,1)}, bf16[768,256]{1,0:T(8,128)(2,1)S(1)}, u32[]{:S(2)}) copy-start(bf16[768,256]{1,0:T(8,128)(2,1)S(1)} %collective-permute-done.4.rest_5_.rest_3_) | copy-start | bytes 1179652
  81.7 0.7 copy-start.11
  87.6 9.1 %collective-permute-start.5 = (bf16[8,2,128,256]{3,2,1,0:T(8,128)(2,1)S(1)}, bf16[8,2,128,256]{3,2,1,0:T(8,128)(2,1)S(1)}, u32[]{:S(2)}, u32[]{:S(2)}) collective-permute-start(bf16[8,2,128,256]{3,2,1,0:T(8,128)(2,1)S(1)} %get-tuple-element.15), channel_id=1, source_target_pairs={{0,1},{1,0},{2,3},{3,2},{4,5},{5,4},{6,7},{7,6},{8,9},{9,8},{10,11... | collective-permute-start | bytes 3145736 | tf_op jit(solution)/shard_map/ppermute | solution.py:336
  96.8 8.3 %copy-start.4 = (s32[32,40]{1,0:T(8,128)S(1)}, s32[32,40]{1,0:T(8,128)}, u32[]{:S(2)}) copy-start(s32[32,40]{1,0:T(8,128)} %listed.1) | copy-start | bytes 15364
  96.8 8.3 %copy-start.5 = (s32[1,40]{1,0:T(1,128)S(1)}, s32[1,40]{1,0:T(1,128)}, u32[]{:S(2)}) copy-start(s32[1,40]{1,0:T(1,128)} %param.19) | copy-start | bytes 484
  96.8 8.3 %copy-start.6 = (s32[1,40]{1,0:T(1,128)S(1)}, s32[1,40]{1,0:T(1,128)}, u32[]{:S(2)}) copy-start(s32[1,40]{1,0:T(1,128)} %param.18) | copy-start | bytes 484
  98.1 21.4 %all-to-all-start.1 = ((bf16[8,2,128,256]{3,2,1,0:T(8,128)(2,1)}), bf16[8,2,128,256]{3,2,1,0:T(8,128)(2,1)S(1)}, u32[]{:S(2)}, u32[]{:S(2)}) async-start(bf16[8,2,128,256]{3,2,1,0:T(8,128)(2,1)} %add_convert_fusion.1), calls=%async_computation.1 | async-start | bytes 2097152 | tf_op jit(solution)/shard_map/all_to_all | solution.py:381
  105.1 1.3 copy-start.2
  110.5 0.8 copy-start
  119.5 39.3 %copy-start.1 = (bf16[2048,128]{1,0:T(8,128)(2,1)S(1)}, bf16[2048,128]{1,0:T(8,128)(2,1)}, u32[]{:S(2)}) copy-start(bf16[2048,128]{1,0:T(8,128)(2,1)} %copy-done) | copy-start | bytes 1572868
  150.4 14.6 %collective-permute-start.8 = (bf16[1024,256]{1,0:T(8,128)(2,1)S(1)}, bf16[1024,256]{1,0:T(8,128)(2,1)S(1)}, u32[]{:S(2)}, u32[]{:S(2)}) collective-permute-start(bf16[1024,256]{1,0:T(8,128)(2,1)S(1)} %all_gather.15.rest_2_), channel_id=1, source_target_pairs={{240,0},{0,16},{16,32},{32,48},{48,64},{64,80},{80,96},{96,112},{1... | collective-permute-start | bytes 1572872 | tf_op jit(solution)/shard_map/ppermute | solution.py:31
  152.3 14.6 %collective-permute-start.6 = (bf16[1024,256]{1,0:T(8,128)(2,1)S(1)}, bf16[1024,256]{1,0:T(8,128)(2,1)S(1)}, u32[]{:S(2)}, u32[]{:S(2)}) collective-permute-start(bf16[1024,256]{1,0:T(8,128)(2,1)S(1)} %all_gather.15.rest_2_), channel_id=1, source_target_pairs={{16,0},{32,16},{48,32},{64,48},{80,64},{96,80},{112,96},{128,112},... | collective-permute-start | bytes 1572872 | tf_op jit(solution)/shard_map/ppermute | solution.py:31
  158.8 12.7 %collective-permute-start.10 = (bf16[2048,128]{1,0:T(8,128)(2,1)S(1)}, bf16[2048,128]{1,0:T(8,128)(2,1)S(1)}, u32[]{:S(2)}, u32[]{:S(2)}) collective-permute-start(bf16[2048,128]{1,0:T(8,128)(2,1)S(1)} %copy-done.1), channel_id=1, source_target_pairs={{0,256},{256,0},{1,257},{257,1},{2,258},{258,2},{3,259},{259,3},{4... | collective-permute-start | bytes 1572872 | tf_op jit(solution)/shard_map/ppermute | solution.py:388
  165.0 8.3 %collective-permute-start.9 = (bf16[512,256]{1,0:T(8,128)(2,1)S(1)}, bf16[512,256]{1,0:T(8,128)(2,1)S(1)}, u32[]{:S(2)}, u32[]{:S(2)}) collective-permute-start(bf16[512,256]{1,0:T(8,128)(2,1)S(1)} %slice.28), channel_id=1, source_target_pairs={{240,0},{0,16},{16,32},{32,48},{48,64},{64,80},{80,96},{96,112},{1... | collective-permute-start | bytes 786440 | tf_op jit(solution)/shard_map/ppermute | solution.py:31
  167.0 7.9 %collective-permute-start.7 = (bf16[512,256]{1,0:T(8,128)(2,1)S(1)}, bf16[512,256]{1,0:T(8,128)(2,1)S(1)}, u32[]{:S(2)}, u32[]{:S(2)}) collective-permute-start(bf16[512,256]{1,0:T(8,128)(2,1)S(1)} %slice.27), channel_id=1, source_target_pairs={{16,0},{32,16},{48,32},{64,48},{80,64},{96,80},{112,96},{128,112},... | collective-permute-start | bytes 786440 | tf_op jit(solution)/shard_map/ppermute | solution.py:31
  179.4 10.4 %collective-permute-start.11 = (bf16[2,8,128,256]{3,2,1,0:T(8,128)(2,1)S(1)}, bf16[2,8,128,256]{3,2,1,0:T(8,128)(2,1)S(1)}, u32[]{:S(2)}, u32[]{:S(2)}) collective-permute-start(bf16[2,8,128,256]{3,2,1,0:T(8,128)(2,1)S(1)} %get-tuple-element.21), channel_id=1, source_target_pairs={{0,1},{1,0},{2,3},{3,2},{4,5},{5,4},{6,7},{7,6},{8,9},{9,8},{10,11... | collective-permute-start | bytes 3145736 | tf_op jit(solution)/shard_map/ppermute | solution.py:336
  189.7 23.6 %copy-start.3 = (bf16[512,512]{1,0:T(8,128)(2,1)S(1)}, bf16[512,512]{1,0:T(8,128)(2,1)}, u32[]{:S(2)}) copy-start(bf16[512,512]{1,0:T(8,128)(2,1)} %weight_ref.3) | copy-start | bytes 1572868

commit v9 on v8

--- a/solution.py
+++ b/solution.py
@@ -17,8 +17,7 @@
 LIST = 40
 WIDE = 128
 META = 16
-CARRY = BLOCK + 2 * FEAT
-PAY = CARRY + META
+PAY = BLOCK + META
 DOM = ("x_lo", "zq", "zr")
 Z = ("zq", "zr")
 GRID = ("x_hi", "y", "core")
@@ -35,7 +34,7 @@
     return pltpu.CompilerParams(vmem_limit_bytes=mib << 20)
 
 
-def payload_body(cols, counts, feats, hist, out, feats_in, hist_in, sems):
+def payload_body(cols, counts, feats, hist, out, own, feats_in, hist_in, sems):
     moves = [
         pltpu.make_async_copy(feats, feats_in, sems.at[0]),
         pltpu.make_async_copy(hist, hist_in, sems.at[1]),
@@ -53,21 +52,25 @@
         move.wait()
     for j in range(2):
         out[j, :BLOCK] = feats_in[:, j * HALF : (j + 1) * HALF]
-        for k in range(2):
-            start = BLOCK + k * FEAT
-            out[j, start : start + FEAT] = hist_in[:, k * HALF : (k + 1) * HALF]
-        out[j, CARRY:] = meta
+        out[j, BLOCK:] = meta
+        own[j * FEAT : (j + 1) * FEAT] = hist_in[:, j * HALF : (j + 1) * HALF]
 
 
 def make_payload(cols, counts, feats, hist):
     return pl.pallas_call(
         payload_body,
-        out_shape=jax.ShapeDtypeStruct((2, PAY, HALF), jnp.bfloat16),
+        out_shape=(
+            jax.ShapeDtypeStruct((2, PAY, HALF), jnp.bfloat16),
+            jax.ShapeDtypeStruct((2 * FEAT, HALF), jnp.bfloat16),
+        ),
         grid_spec=pltpu.PrefetchScalarGridSpec(
             num_scalar_prefetch=2,
             grid=(1,),
             in_specs=[pl.BlockSpec(memory_space=pltpu.HBM)] * 2,
-            out_specs=pl.BlockSpec((2, PAY, HALF), lambda i, *_: (0, 0, 0)),
+            out_specs=(
+                pl.BlockSpec((2, PAY, HALF), lambda i, *_: (0, 0, 0)),
+                pl.BlockSpec((2 * FEAT, HALF), lambda i, *_: (0, 0)),
+            ),
             scratch_shapes=[
                 pltpu.VMEM(feats.shape, jnp.bfloat16),
                 pltpu.VMEM(hist.shape, jnp.bfloat16),
@@ -86,7 +89,7 @@
         extras = rest[2 + n_chunks : 4 + n_chunks]
         keep, send, panel, adj, sems, added = rest[-6:]
     else:
-        keep, send, panel, adj, sems = rest[-5:]
+        keep, send, store, panel, adj, sems = rest[-6:]
     core = spot[1]
     moves = []
 
@@ -118,7 +121,7 @@
             z = col & 15
             ahead = z - spot[3]
             index = (ahead & 3) * 4 + (z >> 2)
-            start = pl.multiple_of((index * 2 + (col >> 4)) * stride, 2 * FEAT)
+            start = pl.multiple_of(index * stride + (col >> 4) * BLOCK, 2 * FEAT)
             right.append(panel[pl.ds(start, BLOCK), :])
         return jnp.dot(
             jnp.concatenate(left, axis=1),
@@ -144,6 +147,10 @@
 
     for n in range(n_chunks):
         moves[n].wait()
+    if not second:
+        for d in range(16):
+            source = panel.at[pl.ds(d * stride + 2 * BLOCK, 2 * FEAT)]
+            move(source, store.at[pl.ds(d * 2 * FEAT, 2 * FEAT)])
     for k in range(2):
         for c in range(4):
             moves[n_chunks + 4 * k + c].wait()
@@ -151,30 +158,37 @@
                 moves[n_chunks + 8 + k].wait()
             two_rows(k, 2 * c)
             two_rows(k, 2 * c + 1)
+    if not second:
+        for d in range(16):
+            moves[n_chunks + 8 + d].wait()
 
 
 def tile_product(numbers, spot, tiles, chunks, extras):
     operands = [*tiles, *chunks, *extras]
     second = bool(extras)
-    stride = sum(chunk.shape[0] for chunk in chunks) // 32
+    stride = sum(chunk.shape[0] for chunk in chunks) // 16
     shape = (2, ROWS // 2, BLOCK, HALF) if second else (ROWS // 2, 2, BLOCK, HALF)
     half = jax.ShapeDtypeStruct(shape, jnp.bfloat16)
     scratch = [
-        pltpu.VMEM((32 * stride, HALF), jnp.bfloat16),
+        pltpu.VMEM((16 * stride, HALF), jnp.bfloat16),
         pltpu.VMEM((2 * ROWS * SLOTS, BLOCK, BLOCK), jnp.bfloat16),
-        pltpu.SemaphoreType.DMA((len(chunks) + 8 + len(extras),)),
+        pltpu.SemaphoreType.DMA((len(chunks) + 8 + (2 if second else 16),)),
     ]
     if second:
         scratch.append(pltpu.VMEM((2, ROWS * BLOCK, WIDE), jnp.bfloat16))
     out_spec = pl.BlockSpec(shape, lambda i, *_: (0,) * len(shape))
+    outs, out_specs = [half, half], [out_spec, out_spec]
+    if not second:
+        outs.append(jax.ShapeDtypeStruct((32 * FEAT, HALF), jnp.bfloat16))
+        out_specs.append(pl.BlockSpec(memory_space=pltpu.HBM))
     return pl.pallas_call(
         functools.partial(tile_body, second, stride, len(chunks)),
-        out_shape=(half, half),
+        out_shape=tuple(outs),
         grid_spec=pltpu.PrefetchScalarGridSpec(
             num_scalar_prefetch=2,
             grid=(1,),
             in_specs=[pl.BlockSpec(memory_space=pltpu.HBM)] * len(operands),
-            out_specs=(out_spec, out_spec),
+            out_specs=tuple(out_specs),
             scratch_shapes=scratch,
         ),
         compiler_params=params(20),
@@ -182,21 +196,12 @@
     )(numbers, spot, *operands)
 
 
-def history_body(n_chunks, listed, order, rows, spot, adj, *rest):
-    chunks = rest[:n_chunks]
-    out, weights, store, total, sems = rest[n_chunks:]
-    moves = [pltpu.make_async_copy(adj, weights, sems.at[0])]
-    start = 0
-    for source in chunks:
-        for k in range(source.shape[0] // CARRY):
-            moves.append(
-                pltpu.make_async_copy(
-                    source.at[pl.ds(k * CARRY + BLOCK, 2 * FEAT)],
-                    store.at[pl.ds(start, 2 * FEAT)],
-                    sems.at[len(moves)],
-                )
-            )
-            start += 2 * FEAT
+def history_body(listed, order, rows, spot, adj, same, other, out, weights, store, total, sems):
+    moves = [
+        pltpu.make_async_copy(adj, weights, sems.at[0]),
+        pltpu.make_async_copy(same, store.at[0], sems.at[1]),
+        pltpu.make_async_copy(other, store.at[1], sems.at[2]),
+    ]
     for move in moves:
         move.start()
     total[...] = jnp.zeros_like(total)
@@ -208,12 +213,13 @@
         owner = block >> 2
         piece = block & 3
         z = owner & 15
-        place = (((z - spot[2]) & 3) * 4 + (z >> 2)) * 2 + (owner >> 4)
-        source = pl.multiple_of(place * (2 * FEAT) + (piece >> 1) * FEAT, FEAT)
+        zone = ((z - spot[2]) & 3) * 4 + (z >> 2)
+        place = zone * (2 * FEAT) + (piece >> 1) * FEAT
+        source = pl.multiple_of(place, FEAT)
         lane = pl.multiple_of((piece & 1) * BLOCK, BLOCK)
         return lax.dot_general(
             weights[slot],
-            store[pl.ds(source, FEAT), pl.ds(lane, BLOCK)],
+            store[(owner >> 4) ^ spot[3], pl.ds(source, FEAT), pl.ds(lane, BLOCK)],
             (((1,), (1,)), ((), ())),
             preferred_element_type=jnp.float32,
         )
@@ -229,25 +235,25 @@
     out[...] = pltpu.roll(total[...], spot[1] * FEAT, 1).astype(jnp.bfloat16)
 
 
-def history_term(listed, order, rows, spot, adj, chunks):
-    return pl.pallas_call(
-        functools.partial(history_body, len(chunks)),
+def history_term(listed, order, rows, spot, adj, same, other):
+    return pl.pallas_call(
+        history_body,
         out_shape=jax.ShapeDtypeStruct((ROWS * BLOCK, WIDE), jnp.bfloat16),
         grid_spec=pltpu.PrefetchScalarGridSpec(
             num_scalar_prefetch=4,
             grid=(1,),
-            in_specs=[pl.BlockSpec(memory_space=pltpu.HBM)] * (1 + len(chunks)),
+            in_specs=[pl.BlockSpec(memory_space=pltpu.HBM)] * 3,
             out_specs=pl.BlockSpec((ROWS * BLOCK, WIDE), lambda i, *_: (0, 0)),
             scratch_shapes=[
                 pltpu.VMEM(adj.shape, jnp.bfloat16),
-                pltpu.VMEM((64 * FEAT, HALF), jnp.bfloat16),
+                pltpu.VMEM((2, *same.shape), jnp.bfloat16),
                 pltpu.VMEM((ROWS * BLOCK, WIDE), jnp.float32),
-                pltpu.SemaphoreType.DMA((33,)),
+                pltpu.SemaphoreType.DMA((3,)),
             ],
         ),
         compiler_params=params(16),
         name="history_term",
-    )(listed, order, rows, spot, adj, *chunks)
+    )(listed, order, rows, spot, adj, same, other)
 
 
 def add_parts(parts):
@@ -359,9 +365,9 @@
     group = jnp.where(x_lo == x_hi, (grid_index // 4) % 2, -1)
     spot = jnp.stack([x_lo, lax.axis_index("core"), group, lax.axis_index(Z)])
     spot = spot.astype(jnp.int32)
-    hist_spot = jnp.stack([lax.axis_index(DOM), grid_index % 4, lax.axis_index(Z)]).astype(jnp.int32)
-
-    payload = make_payload(
+    hist_spot = jnp.stack([lax.axis_index(DOM), grid_index % 4, lax.axis_index(Z), x_lo]).astype(jnp.int32)
+
+    payload, own_store = make_payload(
         cols,
         counts,
         pltpu.with_memory_space_constraint(node_feats, pltpu.HBM),
@@ -370,21 +376,25 @@
     received = lax.all_to_all(payload, "x_lo", 0, 0, tiled=True)
     adj_held, received = lax.optimization_barrier((adj, received))
     partner = lax.ppermute(adj_held, "x_lo", SWAP)
-    chunks = gather_quads(received[:, :CARRY].reshape(2 * CARRY, HALF))
+    chunk = jnp.concatenate([received[0, :BLOCK], received[1, :BLOCK], own_store], axis=0)
+    chunks = gather_quads(chunk)
     chunks = [pltpu.with_memory_space_constraint(chunk, pltpu.HBM) for chunk in chunks]
     adj = pltpu.with_memory_space_constraint(adj, pltpu.HBM)
-    numbers = received[:, CARRY, :80].astype(jnp.int32)
-    mine = history_term(hist_list, hist_col[0], hist_row[0], hist_spot, hist_adj[0], chunks)
-
+    numbers = received[:, BLOCK, :80].astype(jnp.int32)
     tables = (numbers, spot)
-    both = swap_cores(*tile_product(*tables, (adj, partner), chunks, ()))
+    keep, send, store = tile_product(*tables, (adj, partner), chunks, ())
+    both = swap_cores(keep, send)
     agg = add_parts(lax.all_to_all(both, SIDE, 0, 0, tiled=True))
     halves = lax.all_gather(agg, "x_lo", axis=0, tiled=False)
     hidden, chunk = first_dense(
         halves, pltpu.with_memory_space_constraint(w_first, pltpu.HBM), spot
     )
 
-    chunk, mine = lax.optimization_barrier((chunk, mine))
+    chunk, store = lax.optimization_barrier((chunk, store))
+    other_store = lax.ppermute(store, "x_lo", SWAP)
+    mine = history_term(
+        hist_list, hist_col[0], hist_row[0], hist_spot, hist_adj[0], store, other_store
+    )
     extras = (mine, lax.ppermute(mine, "x_lo", SWAP))
     chunks = gather_quads(chunk)
     both = swap_cores(*tile_product(*tables, (adj, partner), chunks, extras))

time: 215 us -> 209 us (0.972)
  waiting for transfers between devices: 37.7 us -> 19 us
  blocking collectives: 96.9 us -> 111 us
    all_to_all x0 -> x1, blocking collectives: none -> 21.9 us  [local(): agg = add_parts(lax.all_to_all(both, SIDE, 0, 0, tiled=True))]
    ppermute x8, waiting for transfers between devices: 25 us -> 14.4 us  [from_z(): return lax.ppermute(value, Z, [((z + offset) % 16, z) for z in range(16)])]
    all_to_all x1 -> x0, waiting for transfers between devices: 8.2 us -> none  [local(): agg = add_parts(lax.all_to_all(both, SIDE, 0, 0, tiled=True))]
    all_to_all x1 -> x0, starting transfers between devices: 6.87 us -> none  [local(): agg = add_parts(lax.all_to_all(both, SIDE, 0, 0, tiled=True))]
    ppermute x2, starting transfers between devices: 14.9 us -> 18.5 us  [swap_cores(): other = lax.ppermute(send, 'core', SWAP)]
    all_gather x2, blocking collectives: 61 us -> 58 us  [gather_quads(): same = lax.all_gather(chunk, 'zq', axis=0, tiled=True)]
    ppermute x0 -> x1, starting transfers between devices: none -> 2.91 us  [local(): other_store = lax.ppermute(store, 'x_lo', SWAP)]
    all_to_all x1, blocking collectives: 23.3 us -> 20.4 us  [local(): lax.all_to_all(both.reshape(16, BLOCK, HALF), ALL_SIDE, 0, 0, tiled=True)]
  transfers between devices with their start and end apart: 13 -> 13, of which waited for: 9 -> 7; matrix products, arithmetic and copies ran while one was open for 1% -> 1% of each run, Pallas kernels for 2% -> 2%
where the time goes in v9:
time: 209 us; the launch traced here: 208 us
  blocking collectives  111 us (53%)
  starting transfers between devices  53 us (25%)
  Pallas kernels  19.1 us (9%)
  waiting for transfers between devices  19 us (9%)
  local copies, waits for them, and re-layouts  4.21 us (2%)
    all_gather x2, blocking collectives, gather_quads(): same = lax.all_gather(chunk, 'zq', axis=0, tiled=True)  58 us
    ppermute x8, starting transfers between devices, from_z(): return lax.ppermute(value, Z, [((z + offset) % 16, z) for z in range(16)])  27.8 us
    all_to_all x1, blocking collectives, local(): agg = add_parts(lax.all_to_all(both, SIDE, 0, 0, tiled=True))  21.9 us
    all_to_all x1, blocking collectives, local(): lax.all_to_all(both.reshape(16, BLOCK, HALF), ALL_SIDE, 0, 0, tiled=True)  20.4 us
    ppermute x2, starting transfers between devices, swap_cores(): other = lax.ppermute(send, 'core', SWAP)  18.5 us
    ppermute x8, waiting for transfers between devices, from_z(): return lax.ppermute(value, Z, [((z + offset) % 16, z) for z in range(16)])  14.4 us
    pallas_call x2, Pallas kernels, tile_product(): pl.pallas_call(functools.partial(tile_body, second, stride, len(chunks)),...  9.85 us
    all_to_all x1, blocking collectives, local(): received = lax.all_to_all(payload, 'x_lo', 0, 0, tiled=True)  6.52 us
  transfers between devices with their start and end apart: 13, of which 7 were waited for; matrix products, arithmetic and copies ran while one was open for 1% of the time, Pallas kernels for 2%

profile of v9, /device:TPU:1, one launch (start us, length us, event | category | flops | bytes accessed | tf_op | source)
XLA Modules:
  0.0 208.4 jit_solution(17031466942378344211)
XLA Ops:
  0.6 1.6 payload.1
  2.3 6.5 %all_to_all.15 = bf16[2,144,256]{2,1,0:T(8,128)(2,1)S(1)} all-to-all(bf16[2,144,256]{2,1,0:T(8,128)(2,1)S(1)} %get-tuple-element.15), channel_id=1, replica_groups=mesh['x_lo'=2,'zq'=4,'zr'=4,'x_hi'=2,'y'=4,'core'=2] {'x_lo'}, dimensions={0} | all-to-all | bytes 294912 | tf_op jit(solution)/shard_map/all_to_all | solution.py:376
  8.8 1.9 collective-permute-start
  10.7 34.3 %all_gather.12.rest_2_ = bf16[1280,256]{1,0:T(8,128)(2,1)S(1)} all-gather(bf16[320,256]{1,0:T(8,128)(2,1)S(1)} %pad_maximum_fusion), channel_id=1, replica_groups=mesh['x_lo'=2,'zq'=4,'zr'=4,'x_hi'=2,'y'=4,'core'=2] {'zq'}, dimensions={0}, use_global_device_ids=true | all-gather | bytes 819200 | tf_op jit(solution)/shard_map/all_gather | solution.py:333
  45.1 1.9 collective-permute-start.3
  47.0 4.6 %collective-permute-start.1 = (bf16[1280,256]{1,0:T(8,128)(2,1)S(1)}, bf16[1280,256]{1,0:T(8,128)(2,1)}, u32[]{:S(2)}, u32[]{:S(2)}) collective-permute-start(bf16[1280,256]{1,0:T(8,128)(2,1)S(1)} %all_gather.12.rest_2_), channel_id=1, source_target_pairs={{16,0},{32,16},{48,32},{64,48},{80,64},{96,80},{112,96},{128,112},... | collective-permute-start | bytes 1966088 | tf_op jit(solution)/shard_map/ppermute | solution.py:30
  51.6 7.3 %collective-permute-done.3.rest_6_ = bf16[1280,256]{1,0:T(8,128)(2,1)S(1)} collective-permute-done((bf16[1280,256]{1,0:T(8,128)(2,1)S(1)}, bf16[1280,256]{1,0:T(8,128)(2,1)S(1)}, u32[]{:S(2)}, u32[]{:S(2)}) %collective-permute-start.3) | collective-permute-done | bytes 655392 | tf_op jit(solution)/shard_map/ppermute | solution.py:30
  59.0 1.9 collective-permute-start.4
  60.9 1.0 slice.29
  61.9 4.6 %collective-permute-start.2 = (bf16[640,256]{1,0:T(8,128)(2,1)S(1)}, bf16[640,256]{1,0:T(8,128)(2,1)S(1)}, u32[]{:S(2)}, u32[]{:S(2)}) collective-permute-start(bf16[640,256]{1,0:T(8,128)(2,1)S(1)} %slice.29), channel_id=1, source_target_pairs={{16,0},{32,16},{48,32},{64,48},{80,64},{96,80},{112,96},{128,112},... | collective-permute-start | bytes 983048 | tf_op jit(solution)/shard_map/ppermute | solution.py:30
  66.7 1.4 collective-permute-done.4.rest_5_
  68.2 2.4 %collective-permute-done.2.rest_4_ = bf16[640,256]{1,0:T(8,128)(2,1)S(1)} collective-permute-done((bf16[640,256]{1,0:T(8,128)(2,1)S(1)}, bf16[640,256]{1,0:T(8,128)(2,1)S(1)}, u32[]{:S(2)}, u32[]{:S(2)}) %collective-permute-start.2) | collective-permute-done | bytes 327712 | tf_op jit(solution)/shard_map/ppermute | solution.py:30
  71.3 5.3 %tile_product.2 = (bf16[8,2,128,256]{3,2,1,0:T(8,128)(2,1)S(1)}, bf16[8,2,128,256]{3,2,1,0:T(8,128)(2,1)S(1)}, bf16[1024,256]{1,0:T(8,128)(2,1)}) custom-call(s32[2,80]{1,0:T(2,128)S(1)} %fusion.numbers, s32[4]{0:T(128)S(1)} %pad_add_fusion.spot.spot_ref, bf16[64,128,128]{2,1,0:T(8,128)(2,1)} %bitcast.32, ...), custom_call_target="tpu_custom_call" | custom-call | tf_op jit(solution)/shard_map/tile_product/pallas_call | solution.py:184
  76.6 9.4 %collective-permute-start.5 = (bf16[8,2,128,256]{3,2,1,0:T(8,128)(2,1)S(1)}, bf16[8,2,128,256]{3,2,1,0:T(8,128)(2,1)S(1)}, u32[]{:S(2)}, u32[]{:S(2)}) collective-permute-start(bf16[8,2,128,256]{3,2,1,0:T(8,128)(2,1)S(1)} %get-tuple-element.20), channel_id=1, source_target_pairs={{0,1},{1,0},{2,3},{3,2},{4,5},{5,4},{6,7},{7,6},{8,9},{9,8},{10,11... | collective-permute-start | bytes 3145736 | tf_op jit(solution)/shard_map/ppermute | solution.py:342
  86.0 2.3 %collective-permute-done.5 = bf16[8,2,128,256]{3,2,1,0:T(8,128)(2,1)S(1)} collective-permute-done((bf16[8,2,128,256]{3,2,1,0:T(8,128)(2,1)S(1)}, bf16[8,2,128,256]{3,2,1,0:T(8,128)(2,1)S(1)}, u32[]{:S(2)}, u32[]{:S(2)}) %collective-permute-start.5) | collective-permute-done | bytes 1048608 | tf_op jit(solution)/shard_map/ppermute | solution.py:342
  88.7 21.9 %all_to_all.16.parts_ref = bf16[8,2,128,256]{3,2,1,0:T(8,128)(2,1)S(1)} all-to-all(bf16[8,2,128,256]{3,2,1,0:T(8,128)(2,1)S(1)} %add_convert_fusion.1), channel_id=1, replica_groups=mesh['x_lo'=2,'zq'=4,'zr'=4,'x_hi'=2,'y'=4,'core'=2] {'x_hi','y'}, dimensions={0} | all-to-all | bytes 2097152 | tf_op jit(solution)/shard_map/all_to_all | solution.py:387
  110.7 4.5 %all-gather = bf16[4,128,256]{2,1,0:T(8,128)(2,1)S(1)} all-gather(bf16[2,128,256]{2,1,0:T(8,128)(2,1)S(1)} %add_parts.1), channel_id=2, replica_groups=mesh['x_lo'=2,'zq'=4,'zr'=4,'x_hi'=2,'y'=4,'core'=2] {'x_lo'}, dimensions={0}, use_global_device_ids=true | all-gather | bytes 393216 | tf_op jit(solution)/shard_map/all_gather | solution.py:388
  115.2 2.5 %first_dense.1 = (bf16[128,512]{1,0:T(8,128)(2,1)}, bf16[256,256]{1,0:T(8,128)(2,1)S(1)}) custom-call(s32[4]{0:T(128)S(1)} %pad_add_fusion.spot.spot_ref, bf16[2,2,128,256]{3,2,1,0:T(8,128)(2,1)S(1)} %bitcast.28, bf16[512,512]{1,0:T(8,128)(2,1)} %weight_ref.2), custom_call_target="tpu_custom_call" | custom-call | tf_op jit(solution)/shard_map/first_dense/pallas_call | solution.py:288
  117.7 2.9 %collective-permute-start.10 = (bf16[1024,256]{1,0:T(8,128)(2,1)}, bf16[1024,256]{1,0:T(8,128)(2,1)}, u32[]{:S(2)}, u32[]{:S(2)}) collective-permute-start(bf16[1024,256]{1,0:T(8,128)(2,1)} %get-tuple-element.25.same), channel_id=1, source_target_pairs={{0,256},{256,0},{1,257},{257,1},{2,258},{258,2},{3,259},{259,3},{4... | collective-permute-start | bytes 1572872 | tf_op jit(solution)/shard_map/ppermute | solution.py:394
  120.7 23.6 %all_gather.15.rest_2_ = bf16[1024,256]{1,0:T(8,128)(2,1)S(1)} all-gather(bf16[256,256]{1,0:T(8,128)(2,1)S(1)} %get-tuple-element.24), channel_id=1, replica_groups=mesh['x_lo'=2,'zq'=4,'zr'=4,'x_hi'=2,'y'=4,'core'=2] {'zq'}, dimensions={0}, use_global_device_ids=true | all-gather | bytes 655360 | tf_op jit(solution)/shard_map/all_gather | solution.py:333
  144.3 1.9 collective-permute-start.8
  146.2 6.4 %collective-permute-start.6 = (bf16[1024,256]{1,0:T(8,128)(2,1)S(1)}, bf16[1024,256]{1,0:T(8,128)(2,1)}, u32[]{:S(2)}, u32[]{:S(2)}) collective-permute-start(bf16[1024,256]{1,0:T(8,128)(2,1)S(1)} %all_gather.15.rest_2_), channel_id=1, source_target_pairs={{16,0},{32,16},{48,32},{64,48},{80,64},{96,80},{112,96},{128,112},... | collective-permute-start | bytes 1572872 | tf_op jit(solution)/shard_map/ppermute | solution.py:30
  152.7 1.3 copy-done
  154.0 4.0 %history_term.1.rest_7_ = bf16[2048,128]{1,0:T(8,128)(2,1)S(1)} custom-call(s32[32,40]{1,0:T(8,128)S(1)} %copy-done.2, s32[40]{0:T(128)S(1)} %bitcast.29, s32[40]{0:T(128)S(1)} %bitcast.30, s32[4]{0:T(128)S(1)} %pad_add_fusion.1.spot, bf16[40,128,128]{2,1,0:T(8,128)(2,1)S(1)} %bitcast.27, bf16[1024,256]{1,0:T(8,128)(2,1)} %get-tuple-element.25.same, ...), custom_call_target="tpu_custom_call" | custom-call | tf_op jit(solution)/shard_map/history_term/pallas_call | solution.py:239
  158.0 1.9 collective-permute-start.11
  160.0 1.9 collective-permute-start.9
  162.9 4.6 %collective-permute-start.7 = (bf16[512,256]{1,0:T(8,128)(2,1)S(1)}, bf16[512,256]{1,0:T(8,128)(2,1)S(1)}, u32[]{:S(2)}, u32[]{:S(2)}) collective-permute-start(bf16[512,256]{1,0:T(8,128)(2,1)S(1)} %slice.31), channel_id=1, source_target_pairs={{16,0},{32,16},{48,32},{64,48},{80,64},{96,80},{112,96},{128,112},... | collective-permute-start | bytes 786440 | tf_op jit(solution)/shard_map/ppermute | solution.py:30
  168.3 2.5 %collective-permute-done.7.rest_4_ = bf16[512,256]{1,0:T(8,128)(2,1)S(1)} collective-permute-done((bf16[512,256]{1,0:T(8,128)(2,1)S(1)}, bf16[512,256]{1,0:T(8,128)(2,1)S(1)}, u32[]{:S(2)}, u32[]{:S(2)}) %collective-permute-start.7) | collective-permute-done | bytes 262176 | tf_op jit(solution)/shard_map/ppermute | solution.py:30
  170.8 4.6 %tile_product.3 = (bf16[2,8,128,256]{3,2,1,0:T(8,128)(2,1)S(1)}, bf16[2,8,128,256]{3,2,1,0:T(8,128)(2,1)S(1)}) custom-call(s32[2,80]{1,0:T(2,128)S(1)} %fusion.numbers, s32[4]{0:T(128)S(1)} %pad_add_fusion.spot.spot_ref, bf16[64,128,128]{2,1,0:T(8,128)(2,1)} %bitcast.33, bf16[64,128,128]{2,1,0:T(8,128)(2,1)S(1)} %collective-permute-done.rest_1_, ...), custom_call_target="tpu_custom_call" | custom-call | tf_op jit(solution)/shard_map/tile_product/pallas_call | solution.py:184
  175.4 9.0 %collective-permute-start.12 = (bf16[2,8,128,256]{3,2,1,0:T(8,128)(2,1)S(1)}, bf16[2,8,128,256]{3,2,1,0:T(8,128)(2,1)S(1)}, u32[]{:S(2)}, u32[]{:S(2)}) collective-permute-start(bf16[2,8,128,256]{3,2,1,0:T(8,128)(2,1)S(1)} %get-tuple-element.27), channel_id=1, source_target_pairs={{0,1},{1,0},{2,3},{3,2},{4,5},{5,4},{6,7},{7,6},{8,9},{9,8},{10,11... | collective-permute-start | bytes 3145736 | tf_op jit(solution)/shard_map/ppermute | solution.py:342
  184.4 2.3 %collective-permute-done.12 = bf16[2,8,128,256]{3,2,1,0:T(8,128)(2,1)S(1)} collective-permute-done((bf16[2,8,128,256]{3,2,1,0:T(8,128)(2,1)S(1)}, bf16[2,8,128,256]{3,2,1,0:T(8,128)(2,1)S(1)}, u32[]{:S(2)}, u32[]{:S(2)}) %collective-permute-start.12) | collective-permute-done | bytes 1048608 | tf_op jit(solution)/shard_map/ppermute | solution.py:342
  187.0 20.4 %all_to_all.17 = bf16[16,128,256]{2,1,0:T(8,128)(2,1)S(1)} all-to-all(bf16[16,128,256]{2,1,0:T(8,128)(2,1)S(1)} %bitcast.34), channel_id=1, replica_groups=mesh['x_lo'=2,'zq'=4,'zr'=4,'x_hi'=2,'y'=4,'core'=2] {'x_lo','x_hi','y'}, dimensions={0} | all-to-all | bytes 2097152 | tf_op jit(solution)/shard_map/all_to_all | solution.py:401
  (37 shorter events, 4.7 us)
Async XLA Ops:
  8.8 61.7 %collective-permute-start = (bf16[64,128,128]{2,1,0:T(8,128)(2,1)}, bf16[64,128,128]{2,1,0:T(8,128)(2,1)S(1)}, u32[]{:S(2)}, u32[]{:S(2)}) collective-permute-start(bf16[64,128,128]{2,1,0:T(8,128)(2,1)} %bitcast.31), channel_id=1, source_target_pairs={{0,256},{256,0},{1,257},{257,1},{2,258},{258,2},{3,259},{259,3},{4... | collective-permute-start | bytes 6291464 | tf_op jit(solution)/shard_map/ppermute | solution.py:378
  45.1 25.4 %copy-start.5 = (bf16[1280,256]{1,0:T(8,128)(2,1)}, bf16[1280,256]{1,0:T(8,128)(2,1)S(1)}, u32[]{:S(2)}) copy-start(bf16[1280,256]{1,0:T(8,128)(2,1)S(1)} %all_gather.12.rest_2_) | copy-start | bytes 1966084
  45.1 13.9 %collective-permute-start.3 = (bf16[1280,256]{1,0:T(8,128)(2,1)S(1)}, bf16[1280,256]{1,0:T(8,128)(2,1)S(1)}, u32[]{:S(2)}, u32[]{:S(2)}) collective-permute-start(bf16[1280,256]{1,0:T(8,128)(2,1)S(1)} %all_gather.12.rest_2_), channel_id=1, source_target_pairs={{240,0},{0,16},{16,32},{32,48},{48,64},{64,80},{80,96},{96,112},{1... | collective-permute-start | bytes 1966088 | tf_op jit(solution)/shard_map/ppermute | solution.py:30
  47.0 13.9 %collective-permute-start.1 = (bf16[1280,256]{1,0:T(8,128)(2,1)S(1)}, bf16[1280,256]{1,0:T(8,128)(2,1)}, u32[]{:S(2)}, u32[]{:S(2)}) collective-permute-start(bf16[1280,256]{1,0:T(8,128)(2,1)S(1)} %all_gather.12.rest_2_), channel_id=1, source_target_pairs={{16,0},{32,16},{48,32},{64,48},{80,64},{96,80},{112,96},{128,112},... | collective-permute-start | bytes 1966088 | tf_op jit(solution)/shard_map/ppermute | solution.py:30
  59.0 7.5 %copy-start.6 = (bf16[1280,256]{1,0:T(8,128)(2,1)}, bf16[1280,256]{1,0:T(8,128)(2,1)S(1)}, u32[]{:S(2)}) copy-start(bf16[1280,256]{1,0:T(8,128)(2,1)S(1)} %collective-permute-done.3.rest_6_) | copy-start | bytes 1966084
  59.0 9.1 %collective-permute-start.4 = (bf16[640,256]{1,0:T(8,128)(2,1)S(1)}, bf16[640,256]{1,0:T(8,128)(2,1)S(1)}, u32[]{:S(2)}, u32[]{:S(2)}) collective-permute-start(bf16[640,256]{1,0:T(8,128)(2,1)S(1)} %slice.30), channel_id=1, source_target_pairs={{240,0},{0,16},{16,32},{32,48},{48,64},{64,80},{80,96},{96,112},{1... | collective-permute-start | bytes 983048 | tf_op jit(solution)/shard_map/ppermute | solution.py:30
  61.9 8.6 %collective-permute-start.2 = (bf16[640,256]{1,0:T(8,128)(2,1)S(1)}, bf16[640,256]{1,0:T(8,128)(2,1)S(1)}, u32[]{:S(2)}, u32[]{:S(2)}) collective-permute-start(bf16[640,256]{1,0:T(8,128)(2,1)S(1)} %slice.29), channel_id=1, source_target_pairs={{16,0},{32,16},{48,32},{64,48},{80,64},{96,80},{112,96},{128,112},... | collective-permute-start | bytes 983048 | tf_op jit(solution)/shard_map/ppermute | solution.py:30
  68.2 2.4 %copy-start.7 = (bf16[640,256]{1,0:T(8,128)(2,1)}, bf16[640,256]{1,0:T(8,128)(2,1)S(1)}, u32[]{:S(2)}) copy-start(bf16[640,256]{1,0:T(8,128)(2,1)S(1)} %collective-permute-done.4.rest_5_) | copy-start | bytes 983044
  70.5 0.7 copy-start.8
  76.6 11.7 %collective-permute-start.5 = (bf16[8,2,128,256]{3,2,1,0:T(8,128)(2,1)S(1)}, bf16[8,2,128,256]{3,2,1,0:T(8,128)(2,1)S(1)}, u32[]{:S(2)}, u32[]{:S(2)}) collective-permute-start(bf16[8,2,128,256]{3,2,1,0:T(8,128)(2,1)S(1)} %get-tuple-element.20), channel_id=1, source_target_pairs={{0,1},{1,0},{2,3},{3,2},{4,5},{5,4},{6,7},{7,6},{8,9},{9,8},{10,11... | collective-permute-start | bytes 3145736 | tf_op jit(solution)/shard_map/ppermute | solution.py:342
  88.6 64.1 %copy-start.2 = (s32[32,40]{1,0:T(8,128)S(1)}, s32[32,40]{1,0:T(8,128)}, u32[]{:S(2)}) copy-start(s32[32,40]{1,0:T(8,128)} %listed.1) | copy-start | bytes 15364
  88.7 64.0 %copy-start.3 = (s32[1,40]{1,0:T(1,128)S(1)}, s32[1,40]{1,0:T(1,128)}, u32[]{:S(2)}) copy-start(s32[1,40]{1,0:T(1,128)} %param.19) | copy-start | bytes 484
  88.7 64.0 %copy-start.4 = (s32[1,40]{1,0:T(1,128)S(1)}, s32[1,40]{1,0:T(1,128)}, u32[]{:S(2)}) copy-start(s32[1,40]{1,0:T(1,128)} %param.18) | copy-start | bytes 484
  117.7 35.0 %collective-permute-start.10 = (bf16[1024,256]{1,0:T(8,128)(2,1)}, bf16[1024,256]{1,0:T(8,128)(2,1)}, u32[]{:S(2)}, u32[]{:S(2)}) collective-permute-start(bf16[1024,256]{1,0:T(8,128)(2,1)} %get-tuple-element.25.same), channel_id=1, source_target_pairs={{0,256},{256,0},{1,257},{257,1},{2,258},{258,2},{3,259},{259,3},{4... | collective-permute-start | bytes 1572872 | tf_op jit(solution)/shard_map/ppermute | solution.py:394
  144.3 15.7 %collective-permute-start.8 = (bf16[1024,256]{1,0:T(8,128)(2,1)S(1)}, bf16[1024,256]{1,0:T(8,128)(2,1)S(1)}, u32[]{:S(2)}, u32[]{:S(2)}) collective-permute-start(bf16[1024,256]{1,0:T(8,128)(2,1)S(1)} %all_gather.15.rest_2_), channel_id=1, source_target_pairs={{240,0},{0,16},{16,32},{32,48},{48,64},{64,80},{80,96},{96,112},{1... | collective-permute-start | bytes 1572872 | tf_op jit(solution)/shard_map/ppermute | solution.py:30
  146.2 15.7 %collective-permute-start.6 = (bf16[1024,256]{1,0:T(8,128)(2,1)S(1)}, bf16[1024,256]{1,0:T(8,128)(2,1)}, u32[]{:S(2)}, u32[]{:S(2)}) collective-permute-start(bf16[1024,256]{1,0:T(8,128)(2,1)S(1)} %all_gather.15.rest_2_), channel_id=1, source_target_pairs={{16,0},{32,16},{48,32},{64,48},{80,64},{96,80},{112,96},{128,112},... | collective-permute-start | bytes 1572872 | tf_op jit(solution)/shard_map/ppermute | solution.py:30
  152.7 1.3 copy-start
  158.0 12.8 %collective-permute-start.11 = (bf16[2048,128]{1,0:T(8,128)(2,1)S(1)}, bf16[2048,128]{1,0:T(8,128)(2,1)S(1)}, u32[]{:S(2)}, u32[]{:S(2)}) collective-permute-start(bf16[2048,128]{1,0:T(8,128)(2,1)S(1)} %history_term.1.rest_7_), channel_id=1, source_target_pairs={{0,256},{256,0},{1,257},{257,1},{2,258},{258,2},{3,259},{259,3},{4... | collective-permute-start | bytes 1572872 | tf_op jit(solution)/shard_map/ppermute | solution.py:398
  160.0 8.3 %collective-permute-start.9 = (bf16[512,256]{1,0:T(8,128)(2,1)S(1)}, bf16[512,256]{1,0:T(8,128)(2,1)S(1)}, u32[]{:S(2)}, u32[]{:S(2)}) collective-permute-start(bf16[512,256]{1,0:T(8,128)(2,1)S(1)} %slice.32), channel_id=1, source_target_pairs={{240,0},{0,16},{16,32},{32,48},{48,64},{64,80},{80,96},{96,112},{1... | collective-permute-start | bytes 786440 | tf_op jit(solution)/shard_map/ppermute | solution.py:30
  162.9 7.9 %collective-permute-start.7 = (bf16[512,256]{1,0:T(8,128)(2,1)S(1)}, bf16[512,256]{1,0:T(8,128)(2,1)S(1)}, u32[]{:S(2)}, u32[]{:S(2)}) collective-permute-start(bf16[512,256]{1,0:T(8,128)(2,1)S(1)} %slice.31), channel_id=1, source_target_pairs={{16,0},{32,16},{48,32},{64,48},{80,64},{96,80},{112,96},{128,112},... | collective-permute-start | bytes 786440 | tf_op jit(solution)/shard_map/ppermute | solution.py:30
  175.4 11.3 %collective-permute-start.12 = (bf16[2,8,128,256]{3,2,1,0:T(8,128)(2,1)S(1)}, bf16[2,8,128,256]{3,2,1,0:T(8,128)(2,1)S(1)}, u32[]{:S(2)}, u32[]{:S(2)}) collective-permute-start(bf16[2,8,128,256]{3,2,1,0:T(8,128)(2,1)S(1)} %get-tuple-element.27), channel_id=1, source_target_pairs={{0,1},{1,0},{2,3},{3,2},{4,5},{5,4},{6,7},{7,6},{8,9},{9,8},{10,11... | collective-permute-start | bytes 3145736 | tf_op jit(solution)/shard_map/ppermute | solution.py:342
  186.7 20.8 %copy-start.1 = (bf16[512,512]{1,0:T(8,128)(2,1)S(1)}, bf16[512,512]{1,0:T(8,128)(2,1)}, u32[]{:S(2)}) copy-start(bf16[512,512]{1,0:T(8,128)(2,1)} %weight_ref.3) | copy-start | bytes 1572868
